TPU v7x, 32 devices: a whole 2x2x4 slice. The times are simulated.
32 devices in a mesh: grp: 8 (over z, x), seq: 4 (over y, core).
Axes of the slice: x: 2, y: 2, z: 4, core: 2. Of those that a mesh axis runs over, the one named last changes fastest.
Arguments:
- prompt_in: bfloat16 [8, 2048, 768], P('grp', 'seq'), may hold values from -6 to 6
- cont_in: bfloat16 [8, 16, 256, 768], P('grp', 'seq'), may hold values from -6 to 6
- prompt_cot: bfloat16 [8, 2048, 768], P('grp', 'seq'), may hold values from -6 to 6
- cont_cot: bfloat16 [8, 16, 256, 768], P('grp', 'seq'), may hold values from -6 to 6
- labels: int32 [8, 16], P('grp', 'seq'), may hold values from 0 to 13
- joint_weight: float32 [768, 2304], P(('grp', 'seq')), may hold values from -0.21875 to 0.21875
- query_bias: float32 [768], P(('grp', 'seq')), may hold values from -3 to 3
- value_bias: float32 [768], P(('grp', 'seq')), may hold values from -0.3 to 0.3
- output_weight: float32 [768, 768], P(('grp', 'seq')), may hold values from -3.5 to 3.5
- output_bias: float32 [768], P(('grp', 'seq')), may hold values from -2 to 2
- first_gain: float32 [768], P(('grp', 'seq')), may hold values from 0.5 to 1.5
- first_shift: float32 [768], P(('grp', 'seq')), may hold values from -2 to 2
- expand_weight: float32 [768, 3072], P(('grp', 'seq')), may hold values from -0.21875 to 0.21875
- expand_bias: float32 [3072], P(('grp', 'seq')), may hold values from -3 to 3
- reduce_weight: float32 [3072, 768], P(('grp', 'seq')), may hold values from -0.109375 to 0.109375
- reduce_bias: float32 [768], P(('grp', 'seq')), may hold values from -2 to 2
- second_gain: float32 [768], P(('grp', 'seq')), may hold values from 0.5 to 1.5
- second_shift: float32 [768], P(('grp', 'seq')), may hold values from -2 to 2
- student_weight: float32 [768, 128], replicated, may hold values from -0.21875 to 0.21875
- student_bias: float32 [128], replicated, may hold values from -2 to 2
- pool_query: float32 [128], replicated, may hold values from -4 to 4
- pool_weight: float32 [128, 128], replicated, may hold values from -0.5 to 0.5
- pool_bias: float32 [128], replicated, may hold values from -2 to 2
- class_weight: float32 [128, 14], replicated, may hold values from -1.5 to 1.5
- class_bias: float32 [14], replicated, may hold values from -3 to 3
Outputs:
- prompt_out: bfloat16 [8, 2048, 768], P('grp', 'seq')
- cont_out: bfloat16 [8, 16, 256, 768], P('grp', 'seq')
- logits: float32 [8, 16, 14], P('grp', 'seq')
- prompt_grad: float32 [8, 2048, 768], P('grp', 'seq')
- cont_grad: float32 [8, 16, 256, 768], P('grp', 'seq')
- joint_weight_grad: float32 [768, 2304], P(('grp', 'seq'))
- query_bias_grad: float32 [768], P(('grp', 'seq'))
- value_bias_grad: float32 [768], P(('grp', 'seq'))
- output_weight_grad: float32 [768, 768], P(('grp', 'seq'))
- output_bias_grad: float32 [768], P(('grp', 'seq'))
- first_gain_grad: float32 [768], P(('grp', 'seq'))
- first_shift_grad: float32 [768], P(('grp', 'seq'))
- expand_weight_grad: float32 [768, 3072], P(('grp', 'seq'))
- expand_bias_grad: float32 [3072], P(('grp', 'seq'))
- reduce_weight_grad: float32 [3072, 768], P(('grp', 'seq'))
- reduce_bias_grad: float32 [768], P(('grp', 'seq'))
- second_gain_grad: float32 [768], P(('grp', 'seq'))
- second_shift_grad: float32 [768], P(('grp', 'seq'))
- student_weight_grad: float32 [768, 128], replicated
- student_bias_grad: float32 [128], replicated
- pool_query_grad: float32 [128], replicated
- pool_weight_grad: float32 [128, 128], replicated
- pool_bias_grad: float32 [128], replicated
- class_weight_grad: float32 [128, 14], replicated
- class_bias_grad: float32 [14], replicated
All inputs are finite; a program needn't handle non-finite values.
Results may differ from a plain program's by a relative error of at most 0.014.
The roundings to bfloat16 on the way count: a program that leaves them out, or rounds other values in their place, can miss the bound.
Values may be sent and summed in bfloat16 or wider, within the bound.
No kernel may reach another device: no remote copies, remote signals or barrier semaphores. Data moves between devices by JAX's collectives and lax.ppermute only.
A program may use at most 448 MiB of HBM per device.

v0:
```python
import jax
import jax.numpy as jnp
from jax import lax
from jax.sharding import PartitionSpec as P

HEAD_DIM = 64
POOL_HEADS = 2


EPSILON = 1e-06
HIGHEST = lax.Precision.HIGHEST
NEGATIVE = -1e30


def layer_norm(rows, gain, shift):
    center = rows - jnp.mean(rows, -1, keepdims=True)
    variance = jnp.mean(center * center, -1, keepdims=True)
    return center * lax.rsqrt(variance + EPSILON) * gain + shift


def gelu_exact(values):
    return jax.nn.gelu(values, approximate=False)


def matmul(left, right):
    return jnp.dot(left, right, preferred_element_type=jnp.float32)


def matmul_left_t(left, right):
    return lax.dot_general(
        left, right, (((0,), (0,)), ((), ())), preferred_element_type=jnp.float32
    )


def matmul_right_t(left, right):
    return lax.dot_general(
        left, right, (((1,), (1,)), ((), ())), preferred_element_type=jnp.float32
    )


def precise(left, right):
    return jnp.dot(left, right, precision=HIGHEST, preferred_element_type=jnp.float32)


def precise_left_t(left, right):
    return lax.dot_general(
        left, right, (((0,), (0,)), ((), ())), precision=HIGHEST, preferred_element_type=jnp.float32
    )


def precise_right_t(left, right):
    return lax.dot_general(
        left, right, (((1,), (1,)), ((), ())), precision=HIGHEST, preferred_element_type=jnp.float32
    )


def head_forward(student, pool_query, pool_weight, pool_bias, class_weight, class_bias, labels):
    count, length, width = student.shape
    split = student.reshape(count, length, POOL_HEADS, width // POOL_HEADS)
    query = pool_query.reshape(POOL_HEADS, width // POOL_HEADS)
    scores = jnp.einsum("clhd,hd->chl", split, query, precision=HIGHEST) * (
        width // POOL_HEADS
    ) ** (-0.5)
    weights = jax.nn.softmax(scores, -1)
    pooled = jnp.einsum("chl,clhd->chd", weights, split, precision=HIGHEST).reshape(count, width)
    hidden = jnp.tanh(precise(pooled, pool_weight) + pool_bias)
    logits = precise(hidden, class_weight) + class_bias
    onehot = (labels[:, None] == jnp.arange(logits.shape[1], dtype=jnp.int32)[None, :]).astype(
        jnp.float32
    )
    loss = jnp.sum(jax.nn.logsumexp(logits, -1) - jnp.sum(onehot * logits, -1))
    return (loss, logits)


def local(
    prompt_in,
    cont_in,
    prompt_cot,
    cont_cot,
    labels,
    joint_weight,
    query_bias,
    value_bias,
    output_weight,
    output_bias,
    first_gain,
    first_shift,
    expand_weight,
    expand_bias,
    reduce_weight,
    reduce_bias,
    second_gain,
    second_shift,
    student_weight,
    student_bias,
    pool_query,
    pool_weight,
    pool_bias,
    class_weight,
    class_bias,
):
    brain = jnp.bfloat16
    (
        joint_full,
        qbias_full,
        vbias_full,
        output_full,
        obias_full,
        fgain_full,
        fshift_full,
        expand_full,
        ebias_full,
        reduce_full,
        rbias_full,
        sgain_full,
        sshift_full,
    ) = (
        lax.all_gather(joint_weight.astype(brain), ("grp", "seq"), axis=0, tiled=True),
        lax.all_gather(query_bias.astype(brain), ("grp", "seq"), axis=0, tiled=True),
        lax.all_gather(value_bias.astype(brain), ("grp", "seq"), axis=0, tiled=True),
        lax.all_gather(output_weight.astype(brain), ("grp", "seq"), axis=0, tiled=True),
        lax.all_gather(output_bias.astype(brain), ("grp", "seq"), axis=0, tiled=True),
        lax.all_gather(first_gain.astype(brain), ("grp", "seq"), axis=0, tiled=True),
        lax.all_gather(first_shift.astype(brain), ("grp", "seq"), axis=0, tiled=True),
        lax.all_gather(expand_weight.astype(brain), ("grp", "seq"), axis=0, tiled=True),
        lax.all_gather(expand_bias.astype(brain), ("grp", "seq"), axis=0, tiled=True),
        lax.all_gather(reduce_weight.astype(brain), ("grp", "seq"), axis=0, tiled=True),
        lax.all_gather(reduce_bias.astype(brain), ("grp", "seq"), axis=0, tiled=True),
        lax.all_gather(second_gain.astype(brain), ("grp", "seq"), axis=0, tiled=True),
        lax.all_gather(second_shift.astype(brain), ("grp", "seq"), axis=0, tiled=True),
    )
    prompt_rows = prompt_in[0]
    share = prompt_rows.shape[0]
    conts = cont_in.shape[1]
    length = cont_in.shape[2]
    width = prompt_rows.shape[1]
    heads = width // HEAD_DIM
    scale = HEAD_DIM ** (-0.5)
    cont_count = conts * length
    rows = jnp.concatenate([prompt_rows, cont_in[0].reshape(cont_count, width)], 0)
    qbias = qbias_full.astype(jnp.float32)
    vbias = vbias_full.astype(jnp.float32)
    joint = matmul(rows, joint_full)
    queries = (joint[:, :width] + qbias).astype(brain)
    keys = joint[:, width : 2 * width].astype(brain)
    values = (joint[:, 2 * width :] + vbias).astype(brain)
    prompt_keys, prompt_values = (
        lax.all_gather(keys[:share], "seq", axis=0, tiled=True),
        lax.all_gather(values[:share], "seq", axis=0, tiled=True),
    )
    cont_k_all = keys[share:]
    cont_v_all = values[share:]
    prompt_source = rows[:share]
    total_prompt = prompt_keys.shape[0]
    far_keys = prompt_keys.reshape(total_prompt, heads, HEAD_DIM)
    far_values = prompt_values.reshape(total_prompt, heads, HEAD_DIM)
    prompt_queries = queries[:share].reshape(share, heads, HEAD_DIM)
    prompt_scores = (
        jnp.einsum("qhd,khd->hqk", prompt_queries, far_keys, preferred_element_type=jnp.float32)
        * scale
    )
    prompt_top = jnp.max(prompt_scores, -1, keepdims=True)
    prompt_exp = jnp.exp(prompt_scores - prompt_top)
    prompt_total = jnp.sum(prompt_exp, -1, keepdims=True)
    prompt_probs = (prompt_exp / prompt_total).astype(brain)
    prompt_context = (
        jnp.einsum("hqk,khd->qhd", prompt_probs, far_values, preferred_element_type=jnp.float32)
        .astype(brain)
        .reshape(share, width)
    )
    prompt_lse = prompt_top + jnp.log(prompt_total)
    per_block = min(conts, 2)
    blocks = conts // per_block

    def split_blocks(array):
        return array.reshape(blocks, per_block, length, heads, HEAD_DIM)

    cont_queries = split_blocks(queries[share:])
    cont_keys = split_blocks(cont_k_all)
    cont_values = split_blocks(cont_v_all)
    causal = lax.broadcasted_iota(jnp.int32, (length, length), 0) >= lax.broadcasted_iota(
        jnp.int32, (length, length), 1
    )

    def block_scores(query_block, key_block):
        far = (
            jnp.einsum("nqhd,khd->nhqk", query_block, far_keys, preferred_element_type=jnp.float32)
            * scale
        )
        near = (
            jnp.einsum(
                "nqhd,nkhd->nhqk", query_block, key_block, preferred_element_type=jnp.float32
            )
            * scale
        )
        return (far, jnp.where(causal, near, NEGATIVE))

    def block_forward(item):
        query_block, key_block, value_block = item
        far, near = block_scores(query_block, key_block)
        top = jnp.maximum(jnp.max(far, -1, keepdims=True), jnp.max(near, -1, keepdims=True))
        far_exp = jnp.exp(far - top)
        near_exp = jnp.exp(near - top)
        total = jnp.sum(far_exp, -1, keepdims=True) + jnp.sum(near_exp, -1, keepdims=True)
        context_block = jnp.einsum(
            "nhqk,khd->nqhd",
            (far_exp / total).astype(brain),
            far_values,
            preferred_element_type=jnp.float32,
        )
        context_block = context_block + jnp.einsum(
            "nhqk,nkhd->nqhd",
            (near_exp / total).astype(brain),
            value_block,
            preferred_element_type=jnp.float32,
        )
        return (context_block.astype(brain), top + jnp.log(total))

    cont_context, cont_lse = lax.map(block_forward, (cont_queries, cont_keys, cont_values))
    context = jnp.concatenate([prompt_context, cont_context.reshape(cont_count, width)], 0)
    branch = matmul(context, output_full) + obias_full.astype(jnp.float32)
    first, first_back = jax.vjp(
        layer_norm,
        rows.astype(jnp.float32) + branch,
        fgain_full.astype(jnp.float32),
        fshift_full.astype(jnp.float32),
    )
    first_low = first.astype(brain)
    pre = matmul(first_low, expand_full) + ebias_full.astype(jnp.float32)
    activated, gelu_back = jax.vjp(gelu_exact, pre)
    hidden = activated.astype(brain)
    mixed = first + matmul(hidden, reduce_full) + rbias_full.astype(jnp.float32)
    layer, second_back = jax.vjp(
        layer_norm, mixed, sgain_full.astype(jnp.float32), sshift_full.astype(jnp.float32)
    )
    layer_low = layer.astype(brain)
    student_low = student_weight.astype(brain)
    cont_layer = layer_low[share:]
    student = matmul(cont_layer, student_low) + student_bias

    def head_piece(student_rows, query, pool_w, pool_b, class_w, class_b):
        return head_forward(
            student_rows.reshape(conts, length, student_rows.shape[1]),
            query,
            pool_w,
            pool_b,
            class_w,
            class_b,
            labels[0],
        )

    loss, head_back, logits = jax.vjp(
        head_piece,
        student,
        pool_query,
        pool_weight,
        pool_bias,
        class_weight,
        class_bias,
        has_aux=True,
    )
    d_student, d_query, d_pool_weight, d_pool_bias, d_class_weight, d_class_bias = head_back(
        jnp.ones_like(loss)
    )
    d_student_bias = jnp.sum(d_student, 0)
    d_student_low = d_student.astype(brain)
    d_student_weight = matmul_left_t(cont_layer, d_student_low)
    head_grads = lax.psum(
        (
            d_student_weight,
            d_student_bias,
            d_query,
            d_pool_weight,
            d_pool_bias,
            d_class_weight,
            d_class_bias,
        ),
        ("grp", "seq"),
    )
    cotangent = jnp.concatenate(
        [
            prompt_cot[0].astype(jnp.float32),
            cont_cot[0].reshape(cont_count, width).astype(jnp.float32)
            + matmul_right_t(d_student_low, student_low),
        ],
        0,
    )
    joint_back, output_back, expand_back, reduce_back = (
        lax.all_gather(joint_weight.astype(brain), ("grp", "seq"), axis=0, tiled=True),
        lax.all_gather(output_weight.astype(brain), ("grp", "seq"), axis=0, tiled=True),
        lax.all_gather(expand_weight.astype(brain), ("grp", "seq"), axis=0, tiled=True),
        lax.all_gather(reduce_weight.astype(brain), ("grp", "seq"), axis=0, tiled=True),
    )
    d_mixed, d_second_gain, d_second_shift = second_back(cotangent)
    d_reduce_bias = jnp.sum(d_mixed, 0)
    d_mixed_low = d_mixed.astype(brain)
    d_reduce_weight = matmul_left_t(hidden, d_mixed_low)
    (d_pre,) = gelu_back(matmul_right_t(d_mixed_low, reduce_back))
    d_expand_bias = jnp.sum(d_pre, 0)
    d_pre_low = d_pre.astype(brain)
    d_expand_weight = matmul_left_t(first_low, d_pre_low)
    d_first = d_mixed + matmul_right_t(d_pre_low, expand_back)
    d_inner, d_first_gain, d_first_shift = first_back(d_first)
    d_output_bias = jnp.sum(d_inner, 0)
    d_inner_low = d_inner.astype(brain)
    d_output_weight = matmul_left_t(context, d_inner_low)
    d_context = matmul_right_t(d_inner_low, output_back).astype(brain)
    prompt_dctx = d_context[:share].reshape(share, heads, HEAD_DIM)
    again_scores = (
        jnp.einsum("qhd,khd->hqk", prompt_queries, far_keys, preferred_element_type=jnp.float32)
        * scale
    )
    again_probs = jnp.exp(again_scores - prompt_lse)
    prompt_dprob = jnp.einsum(
        "qhd,khd->hqk", prompt_dctx, far_values, preferred_element_type=jnp.float32
    )
    prompt_delta = jnp.sum(again_probs * prompt_dprob, -1, keepdims=True)
    prompt_dscore = (again_probs * (prompt_dprob - prompt_delta)).astype(brain)
    prompt_dq = (
        jnp.einsum("hqk,khd->qhd", prompt_dscore, far_keys, preferred_element_type=jnp.float32)
        * scale
    )
    far_dk = (
        jnp.einsum(
            "hqk,qhd->khd", prompt_dscore, prompt_queries, preferred_element_type=jnp.float32
        )
        * scale
    )
    far_dv = jnp.einsum(
        "hqk,qhd->khd", again_probs.astype(brain), prompt_dctx, preferred_element_type=jnp.float32
    )

    def block_backward(carry, item):
        query_block, key_block, value_block, lse_block, dctx_block = item
        far, near = block_scores(query_block, key_block)
        far_p = jnp.exp(far - lse_block)
        near_p = jnp.exp(near - lse_block)
        far_dp = jnp.einsum(
            "nqhd,khd->nhqk", dctx_block, far_values, preferred_element_type=jnp.float32
        )
        near_dp = jnp.einsum(
            "nqhd,nkhd->nhqk", dctx_block, value_block, preferred_element_type=jnp.float32
        )
        delta = jnp.sum(far_p * far_dp, -1, keepdims=True) + jnp.sum(
            near_p * near_dp, -1, keepdims=True
        )
        far_ds = (far_p * (far_dp - delta)).astype(brain)
        near_ds = (near_p * (near_dp - delta)).astype(brain)
        block_dq = (
            jnp.einsum("nhqk,khd->nqhd", far_ds, far_keys, preferred_element_type=jnp.float32)
            + jnp.einsum("nhqk,nkhd->nqhd", near_ds, key_block, preferred_element_type=jnp.float32)
        ) * scale
        near_dk = (
            jnp.einsum("nhqk,nqhd->nkhd", near_ds, query_block, preferred_element_type=jnp.float32)
            * scale
        )
        near_dv = jnp.einsum(
            "nhqk,nqhd->nkhd", near_p.astype(brain), dctx_block, preferred_element_type=jnp.float32
        )
        sum_dk = (
            carry[0]
            + jnp.einsum("nhqk,nqhd->khd", far_ds, query_block, preferred_element_type=jnp.float32)
            * scale
        )
        sum_dv = carry[1] + jnp.einsum(
            "nhqk,nqhd->khd", far_p.astype(brain), dctx_block, preferred_element_type=jnp.float32
        )
        return ((sum_dk, sum_dv), (block_dq, near_dk, near_dv))

    (far_dk, far_dv), (cont_dq, cont_dk, cont_dv) = lax.scan(
        block_backward,
        (far_dk, far_dv),
        (cont_queries, cont_keys, cont_values, cont_lse, split_blocks(d_context[share:])),
    )
    d_queries = jnp.concatenate(
        [prompt_dq.reshape(share, width), cont_dq.reshape(cont_count, width)], 0
    )
    d_query_low = d_queries.astype(brain)
    cont_kv = jnp.concatenate(
        [cont_dk.reshape(cont_count, width), cont_dv.reshape(cont_count, width)], 1
    )
    cont_kv_low = cont_kv.astype(brain)
    kv_back = joint_back[:, width:]
    kv_back_wide = kv_back.astype(jnp.float32)
    own_dk, own_dv = (
        lax.psum_scatter(
            far_dk.reshape(total_prompt, width).astype(jnp.bfloat16),
            "seq",
            scatter_dimension=0,
            tiled=True,
        ).astype(jnp.float32),
        lax.psum_scatter(
            far_dv.reshape(total_prompt, width).astype(jnp.bfloat16),
            "seq",
            scatter_dimension=0,
            tiled=True,
        ).astype(jnp.float32),
    )
    prompt_kv_f = jnp.concatenate([own_dk, own_dv], 1)
    prompt_part = precise_right_t(prompt_kv_f, kv_back_wide)
    d_query_bias = jnp.sum(d_queries, 0)
    d_value_bias = jnp.sum(cont_kv[:, width:], 0) + jnp.sum(prompt_kv_f[:, width:], 0)
    query_columns = matmul_left_t(rows, d_query_low)
    kv_columns = matmul_left_t(rows[share:], cont_kv_low) + precise_left_t(
        prompt_source.astype(jnp.float32), prompt_kv_f
    )
    d_joint_weight = jnp.concatenate([query_columns, kv_columns], 1)
    d_rows = d_inner + matmul_right_t(d_query_low, joint_back[:, :width])
    d_prompt_rows = d_rows[:share] + prompt_part
    d_cont_rows = d_rows[share:] + matmul_right_t(cont_kv_low, kv_back)
    shards = (
        lax.psum_scatter(d_joint_weight, ("grp", "seq"), scatter_dimension=0, tiled=True),
        lax.psum_scatter(d_query_bias, ("grp", "seq"), scatter_dimension=0, tiled=True),
        lax.psum_scatter(d_value_bias, ("grp", "seq"), scatter_dimension=0, tiled=True),
        lax.psum_scatter(d_output_weight, ("grp", "seq"), scatter_dimension=0, tiled=True),
        lax.psum_scatter(d_output_bias, ("grp", "seq"), scatter_dimension=0, tiled=True),
        lax.psum_scatter(d_first_gain, ("grp", "seq"), scatter_dimension=0, tiled=True),
        lax.psum_scatter(d_first_shift, ("grp", "seq"), scatter_dimension=0, tiled=True),
        lax.psum_scatter(d_expand_weight, ("grp", "seq"), scatter_dimension=0, tiled=True),
        lax.psum_scatter(d_expand_bias, ("grp", "seq"), scatter_dimension=0, tiled=True),
        lax.psum_scatter(d_reduce_weight, ("grp", "seq"), scatter_dimension=0, tiled=True),
        lax.psum_scatter(d_reduce_bias, ("grp", "seq"), scatter_dimension=0, tiled=True),
        lax.psum_scatter(d_second_gain, ("grp", "seq"), scatter_dimension=0, tiled=True),
        lax.psum_scatter(d_second_shift, ("grp", "seq"), scatter_dimension=0, tiled=True),
    )
    outputs = (
        layer_low[:share][None],
        cont_layer.reshape(1, conts, length, width),
        logits[None],
        d_prompt_rows[None],
        d_cont_rows.reshape(1, conts, length, width),
    )
    return outputs + tuple(shards) + tuple(head_grads)


def solution(mesh):
    placed = (
        P("grp", "seq", None),
        P("grp", "seq", None, None),
        P("grp", "seq", None),
        P("grp", "seq", None, None),
        P("grp", "seq"),
        P(("grp", "seq"), None),
        P(("grp", "seq")),
        P(("grp", "seq")),
        P(("grp", "seq"), None),
        P(("grp", "seq")),
        P(("grp", "seq")),
        P(("grp", "seq")),
        P(("grp", "seq"), None),
        P(("grp", "seq")),
        P(("grp", "seq"), None),
        P(("grp", "seq")),
        P(("grp", "seq")),
        P(("grp", "seq")),
        P(),
        P(),
        P(),
        P(),
        P(),
        P(),
        P(),
    )
    return jax.shard_map(
        local,
        mesh=mesh,
        in_specs=placed,
        out_specs=(
            P("grp", "seq", None),
            P("grp", "seq", None, None),
            P("grp", "seq", None),
            P("grp", "seq", None),
            P("grp", "seq", None, None),
            P(("grp", "seq"), None),
            P(("grp", "seq")),
            P(("grp", "seq")),
            P(("grp", "seq"), None),
            P(("grp", "seq")),
            P(("grp", "seq")),
            P(("grp", "seq")),
            P(("grp", "seq"), None),
            P(("grp", "seq")),
            P(("grp", "seq"), None),
            P(("grp", "seq")),
            P(("grp", "seq")),
            P(("grp", "seq")),
            P(),
            P(),
            P(),
            P(),
            P(),
            P(),
            P(),
        ),
        check_vma=False,
    )
```

profile of v0, /device:TPU:0, one launch (start us, length us, event | category | flops | bytes accessed | tf_op | source)
XLA Modules:
  0.0 1756.2 jit_solution(9419621637809130699)
XLA Ops:
  8.9 65.5 %all-gather.7.cloned.1.call-done = bf16[768,2304]{1,0:T(8,128)(2,1)} async-done(((bf16[24,2304]{1,0:T(8,128)(2,1)}), bf16[768,2304]{1,0:T(8,128)(2,1)}) %all-gather.7.cloned.1.call-update) | async-done | bytes 3538960 | tf_op jit(solution)/shard_map/all_gather | solution.py:118
  91.9 39.3 %all-reduce.20 = (bf16[768]{0:T(1024)(128)(2,1)S(1)}, bf16[768]{0:T(1024)(128)(2,1)S(1)}, bf16[768]{0:T(1024)(128)(2,1)S(1)}, bf16[768]{0:T(1024)(128)(2,1)S(1)}...) all-reduce(bf16[768]{0:T(1024)(128)(2,1)S(1)} %dynamic-update-slice, ...), channel_id=1, replica_groups=mesh['grp'=8,'seq'=4] {'grp','seq'}, use_global_device_ids=true, to_apply=%add.2 | all-reduce | flops 9216 | bytes 36864
  244.1 156.4 %while.32 = (s32[]{:T(128)}, bf16[2,2,256,12,64]{2,1,0,4,3:T(2,128)(2,1)}, f32[2,2,12,256,1]{3,1,2,4,0:T(2,128)S(1)}, bf16[2,2,256,12,64]{2,4,1,3,0:T(8,128)(2,1...) while((s32[]{:T(128)}, ...), condition=%wide.region_7.8_spmd.clone, body=%wide.region_2.7_spmd.clone.sunk | while | flops 3756845056 | bytes 228091088 | solution.py:219
  252.3 21.2 %bitcast_reduce_fusion.4 = (f32[2,12,256]{2,0,1:T(2,128)S(1)}, f32[12,2,256,2048]{3,2,1,0:T(8,128)}) fusion(bf16[2048,12,64]{0,2,1:T(8,128)(2,1)S(1)} %get-tuple-element.684, bf16[2,2,256,12,64]{2,4,1,3,0:T(8,128)(2,1)} %get-tuple-element.683, s32[]{:T(128)S(6)} %copy.390), kind=kOutput, calls=%fused_computation.3.clone.1 | convolution fusion | flops 1635772416 | bytes 54288388 | tf_op jit(solution)/shard_map/while/body/eval_jaxpr/nqhd,khd->nhqk/dot_general | solution.py:187
  273.6 21.1 %fusion.250 = f32[2,12,256]{2,0,1:T(2,128)S(1)} fusion(f32[12,2,256,2048]{3,2,1,0:T(8,128)} %get-tuple-element.637, f32[2,12,256]{2,0,1:T(2,128)S(1)} %copy_maximum_fusion.2), kind=kLoop, calls=%fused_computation.6.clone.1 | loop fusion | flops 37742592 | bytes 50380800 | tf_op jit(solution)/shard_map/while/body/eval_jaxpr/reduce_sum | solution.py:204
  330.4 21.4 %bitcast_reduce_fusion.4 = (f32[2,12,256]{2,0,1:T(2,128)S(1)}, f32[12,2,256,2048]{3,2,1,0:T(8,128)}) fusion(bf16[2048,12,64]{0,2,1:T(8,128)(2,1)S(1)} %get-tuple-element.684, bf16[2,2,256,12,64]{2,4,1,3,0:T(8,128)(2,1)} %get-tuple-element.683, s32[]{:T(128)S(6)} %copy.390), kind=kOutput, calls=%fused_computation.3.clone.1 | convolution fusion | flops 1635772416 | bytes 54288388 | tf_op jit(solution)/shard_map/while/body/eval_jaxpr/nqhd,khd->nhqk/dot_general | solution.py:187
  351.8 20.9 %fusion.250 = f32[2,12,256]{2,0,1:T(2,128)S(1)} fusion(f32[12,2,256,2048]{3,2,1,0:T(8,128)} %get-tuple-element.637, f32[2,12,256]{2,0,1:T(2,128)S(1)} %copy_maximum_fusion.2), kind=kLoop, calls=%fused_computation.6.clone.1 | loop fusion | flops 37742592 | bytes 50380800 | tf_op jit(solution)/shard_map/while/body/eval_jaxpr/reduce_sum | solution.py:204
  413.3 54.2 %multiply_convert_fusion.2 = (bf16[1536,3072]{1,0:T(8,128)(2,1)}, f32[1536,3072]{1,0:T(8,128)}, f32[1536,3072]{1,0:T(8,128)}) fusion(f32[3072]{0:T(1024)S(1)} %copy-done.74, bf16[768,3072]{1,0:T(8,128)(2,1)} %all-gather.15.cloned.1.call-done, f32[1536,768]{1,0:T(8,128)} %copy-done.13, f32[768]{0:T(1024)S(1)} %copy-done.79, f32[768]{0:T(1024)S(1)} %copy-done.71, ...), kind=kOutput, calls=%fused_computation.107 | convolution fusion | flops 7565082624 | bytes 56653824 | tf_op jit(solution)/shard_map/dot_general | solution.py:26
  502.9 27.1 %fusion.162 = (f32[3072]{0:T(1024)}, bf16[1536,3072]{1,0:T(8,128)(2,1)}) fusion(f32[1536,3072]{1,0:T(8,128)} %get-tuple-element.467, bf16[3072,768]{1,0:T(8,128)(2,1)} %all-gather.17.cloned.1.call-done, f32[1536,768]{1,0:T(8,128)} %get-tuple-element.465, f32[1536]{0:T(1024)S(1)} %negate_multiply_fusion.2, f32[1536,3072]{1,0:T(8,128)} %get-tuple-element.492, ...), kind=kOutput, calls=%fused_computation.258 | convolution fusion | flops 7325611008 | bytes 56653824 | tf_op jit(solution)/shard_map/dot_general | solution.py:36
  553.5 21.6 %fusion.89 = f32[2048,12,64]{0,2,1:T(8,128)} fusion(bf16[512,12,64]{0,2,1:T(8,128)(2,1)S(1)} %bitcast.442, f32[12,512,2048]{2,1,0:T(8,128)} %get-tuple-element.489, f32[12,512]{1,0:T(8,128)S(1)} %copy-done.38), kind=kOutput, calls=%fused_computation.152 | convolution fusion | flops 1648361472 | bytes 57434112 | tf_op jit(solution)/shard_map/hqk,qhd->khd/dot_general | solution.py:329
  575.1 32.7 %multiply_reduce_fusion.1 = (f32[12,512]{1,0:T(8,128)S(1)}, f32[12,512,2048]{2,1,0:T(8,128)}) fusion(f32[12,512,2048]{2,1,0:T(8,128)} %get-tuple-element.489, f32[12,512]{1,0:T(8,128)S(1)} %copy-done.38, bf16[512,12,64]{0,2,1:T(8,128)(2,1)} %bitcast.443, bf16[2048,12,64]{0,2,1:T(8,128)(2,1)S(1)} %copy-done.8), kind=kOutput, calls=%fused_computation.93 | convolution fusion | flops 1660938240 | bytes 104644608 | tf_op jit(solution)/shard_map/qhd,khd->hqk/dot_general | solution.py:314
  611.6 40.5 %multiply_convert_fusion.1 = bf16[12,512,2048]{2,1,0:T(8,128)(2,1)} fusion(f32[12,512,2048]{2,1,0:T(8,128)} %get-tuple-element.499, f32[12,512,2048]{2,1,0:T(8,128)} %get-tuple-element.489, f32[12,512]{1,0:T(8,128)S(1)} %get-tuple-element.498, f32[12,512]{1,0:T(8,128)S(1)} %copy-done.38), kind=kLoop, calls=%fused_computation.92 | loop fusion | flops 62914560 | bytes 125878272 | tf_op jit(solution)/shard_map/convert_element_type | solution.py:318
  667.8 347.4 %while.33 = (s32[]{:T(128)}, f32[2048,12,64]{0,2,1:T(8,128)}, f32[2048,12,64]{0,2,1:T(8,128)}, f32[2,2,256,12,64]{2,4,1,3,0:T(8,128)}, bf16[2,2,256,12,64]{2,4,3...) while((s32[]{:T(128)}, f32[2048,12,64]{0,2,1:T(8,128)}, ...), condition=%wide.region_25.26_spmd.clone, body=%wide.region_22.25_spmd.clone.sunk | while | flops 9240242176 | bytes 558320000 | solution.py:370
  700.9 23.5 %bitcast_add_fusion.8 = f32[2048,12,64]{0,2,1:T(8,128)} fusion(f32[2048,12,64]{0,2,1:T(8,128)} %get-tuple-element.705, f32[12,2,256,2048]{3,2,1,0:T(8,128)} %fusion.269, f32[2,12,256]{2,0,1:T(2,128)S(1)} %dynamic-slice_bitcast_fusion.25, bf16[1,2,256,12,64]{2,1,0,4,3:T(2,128)(2,1)} %copy-done.7), kind=kOutput, calls=%fused_computation.46.clone.1 | convolution fusion | flops 1649934336 | bytes 63725568 | tf_op jit(solution)/shard_map/while/body/eval_jaxpr/nhqk,nqhd->khd/dot_general | solution.py:365
  724.4 34.5 %fusion.270 = (f32[2,12,256]{2,0,1:T(2,128)S(1)}, f32[12,2,256,2048]{3,2,1,0:T(8,128)}) fusion(f32[12,2,256,2048]{3,2,1,0:T(8,128)} %fusion.269, f32[2,12,256]{2,0,1:T(2,128)S(1)} %dynamic-slice_bitcast_fusion.25, bf16[2048,12,64]{0,2,1:T(8,128)(2,1)} %get-tuple-element.727, bf16[1,2,256,12,64]{2,1,0,4,3:T(2,128)(2,1)} %copy-done.7), kind=kOutput, calls=%fused_computation.37.clone.1 | convolution fusion | flops 1660938240 | bytes 104644608 | tf_op jit(solution)/shard_map/while/body/eval_jaxpr/nqhd,khd->nhqk/dot_general | solution.py:338
  758.9 40.4 %fusion.272 = bf16[2,12,256,2048]{3,2,0,1:T(8,128)(2,1)} fusion(f32[12,2,256,2048]{3,2,1,0:T(8,128)} %get-tuple-element.657, f32[12,2,256,2048]{3,2,1,0:T(8,128)} %fusion.269, f32[2,12,256]{2,0,1:T(2,128)S(1)} %copy_add_fusion.4, f32[2,12,256]{2,0,1:T(2,128)S(1)} %dynamic-slice_bitcast_fusion.25), kind=kLoop, calls=%fused_computation.39.clone.1 | loop fusion | flops 62914560 | bytes 125878272 | tf_op jit(solution)/shard_map/while/body/eval_jaxpr/convert_element_type | solution.py:347
  874.4 23.5 %bitcast_add_fusion.8 = f32[2048,12,64]{0,2,1:T(8,128)} fusion(f32[2048,12,64]{0,2,1:T(8,128)} %get-tuple-element.705, f32[12,2,256,2048]{3,2,1,0:T(8,128)} %fusion.269, f32[2,12,256]{2,0,1:T(2,128)S(1)} %dynamic-slice_bitcast_fusion.25, bf16[1,2,256,12,64]{2,1,0,4,3:T(2,128)(2,1)} %copy-done.7), kind=kOutput, calls=%fused_computation.46.clone.1 | convolution fusion | flops 1649934336 | bytes 63725568 | tf_op jit(solution)/shard_map/while/body/eval_jaxpr/nhqk,nqhd->khd/dot_general | solution.py:365
  897.9 34.4 %fusion.270 = (f32[2,12,256]{2,0,1:T(2,128)S(1)}, f32[12,2,256,2048]{3,2,1,0:T(8,128)}) fusion(f32[12,2,256,2048]{3,2,1,0:T(8,128)} %fusion.269, f32[2,12,256]{2,0,1:T(2,128)S(1)} %dynamic-slice_bitcast_fusion.25, bf16[2048,12,64]{0,2,1:T(8,128)(2,1)} %get-tuple-element.727, bf16[1,2,256,12,64]{2,1,0,4,3:T(2,128)(2,1)} %copy-done.7), kind=kOutput, calls=%fused_computation.37.clone.1 | convolution fusion | flops 1660938240 | bytes 104644608 | tf_op jit(solution)/shard_map/while/body/eval_jaxpr/nqhd,khd->nhqk/dot_general | solution.py:338
  932.4 40.4 %fusion.272 = bf16[2,12,256,2048]{3,2,0,1:T(8,128)(2,1)} fusion(f32[12,2,256,2048]{3,2,1,0:T(8,128)} %get-tuple-element.657, f32[12,2,256,2048]{3,2,1,0:T(8,128)} %fusion.269, f32[2,12,256]{2,0,1:T(2,128)S(1)} %copy_add_fusion.4, f32[2,12,256]{2,0,1:T(2,128)S(1)} %dynamic-slice_bitcast_fusion.25), kind=kLoop, calls=%fused_computation.39.clone.1 | loop fusion | flops 62914560 | bytes 125878272 | tf_op jit(solution)/shard_map/while/body/eval_jaxpr/convert_element_type | solution.py:347
  1174.7 42.0 %all-reduce.18 = (f32[768]{0:T(1024)S(1)}, f32[768]{0:T(1024)S(1)}, f32[768]{0:T(1024)S(1)}, f32[768]{0:T(1024)S(1)}, f32[768]{0:T(1024)S(1)}, /*index=5*/f32[30...) all-reduce(f32[768]{0:T(1024)S(1)} %reduce_sum.353, ...), channel_id=5, replica_groups=mesh['grp'=8,'seq'=4] {'grp','seq'}, use_global_device_ids=true, to_apply=%region_31.32.clone | all-reduce | flops 11406 | bytes 91248
  1232.7 105.9 %reduce-scatter.13.cloned.1.call-done = f32[24,768]{1,0:T(8,128)} async-done(((f32[768,768]{1,0:T(8,128)}), f32[24,768]{1,0:T(8,128)}) %reduce-scatter.13.cloned.1.call-update) | async-done | bytes 73744 | tf_op jit(solution)/shard_map/reduce_scatter | solution.py:415
  1338.6 141.2 %reduce-scatter.17.cloned.1.call-done = f32[96,768]{1,0:T(8,128)} async-done(((f32[3072,768]{1,0:T(8,128)}), f32[96,768]{1,0:T(8,128)}) %reduce-scatter.17.cloned.1.call-update) | async-done | bytes 294928 | tf_op jit(solution)/shard_map/reduce_scatter | solution.py:421
  1479.8 141.9 %reduce-scatter.15.cloned.1.call-done = f32[24,3072]{1,0:T(8,128)} async-done(((f32[768,3072]{1,0:T(8,128)}), f32[24,3072]{1,0:T(8,128)}) %reduce-scatter.15.cloned.1.call-update) | async-done | bytes 294928 | tf_op jit(solution)/shard_map/reduce_scatter | solution.py:419
  1621.7 124.4 %reduce-scatter.19.cloned.1.call-done = f32[24,2304]{1,0:T(8,128)} async-done(((f32[768,2304]{1,0:T(8,128)}), f32[24,2304]{1,0:T(8,128)}) %reduce-scatter.19.cloned.1.call-update) | async-done | bytes 221200
  (504 shorter events, 621.5 us)
Async XLA Ops:
  7.2 479.6 %copy-start = (f32[128,128]{1,0:T(8,128)S(1)}, f32[128,128]{1,0:T(8,128)}, u32[]{:S(2)}) copy-start(f32[128,128]{1,0:T(8,128)} %param.50) | copy-start | bytes 196612
  7.2 67.2 %all-gather.7.cloned.1.call-start = ((), (), s32[]{:S(2)}) async-start(), calls=%async_computation.6 | async-start | bytes 3649536 | tf_op jit(solution)/shard_map/all_gather | solution.py:118
  8.9 164.9 %all-gather.11.cloned.1.call-start = ((), (), s32[]{:S(2)}) async-start(), calls=%async_computation.8 | async-start | bytes 3932160 | tf_op jit(solution)/shard_map/all_gather | solution.py:148
  89.7 129.0 %all-gather.9.cloned.1.call-start = ((), (), s32[]{:S(2)}) async-start(), calls=%async_computation.7 | async-start | bytes 3932160 | tf_op jit(solution)/shard_map/all_gather | solution.py:149
  138.2 266.6 %all-gather.13.cloned.1.call-start = ((), (), s32[]{:S(2)}) async-start(), calls=%async_computation.9 | async-start | bytes 1216512 | tf_op jit(solution)/shard_map/all_gather | solution.py:121
  139.8 273.5 %all-gather.15.cloned.1.call-start = ((), (), s32[]{:S(2)}) async-start(), calls=%async_computation.10 | async-start | bytes 4866048 | tf_op jit(solution)/shard_map/all_gather | solution.py:125
  140.5 327.0 %all-gather.17.cloned.1.call-start = ((), (), s32[]{:S(2)}) async-start(), calls=%async_computation.11 | async-start | bytes 4866048 | tf_op jit(solution)/shard_map/all_gather | solution.py:127
  142.2 985.0 %reduce-scatter.9.cloned.1.call-start = ((), (), s32[]{:S(2)}) async-start(), calls=%async_computation.12 | async-start | bytes 3932160 | tf_op jit(solution)/shard_map/reduce_scatter | solution.py:386
  244.1 160.6 %copy-start.82 = (f32[768]{0:T(1024)S(1)}, f32[768]{0:T(1024)}, u32[]{:S(2)}) copy-start(f32[768]{0:T(1024)} %convert_element_type.194) | copy-start | bytes 9220
  273.6 21.1 %copy-start.5 = (f32[2,12,256,256]{2,3,1,0:T(8,128)S(1)}, f32[2,12,256,256]{2,3,1,0:T(8,128)}, u32[]{:S(2)}) copy-start(f32[2,12,256,256]{2,3,1,0:T(8,128)} %get-tuple-element.640) | copy-start | bytes 18874372 | tf_op jit(solution)/shard_map/while
  409.9 135.4 %copy-start.47 = (f32[1536]{0:T(1024)}, f32[1536]{0:T(1024)S(1)}, u32[]{:S(2)}) copy-start(f32[1536]{0:T(1024)S(1)} %broadcast_multiply_fusion.1) | copy-start | bytes 18436
  413.3 132.0 %copy-start.56 = (f32[1536]{0:T(1024)}, f32[1536]{0:T(1024)S(1)}, u32[]{:S(2)}) copy-start(f32[1536]{0:T(1024)S(1)} %fusion.129) | copy-start | bytes 18436
  413.3 54.3 %copy-start.81 = (f32[768]{0:T(1024)S(1)}, f32[768]{0:T(1024)}, u32[]{:S(2)}) copy-start(f32[768]{0:T(1024)} %convert_element_type.206) | copy-start | bytes 9220
  502.9 27.1 %copy-start.54 = (f32[1536]{0:T(1024)}, f32[1536]{0:T(1024)S(1)}, u32[]{:S(2)}) copy-start(f32[1536]{0:T(1024)S(1)} %negate_multiply_fusion.2) | copy-start | bytes 18436
  553.5 21.6 %copy-start.8 = (bf16[2048,12,64]{0,2,1:T(8,128)(2,1)S(1)}, bf16[2048,12,64]{0,2,1:T(8,128)(2,1)}, u32[]{:S(2)}) copy-start(bf16[2048,12,64]{0,2,1:T(8,128)(2,1)} %get-tuple-element.775) | copy-start | bytes 9437188
  1020.2 108.5 %reduce-scatter.11.cloned.1.call-start = ((), (), s32[]{:S(2)}) async-start(), calls=%async_computation.13 | async-start | bytes 3932160 | tf_op jit(solution)/shard_map/reduce_scatter | solution.py:392
  1025.2 207.5 %all-reduce.23.cloned.1.call-start = ((), (), s32[]{:S(2)}) async-start(), calls=%async_computation.18 | async-start | bytes 917504 | tf_op jit(solution)/shard_map/psum | solution.py:268
  1029.0 309.6 %reduce-scatter.13.cloned.1.call-start = ((), (), s32[]{:S(2)}) async-start(), calls=%async_computation.14 | async-start | bytes 2433024 | tf_op jit(solution)/shard_map/reduce_scatter | solution.py:415
  1036.0 443.8 %reduce-scatter.17.cloned.1.call-start = ((), (), s32[]{:S(2)}) async-start(), calls=%async_computation.16 | async-start | bytes 9732096 | tf_op jit(solution)/shard_map/reduce_scatter | solution.py:421
  1050.6 571.1 %reduce-scatter.15.cloned.1.call-start = ((), (), s32[]{:S(2)}) async-start(), calls=%async_computation.15 | async-start | bytes 9732096 | tf_op jit(solution)/shard_map/reduce_scatter | solution.py:419
  1066.0 680.2 %reduce-scatter.19.cloned.1.call-start = ((), (), s32[]{:S(2)}) async-start(), calls=%async_computation.17 | async-start | bytes 7299072
  1166.4 55.5 %copy-start.23 = (f32[512,768]{0,1:T(8,128)S(1)}, f32[512,768]{0,1:T(8,128)}, u32[]{:S(2)}) copy-start(f32[512,768]{0,1:T(8,128)} %copy-done.22) | copy-start | bytes 4718596
  1166.4 55.5 %copy-start.25 = (f32[512,768]{0,1:T(8,128)S(1)}, f32[512,768]{0,1:T(8,128)}, u32[]{:S(2)}) copy-start(f32[512,768]{0,1:T(8,128)} %copy-done.24) | copy-start | bytes 4718596
  1221.4 528.0 %copy-start.1 = (f32[128,128]{1,0:T(8,128)S(1)}, f32[128,128]{1,0:T(8,128)}, u32[]{:S(2)}) copy-start(f32[128,128]{1,0:T(8,128)} %param.50) | copy-start | bytes 196612
  (109 other events, 690.0 us)
Sparse Core Ops, SparseCore 0:
  11.5 62.8 all-gather.6
  89.8 27.8 all-gather.10
  138.3 28.6 all-gather.8
  170.4 54.1 all-gather.12
  227.9 62.4 all-gather.14
  293.7 62.3 all-gather.16
  1020.3 38.0 reduce-scatter.8
  1061.7 37.9 reduce-scatter.10
  1105.7 126.3 all-reduce.22
  1238.6 99.9 reduce-scatter.12
  1345.1 134.6 reduce-scatter.16
  1487.1 134.5 reduce-scatter.14
  1628.0 118.1 reduce-scatter.18
where the time goes:
time: 1760 us
  matrix products  684 us (39%)
  waiting for transfers between devices  579 us (33%)
  other arithmetic  267 us (15%)
  local copies, waits for them, and re-layouts  127 us (7%)
  blocking collectives  81.3 us (5%)
    reduce_scatter x1, waiting for transfers between devices, local(): lax.psum_scatter(d_expand_weight, ('grp', 'seq'), scatter_dimension=0, ti...  142 us
    reduce_scatter x1, waiting for transfers between devices, local(): lax.psum_scatter(d_reduce_weight, ('grp', 'seq'), scatter_dimension=0, ti...  141 us
    unnamed x14, waiting for transfers between devices  125 us
    reduce_scatter x1, waiting for transfers between devices, local(): lax.psum_scatter(d_output_weight, ('grp', 'seq'), scatter_dimension=0, ti...  106 us
    dot_general x5, matrix products, matmul(): return jnp.dot(left, right, preferred_element_type=jnp.float32)  84.3 us
    dot_general x4, matrix products, block_scores(): jnp.einsum('nqhd,khd->nhqk', query_block, far_keys, preferred_element_typ...  83.5 us
    unnamed x2, blocking collectives  81.3 us
    convert_element_type x2, other arithmetic, block_backward(): far_ds = (far_p * (far_dp - delta)).astype(brain)  80.8 us
  transfers between devices with their start and end apart: 13, of which 5 were waited for; matrix products, arithmetic and copies ran while one was open for 28% of the time, Pallas kernels for 0%

commit v1 on v0

v1 whole, which is shorter than its diff:
```python
import functools

import jax
import jax.numpy as jnp
from jax import lax
from jax.experimental import pallas as pl
from jax.experimental.pallas import tpu as pltpu
from jax.sharding import PartitionSpec as P

HEAD_DIM = 64
POOL_HEADS = 2
PAIR = 2 * HEAD_DIM

EPSILON = 1e-06
HIGHEST = lax.Precision.HIGHEST
NEGATIVE = -1e30
BOTH = ("grp", "seq")
BF16 = jnp.bfloat16
F32 = jnp.float32
LOG2_E = 1.4426950408889634
SUM_LOW, SUM_HIGH = 1e-12, 1e18
VMEM_LIMIT = 56 << 20


def dot(left, right, left_dim, right_dim):
    return lax.dot_general(
        left, right, (((left_dim,), (right_dim,)), ((), ())), preferred_element_type=F32
    )


def precise(left, right):
    return jnp.dot(left, right, precision=HIGHEST, preferred_element_type=F32)


def attention_forward_kernel(near, *refs):
    if near:
        q_ref, k_ref, v_ref, kn_ref, vn_ref, out_ref, inv_ref, exp_ref, vt_ref, s_ref = refs
    else:
        q_ref, k_ref, v_ref, out_ref, inv_ref, exp_ref, vt_ref, s_ref = refs
    far = k_ref.shape[0]
    tile = q_ref.shape[0]

    @pl.when(pl.program_id(1) == 0)
    def _():
        vt_ref[...] = v_ref[...].T

    q = q_ref[...]
    lane = lax.broadcasted_iota(jnp.int32, q.shape, 1)
    masked = [
        jnp.where((lane < HEAD_DIM) if h == 0 else (lane >= HEAD_DIM), q, jnp.zeros_like(q))
        for h in range(2)
    ]
    heads = [slice(h * HEAD_DIM, (h + 1) * HEAD_DIM) for h in range(2)]
    if near:
        vnt = vn_ref[...].T
        allowed = lax.broadcasted_iota(jnp.int32, (tile, tile), 0) <= lax.broadcasted_iota(
            jnp.int32, (tile, tile), 1
        )

    def near_scores(h):
        return jnp.where(allowed, dot(kn_ref[...], masked[h], 1, 1), NEGATIVE)

    def finish(outs):
        out_ref[...] = jnp.concatenate(outs, 0).T.astype(out_ref.dtype)

    outs = []
    fine = None
    for h in range(2):
        e = jnp.exp2(dot(k_ref[...], masked[h], 1, 1) * LOG2_E)
        total = jnp.sum(e, axis=0, keepdims=True)
        low = e.astype(BF16)
        exp_ref[0, 0, h, 0:far, :] = low
        out = dot(vt_ref[heads[h], :], low, 1, 0)
        if near:
            e = jnp.exp2(near_scores(h) * LOG2_E)
            total = total + jnp.sum(e, axis=0, keepdims=True)
            low = e.astype(BF16)
            exp_ref[0, 0, h, far:, :] = low
            out = out + dot(vnt[heads[h], :], low, 1, 0)
        inverse = 1.0 / total
        inv_ref[0, 0, h : h + 1, :] = inverse
        outs.append(out * inverse)
        good = jnp.where((total > SUM_LOW) & (total < SUM_HIGH), 1.0, 0.0)
        fine = good if fine is None else jnp.minimum(fine, good)
    finish(outs)

    @pl.when(jnp.min(fine) < 0.5)
    def _():
        chunk = tile
        steps = far // chunk
        outs = []
        for h in range(2):

            def score(c, top):
                at = pl.multiple_of(c * chunk, chunk)
                s = dot(k_ref[pl.ds(at, chunk), :], masked[h], 1, 1)
                s_ref[pl.ds(at, chunk), :] = s
                return jnp.maximum(top, jnp.max(s, axis=0, keepdims=True))

            top = jnp.full((1, tile), NEGATIVE, F32)
            if near:
                sn = near_scores(h)
                top = jnp.max(sn, axis=0, keepdims=True)
            top = lax.fori_loop(0, steps, score, top)

            def weigh(c, carry):
                total, out = carry
                at = pl.multiple_of(c * chunk, chunk)
                e = jnp.exp2((s_ref[pl.ds(at, chunk), :] - top) * LOG2_E)
                low = e.astype(BF16)
                exp_ref[0, 0, h, pl.ds(at, chunk), :] = low
                part = dot(v_ref[pl.ds(at, chunk), :], low, 0, 0)[heads[h], :]
                return total + jnp.sum(e, axis=0, keepdims=True), out + part

            total = jnp.zeros((1, tile), F32)
            out = jnp.zeros((HEAD_DIM, tile), F32)
            if near:
                e = jnp.exp2((sn - top) * LOG2_E)
                low = e.astype(BF16)
                exp_ref[0, 0, h, far:, :] = low
                total = jnp.sum(e, axis=0, keepdims=True)
                out = dot(vnt[heads[h], :], low, 1, 0)
            total, out = lax.fori_loop(0, steps, weigh, (total, out))
            inverse = 1.0 / total
            inv_ref[0, 0, h : h + 1, :] = inverse
            outs.append(out * inverse)
        finish(outs)


def attention_forward(queries, q_at, far_kv, far, near_at, count, tile):
    near = near_at is not None
    width = queries.shape[1]
    pairs = width // PAIR
    tiles = count // tile
    held = far + (tile if near else 0)
    at = q_at // tile
    specs = [
        pl.BlockSpec((tile, PAIR), lambda h, t: (at + t, h)),
        pl.BlockSpec((far, PAIR), lambda h, t: (0, h)),
        pl.BlockSpec((far, PAIR), lambda h, t: (0, pairs + h)),
    ]
    operands = [queries, far_kv, far_kv]
    if near:
        first = near_at // tile
        specs += [
            pl.BlockSpec((tile, PAIR), lambda h, t: (first + t, h)),
            pl.BlockSpec((tile, PAIR), lambda h, t: (first + t, pairs + h)),
        ]
        operands += [far_kv, far_kv]
    cells = count * held * width // HEAD_DIM
    return pl.pallas_call(
        functools.partial(attention_forward_kernel, near),
        grid=(pairs, tiles),
        in_specs=specs,
        out_specs=[
            pl.BlockSpec((tile, PAIR), lambda h, t: (t, h)),
            pl.BlockSpec((1, 1, 2, tile), lambda h, t: (h, t, 0, 0)),
            pl.BlockSpec((1, 1, 2, held, tile), lambda h, t: (h, t, 0, 0, 0)),
        ],
        out_shape=[
            jax.ShapeDtypeStruct((count, width), BF16),
            jax.ShapeDtypeStruct((pairs, tiles, 2, tile), F32),
            jax.ShapeDtypeStruct((pairs, tiles, 2, held, tile), BF16),
        ],
        scratch_shapes=[pltpu.VMEM((PAIR, far), BF16), pltpu.VMEM((far, tile), F32)],
        compiler_params=pltpu.CompilerParams(vmem_limit_bytes=VMEM_LIMIT),
        cost_estimate=pl.CostEstimate(
            flops=4 * cells * HEAD_DIM, bytes_accessed=2 * cells, transcendentals=cells
        ),
        name="attention_forward",
    )(*operands)


def attention_backward_kernel(near, *refs):
    if near:
        (
            q_ref,
            k_ref,
            v_ref,
            kn_ref,
            vn_ref,
            out_ref,
            dout_ref,
            inv_ref,
            exp_ref,
            dk_in_ref,
            dv_in_ref,
            dq_ref,
            dkn_ref,
            dvn_ref,
            dk_ref,
            dv_ref,
            kt_ref,
            dkt_ref,
            dvt_ref,
        ) = refs
    else:
        (
            q_ref,
            k_ref,
            v_ref,
            out_ref,
            dout_ref,
            inv_ref,
            exp_ref,
            dq_ref,
            dk_ref,
            dv_ref,
            kt_ref,
            dkt_ref,
            dvt_ref,
        ) = refs
    far = k_ref.shape[0]
    tile = q_ref.shape[0]
    at = pl.program_id(1)

    @pl.when(at == 0)
    def _():
        kt_ref[...] = k_ref[...].T
        if near:
            dkt_ref[...] = dk_in_ref[...]
            dvt_ref[...] = dv_in_ref[...]
        else:
            dkt_ref[...] = jnp.zeros_like(dkt_ref)
            dvt_ref[...] = jnp.zeros_like(dvt_ref)

    qt = q_ref[...].T
    dout = dout_ref[...].astype(F32).T
    product = out_ref[...].astype(F32).T * dout
    if near:
        knt = kn_ref[...].T
    zero = jnp.zeros((HEAD_DIM, tile), BF16)
    dqs, dkn, dvn = [], [], []
    for h in range(2):
        rows = slice(h * HEAD_DIM, (h + 1) * HEAD_DIM)
        inverse = inv_ref[0, 0, h : h + 1, :]
        delta = jnp.sum(product[rows, :], axis=0, keepdims=True) * inverse
        do = (dout[rows, :] * inverse).astype(BF16)
        padded = jnp.concatenate([do, zero] if h == 0 else [zero, do], 0)
        e = exp_ref[0, 0, h, 0:far, :]
        ds = (e.astype(F32) * (dot(v_ref[...], padded, 1, 0) - delta)).astype(BF16)
        dvt_ref[rows, :] += dot(do, e, 1, 1)
        dkt_ref[rows, :] += dot(qt[rows, :], ds, 1, 1)
        dq = dot(kt_ref[rows, :], ds, 1, 0)
        if near:
            e = exp_ref[0, 0, h, far:, :]
            ds = (e.astype(F32) * (dot(vn_ref[...], padded, 1, 0) - delta)).astype(BF16)
            dvn.append(dot(do, e, 1, 1))
            dkn.append(dot(qt[rows, :], ds, 1, 1))
            dq = dq + dot(knt[rows, :], ds, 1, 0)
        dqs.append(dq * HEAD_DIM ** (-0.5))
    dq_ref[...] = jnp.concatenate(dqs, 0).T.astype(dq_ref.dtype)
    if near:
        dkn_ref[...] = jnp.concatenate(dkn, 0).T.astype(dkn_ref.dtype)
        dvn_ref[...] = jnp.concatenate(dvn, 0).T.astype(dvn_ref.dtype)

    @pl.when(at == pl.num_programs(1) - 1)
    def _():
        if near:
            dk_ref[...] = dkt_ref[...].T.astype(dk_ref.dtype)
            dv_ref[...] = dvt_ref[...].T.astype(dv_ref.dtype)
        else:
            dk_ref[...] = dkt_ref[...]
            dv_ref[...] = dvt_ref[...]


def attention_backward(
    queries, q_at, far_kv, far, near_at, context, d_context, inverse, held_exp, sums, tile, h0, nh
):
    near = sums is not None
    width = queries.shape[1]
    pairs = width // PAIR
    count = context.shape[0]
    tiles = count // tile
    held = held_exp.shape[3]
    at = q_at // tile
    specs = [
        pl.BlockSpec((tile, PAIR), lambda h, t: (at + t, h0 + h)),
        pl.BlockSpec((far, PAIR), lambda h, t: (0, h0 + h)),
        pl.BlockSpec((far, PAIR), lambda h, t: (0, pairs + h0 + h)),
    ]
    operands = [queries, far_kv, far_kv]
    if near:
        first = near_at // tile
        specs += [
            pl.BlockSpec((tile, PAIR), lambda h, t: (first + t, h0 + h)),
            pl.BlockSpec((tile, PAIR), lambda h, t: (first + t, pairs + h0 + h)),
        ]
        operands += [far_kv, far_kv]
    specs += [
        pl.BlockSpec((tile, PAIR), lambda h, t: (t, h0 + h)),
        pl.BlockSpec((tile, PAIR), lambda h, t: (at + t, h0 + h)),
        pl.BlockSpec((1, 1, 2, tile), lambda h, t: (h0 + h, t, 0, 0)),
        pl.BlockSpec((1, 1, 2, held, tile), lambda h, t: (h0 + h, t, 0, 0, 0)),
    ]
    operands += [context, d_context, inverse, held_exp]
    turned = pl.BlockSpec((PAIR, far), lambda h, t: (h, 0))
    row = pl.BlockSpec((tile, PAIR), lambda h, t: (t, h))
    row_shape = jax.ShapeDtypeStruct((count, nh * PAIR), BF16)
    if near:
        specs += [turned, turned]
        operands += list(sums)
        column = pl.BlockSpec((far, PAIR), lambda h, t: (0, h))
        column_shape = jax.ShapeDtypeStruct((far, nh * PAIR), BF16)
    else:
        column = turned
        column_shape = jax.ShapeDtypeStruct((nh * PAIR, far), F32)
    cells = count * held * nh * 2
    return pl.pallas_call(
        functools.partial(attention_backward_kernel, near),
        grid=(nh, tiles),
        in_specs=specs,
        out_specs=[row] + ([row, row] if near else []) + [column, column],
        out_shape=[row_shape] * (3 if near else 1) + [column_shape] * 2,
        scratch_shapes=[
            pltpu.VMEM((PAIR, far), BF16),
            pltpu.VMEM((PAIR, far), F32),
            pltpu.VMEM((PAIR, far), F32),
        ],
        compiler_params=pltpu.CompilerParams(vmem_limit_bytes=VMEM_LIMIT),
        cost_estimate=pl.CostEstimate(
            flops=8 * cells * HEAD_DIM, bytes_accessed=2 * cells, transcendentals=0
        ),
        name="attention_backward",
    )(*operands)


def layer_norm(rows, gain, shift):
    center = rows - jnp.mean(rows, -1, keepdims=True)
    variance = jnp.mean(center * center, -1, keepdims=True)
    return center * lax.rsqrt(variance + EPSILON) * gain + shift


def gelu_pair(pre):
    half = 0.5 * (1.0 + lax.erf(pre * (0.5**0.5)))
    slope = half + pre * (jnp.exp(-0.5 * pre * pre) * 0.3989422804014327)
    return pre * half, slope


def head_forward(student, pool_query, pool_weight, pool_bias, class_weight, class_bias, labels):
    count, length, width = student.shape
    split = student.reshape(count, length, POOL_HEADS, width // POOL_HEADS)
    query = pool_query.reshape(POOL_HEADS, width // POOL_HEADS)
    scores = jnp.einsum("clhd,hd->chl", split, query, precision=HIGHEST) * (
        width // POOL_HEADS
    ) ** (-0.5)
    weights = jax.nn.softmax(scores, -1)
    pooled = jnp.einsum("chl,clhd->chd", weights, split, precision=HIGHEST).reshape(count, width)
    hidden = jnp.tanh(precise(pooled, pool_weight) + pool_bias)
    logits = precise(hidden, class_weight) + class_bias
    onehot = (labels[:, None] == jnp.arange(logits.shape[1], dtype=jnp.int32)[None, :]).astype(F32)
    loss = jnp.sum(jax.nn.logsumexp(logits, -1) - jnp.sum(onehot * logits, -1))
    return (loss, logits)


def gather(shard, axes=BOTH):
    return lax.all_gather(shard, axes, axis=0, tiled=True)


def local(
    prompt_in,
    cont_in,
    prompt_cot,
    cont_cot,
    labels,
    joint_weight,
    query_bias,
    value_bias,
    output_weight,
    output_bias,
    first_gain,
    first_shift,
    expand_weight,
    expand_bias,
    reduce_weight,
    reduce_bias,
    second_gain,
    second_shift,
    student_weight,
    student_bias,
    pool_query,
    pool_weight,
    pool_bias,
    class_weight,
    class_bias,
):
    prompt_rows = prompt_in[0]
    share, width = prompt_rows.shape
    _, conts, length, _ = cont_in.shape
    cont_count = conts * length
    part = joint_weight.shape[0]
    devices = width // part
    hidden_width = expand_weight.shape[1]
    tile = min(share, length)

    vectors = [
        query_bias,
        value_bias,
        output_bias,
        first_gain,
        first_shift,
        reduce_bias,
        second_gain,
        second_shift,
    ]
    beside = jnp.concatenate(
        [v[:, None] for v in vectors] + [expand_bias.reshape(part, hidden_width // width)], 1
    )
    beside = jnp.pad(beside, ((0, 0), (0, 128 - beside.shape[1])))
    joint_all = gather(jnp.concatenate([joint_weight, beside], 1).astype(BF16))
    prompt_all = gather(prompt_rows, "seq")
    far = prompt_all.shape[0]
    out_expand = gather(jnp.concatenate([output_weight, expand_weight], 1).astype(BF16))
    reduce_full = gather(reduce_weight.astype(BF16))
    joint_full = joint_all[:, : 3 * width]
    flat = joint_all[:, 3 * width :].astype(F32)
    qbias, vbias, obias, fgain, fshift, rbias, sgain, sshift = (flat[:, i] for i in range(8))
    ebias = flat[:, 8 : 8 + hidden_width // width].reshape(hidden_width)
    output_full = out_expand[:, :width]
    expand_full = out_expand[:, width:]

    cont_rows = cont_in[0].reshape(cont_count, width)
    rows = jnp.concatenate([prompt_rows, cont_rows], 0)
    key_rows = jnp.concatenate([prompt_all, cont_rows], 0)
    queries = (dot(rows, joint_full[:, :width], 1, 0) + qbias).astype(BF16) * HEAD_DIM ** (-0.5)
    kv_bias = jnp.concatenate([jnp.zeros_like(vbias), vbias])
    keys_values = (dot(key_rows, joint_full[:, width:], 1, 0) + kv_bias).astype(BF16)

    prompt_context, prompt_inv, prompt_exp = attention_forward(
        queries, 0, keys_values, far, None, share, tile
    )
    cont_context, cont_inv, cont_exp = attention_forward(
        queries, share, keys_values, far, far, cont_count, length
    )
    context = jnp.concatenate([prompt_context, cont_context], 0)

    branch = dot(context, output_full, 1, 0) + obias
    first, first_back = jax.vjp(layer_norm, rows.astype(F32) + branch, fgain, fshift)
    first_low = first.astype(BF16)
    activated, slope = gelu_pair(dot(first_low, expand_full, 1, 0) + ebias)
    hidden = activated.astype(BF16)
    slope = slope.astype(BF16)
    mixed = first + dot(hidden, reduce_full, 1, 0) + rbias
    layer, second_back = jax.vjp(layer_norm, mixed, sgain, sshift)
    layer_low = layer.astype(BF16)
    student_low = student_weight.astype(BF16)
    cont_layer = layer_low[share:]
    student = dot(cont_layer, student_low, 1, 0) + student_bias

    def head_piece(student_rows, query, pool_w, pool_b, class_w, class_b):
        return head_forward(
            student_rows.reshape(conts, length, student_rows.shape[1]),
            query,
            pool_w,
            pool_b,
            class_w,
            class_b,
            labels[0],
        )

    loss, head_back, logits = jax.vjp(
        head_piece,
        student,
        pool_query,
        pool_weight,
        pool_bias,
        class_weight,
        class_bias,
        has_aux=True,
    )
    d_student, d_query, d_pool_weight, d_pool_bias, d_class_weight, d_class_bias = head_back(
        jnp.ones_like(loss)
    )
    d_student_bias = jnp.sum(d_student, 0)
    d_student_low = d_student.astype(BF16)
    d_student_weight = dot(cont_layer, d_student_low, 0, 0)
    cotangent = jnp.concatenate(
        [
            prompt_cot[0].astype(F32),
            cont_cot[0].reshape(cont_count, width).astype(F32)
            + dot(d_student_low, student_low, 1, 1),
        ],
        0,
    )
    d_mixed, d_second_gain, d_second_shift = second_back(cotangent)
    d_reduce_bias = jnp.sum(d_mixed, 0)
    d_mixed_low = d_mixed.astype(BF16)
    d_reduce_weight = dot(hidden, d_mixed_low, 0, 0).astype(BF16)
    d_pre = dot(d_mixed_low, reduce_full, 1, 1) * slope.astype(F32)
    d_expand_bias = jnp.sum(d_pre, 0)
    d_pre_low = d_pre.astype(BF16)
    d_expand_weight = dot(first_low, d_pre_low, 0, 0).astype(BF16)
    d_first = d_mixed + dot(d_pre_low, expand_full, 1, 1)
    d_inner, d_first_gain, d_first_shift = first_back(d_first)
    d_output_bias = jnp.sum(d_inner, 0)
    d_inner_low = d_inner.astype(BF16)
    d_output_weight = dot(context, d_inner_low, 0, 0).astype(BF16)
    d_context = dot(d_inner_low, output_full, 1, 1).astype(BF16)

    blocks = [d_output_weight.reshape(devices, part, width)]
    blocks += [
        d_expand_weight[:, i * width : (i + 1) * width].reshape(devices, part, width)
        for i in range(hidden_width // width)
    ]
    blocks += [d_reduce_weight.reshape(devices, -1, width)]
    early = lax.psum_scatter(
        jnp.concatenate(blocks, 1), BOTH, scatter_dimension=0, tiled=True
    )[0].astype(F32)
    count = hidden_width // width
    output_grad = early[:part]
    expand_grad = jnp.concatenate(
        [early[part * (1 + i) : part * (2 + i)] for i in range(count)], 1
    )
    reduce_grad = early[part * (1 + count) :]

    pairs = width // PAIR
    dq_prompt, dk_sum, dv_sum = attention_backward(
        queries, 0, keys_values, far, None, prompt_context, d_context, prompt_inv, prompt_exp,
        None, tile, 0, pairs,
    )
    dq_cont, dk_cont, dv_cont, dk_far, dv_far = attention_backward(
        queries, share, keys_values, far, far, cont_context, d_context, cont_inv, cont_exp,
        (dk_sum, dv_sum), length, 0, pairs,
    )
    d_queries = jnp.concatenate([dq_prompt, dq_cont], 0)
    d_keys = jnp.concatenate([dk_far, dk_cont], 0)
    d_values = jnp.concatenate([dv_far, dv_cont], 0)
    d_query_bias = jnp.sum(d_queries.astype(F32), 0)
    d_value_bias = jnp.sum(d_values.astype(F32), 0)
    d_joint = jnp.concatenate(
        [
            dot(rows, d_queries, 0, 0),
            dot(key_rows, d_keys, 0, 0),
            dot(key_rows, d_values, 0, 0),
        ],
        1,
    ).astype(BF16)
    joint_grad = lax.psum_scatter(d_joint, BOTH, scatter_dimension=0, tiled=True).astype(F32)
    own = lax.psum_scatter(
        jnp.concatenate([dk_far, dv_far], 1), "seq", scatter_dimension=0, tiled=True
    )
    d_kv = jnp.concatenate([own, jnp.concatenate([dk_cont, dv_cont], 1)], 0)
    d_rows = (
        d_inner
        + dot(d_queries, joint_full[:, :width], 1, 1)
        + dot(d_kv, joint_full[:, width:], 1, 1)
    )

    head_grads = (
        d_student_weight,
        d_student_bias,
        d_query,
        d_pool_weight,
        d_pool_bias,
        d_class_weight,
        d_class_bias,
    )
    vector_grads = (
        d_query_bias,
        d_value_bias,
        d_output_bias,
        d_first_gain,
        d_first_shift,
        d_expand_bias,
        d_reduce_bias,
        d_second_gain,
        d_second_shift,
    )
    head_grads, vector_grads = lax.psum((head_grads, vector_grads), BOTH)
    index = lax.axis_index(BOTH)

    def own_part(vector):
        size = vector.shape[0] // devices
        return lax.dynamic_slice(vector, (index * size,), (size,))

    (g_qbias, g_vbias, g_obias, g_fgain, g_fshift, g_ebias, g_rbias, g_sgain, g_sshift) = (
        own_part(v) for v in vector_grads
    )
    return (
        layer_low[:share][None],
        cont_layer.reshape(1, conts, length, width),
        logits[None],
        d_rows[:share][None],
        d_rows[share:].reshape(1, conts, length, width),
        joint_grad,
        g_qbias,
        g_vbias,
        output_grad,
        g_obias,
        g_fgain,
        g_fshift,
        expand_grad,
        g_ebias,
        reduce_grad,
        g_rbias,
        g_sgain,
        g_sshift,
    ) + tuple(head_grads)


def solution(mesh):
    placed = (
        P("grp", "seq", None),
        P("grp", "seq", None, None),
        P("grp", "seq", None),
        P("grp", "seq", None, None),
        P("grp", "seq"),
        P(("grp", "seq"), None),
        P(("grp", "seq")),
        P(("grp", "seq")),
        P(("grp", "seq"), None),
        P(("grp", "seq")),
        P(("grp", "seq")),
        P(("grp", "seq")),
        P(("grp", "seq"), None),
        P(("grp", "seq")),
        P(("grp", "seq"), None),
        P(("grp", "seq")),
        P(("grp", "seq")),
        P(("grp", "seq")),
        P(),
        P(),
        P(),
        P(),
        P(),
        P(),
        P(),
    )
    return jax.shard_map(
        local,
        mesh=mesh,
        in_specs=placed,
        out_specs=(
            P("grp", "seq", None),
            P("grp", "seq", None, None),
            P("grp", "seq", None),
            P("grp", "seq", None),
            P("grp", "seq", None, None),
            P(("grp", "seq"), None),
            P(("grp", "seq")),
            P(("grp", "seq")),
            P(("grp", "seq"), None),
            P(("grp", "seq")),
            P(("grp", "seq")),
            P(("grp", "seq")),
            P(("grp", "seq"), None),
            P(("grp", "seq")),
            P(("grp", "seq"), None),
            P(("grp", "seq")),
            P(("grp", "seq")),
            P(("grp", "seq")),
            P(),
            P(),
            P(),
            P(),
            P(),
            P(),
            P(),
        ),
        check_vma=False,
    )
```

time: 1760 us -> 913 us (0.52)
  matrix products: 684 us -> 147 us
  other arithmetic: 267 us -> 48.3 us
  Pallas kernels: 0 us -> 181 us
  waiting for transfers between devices: 579 us -> 419 us
  local copies, waits for them, and re-layouts: 127 us -> 53.9 us
  blocking collectives: 81.3 us -> 41.4 us
    dot_general x59 -> x25, matrix products: 682 us -> 145 us  [the longest x19 143 us: dot(): lax.dot_general(left, right, (((left_dim,), (right_dim,)), ((), ())), pre...]
    reduce_scatter x5 -> x2, waiting for transfers between devices: 389 us -> 188 us  [the longest x1 133 us: local(): lax.psum_scatter(jnp.concatenate(blocks, 1), BOTH, scatter_dimension=0, t...]
    pallas_call x0 -> x4, Pallas kernels: none -> 181 us  [the longest x2 107 us: attention_backward(): pl.pallas_call(functools.partial(attention_backward_kernel, near), grid=(...]
    convert_element_type x34 -> x5, other arithmetic: 164 us -> 5.95 us  [the longest x1 1.64 us: local(): reduce_full = gather(reduce_weight.astype(BF16))]
    psum x1, waiting for transfers between devices: 0.01 us -> 129 us  [local(): head_grads, vector_grads = lax.psum((head_grads, vector_grads), BOTH)]
    unnamed x14 -> x9, waiting for transfers between devices: 125 us -> 0.83 us
    unnamed x2 -> x0, blocking collectives: 81.3 us -> none
    reduce_sum x11 -> x2, other arithmetic: 77.6 us -> 5.18 us  [the longest x1 3.1 us: local(): d_value_bias = jnp.sum(d_values.astype(F32), 0)]
  transfers between devices with their start and end apart: 13 -> 8, of which waited for: 5 -> 6; matrix products, arithmetic and copies ran while one was open for 28% -> 15% of each run, Pallas kernels for 0% -> 8%
where the time goes in v1:
time: 913 us; the launch traced here: 907 us
  waiting for transfers between devices  419 us (46%)
  Pallas kernels  181 us (20%)
  matrix products  147 us (16%)
  local copies, waits for them, and re-layouts  53.9 us (6%)
  other arithmetic  48.3 us (5%)
  blocking collectives  41.4 us (5%)
  between operations  15.3 us (2%)
    dot_general x19, matrix products, dot(): lax.dot_general(left, right, (((left_dim,), (right_dim,)), ((), ())), pre...  143 us
    reduce_scatter x1, waiting for transfers between devices, local(): lax.psum_scatter(jnp.concatenate(blocks, 1), BOTH, scatter_dimension=0, t...  133 us
    psum x1, waiting for transfers between devices, local(): head_grads, vector_grads = lax.psum((head_grads, vector_grads), BOTH)  129 us
    pallas_call x2, Pallas kernels, attention_backward(): pl.pallas_call(functools.partial(attention_backward_kernel, near), grid=(...  107 us
    all_gather x4, waiting for transfers between devices, gather(): return lax.all_gather(shard, axes, axis=0, tiled=True)  101 us
    pallas_call x2, Pallas kernels, attention_forward(): pl.pallas_call(functools.partial(attention_forward_kernel, near), grid=(p...  74 us
    reduce_scatter x1, waiting for transfers between devices, local(): lax.psum_scatter(jnp.concatenate([dk_far, dv_far], 1), 'seq', scatter_dim...  54.8 us
    psum x1, blocking collectives, local(): head_grads, vector_grads = lax.psum((head_grads, vector_grads), BOTH)  41.4 us
  transfers between devices with their start and end apart: 8, of which 6 were waited for; matrix products, arithmetic and copies ran while one was open for 15% of the time, Pallas kernels for 8%

profile of v1, /device:TPU:0, one launch (start us, length us, event | category | flops | bytes accessed | tf_op | source)
XLA Modules:
  0.0 907.3 jit_solution(478129025120784314)
XLA Ops:
  23.8 55.6 %all-gather.6.cloned.1.call-done = bf16[768,2432]{1,0:T(8,128)(2,1)} async-done(((bf16[24,2432]{1,0:T(8,128)(2,1)}), bf16[768,2432]{1,0:T(8,128)(2,1)}) %all-gather.6.cloned.1.call-update) | async-done | bytes 3735568 | tf_op jit(solution)/shard_map/all_gather | solution.py:357
  82.4 5.2 fusion.26.refs_0_
  87.5 20.8 %all-gather.12.cloned.1.call-done = bf16[1,2048,768]{2,1,0:T(8,128)(2,1)} async-done(((bf16[1,512,768]{2,1,0:T(8,128)(2,1)}), bf16[1,2048,768]{2,1,0:T(8,128)(2,1)}) %all-gather.12.cloned.1.call-update) | async-done | bytes 3145744 | tf_op jit(solution)/shard_map/all_gather | solution.py:357
  108.4 12.9 %add_convert_fusion.refs_1_.refs_2_.refs_3_.refs_4_ = bf16[3072,1536]{1,0:T(8,128)(2,1)} fusion(f32[1536]{0:T(1024)S(1)} %concatenate.59, bf16[768,2432]{1,0:T(8,128)(2,1)} %all-gather.6.cloned.1.call-done, bf16[1024,768]{1,0:T(8,128)(2,1)} %bitcast.192, bf16[2048,768]{1,0:T(8,128)(2,1)} %bitcast.188), kind=kOutput, calls=%fused_computation.9 | convolution fusion | flops 7266631680 | bytes 16521216 | tf_op jit(solution)/shard_map/dot_general | solution.py:26
  121.2 25.7 %attention_forward.2 = (bf16[512,768]{1,0:T(8,128)(2,1)}, f32[6,2,2,256]{3,2,1,0:T(2,128)}, bf16[6,2,2,2048,256]{4,3,2,1,0:T(8,128)(2,1)}) custom-call(bf16[1536,768]{1,0:T(8,128)(2,1)} %fusion.26.refs_0_, bf16[3072,1536]{1,0:T(8,128)(2,1)} %add_convert_fusion.refs_1_.refs_2_.refs_3_.refs_4_, bf16[3072,1536]{1,0:T(8,128)(2,1)} %add_convert_fusion.refs_1_.refs_2_.refs_3_.refs_4_), custom_call_target="tpu_custom_call" | custom-call | flops 3221225472 | bytes 25165824 | tf_op jit(solution)/shard_map/attention_forward/pallas_call | solution.py:151
  148.9 48.4 %attention_forward.3 = (bf16[1024,768]{1,0:T(8,128)(2,1)}, f32[6,4,2,256]{3,2,1,0:T(2,128)}, bf16[6,4,2,2304,256]{4,3,2,1,0:T(8,128)(2,1)}) custom-call(bf16[1536,768]{1,0:T(8,128)(2,1)} %fusion.26.refs_0_, bf16[3072,1536]{1,0:T(8,128)(2,1)} %add_convert_fusion.refs_1_.refs_2_.refs_3_.refs_4_, ...), custom_call_target="tpu_custom_call" | custom-call | flops 7247757312 | bytes 56623104 | tf_op jit(solution)/shard_map/attention_forward/pallas_call | solution.py:151
  207.2 13.8 %multiply_convert_fusion = (bf16[1536,3072]{1,0:T(8,128)(2,1)}, f32[1536,3072]{1,0:T(8,128)}) fusion(f32[3072]{0:T(1024)S(1)} %add.213, bf16[768,3840]{1,0:T(8,128)(2,1)S(1)} %bitcast.185, f32[1536,768]{1,0:T(8,128)S(1)} %get-tuple-element.175, f32[768]{0:T(1024)S(1)} %get-tuple-element.136, f32[768]{0:T(1024)S(1)} %get-tuple-element.137, ...), kind=kOutput, calls=%fused_computation.7 | convolution fusion | flops 7281967104 | bytes 37785600 | tf_op jit(solution)/shard_map/dot_general | solution.py:26
  221.0 24.6 %all-gather.10.cloned.1.call-done = bf16[3072,768]{1,0:T(8,128)(2,1)} async-done(((bf16[96,768]{1,0:T(8,128)(2,1)}), bf16[3072,768]{1,0:T(8,128)(2,1)}) %all-gather.10.cloned.1.call-update) | async-done | bytes 4718608 | tf_op jit(solution)/shard_map/all_gather | solution.py:357
  245.6 12.8 %fusion.81 = (f32[1536]{0:T(1024)S(1)}, f32[1536,768]{1,0:T(8,128)S(1)}) fusion(f32[768]{0:T(1024)S(1)} %get-tuple-element.135, bf16[1536,3072]{1,0:T(8,128)(2,1)} %get-tuple-element.176, bf16[3072,768]{1,0:T(8,128)(2,1)} %all-gather.10.cloned.1.call-done, f32[768]{0:T(1024)S(1)} %get-tuple-element.136, f32[768]{0:T(1024)S(1)} %get-tuple-element.137, ...), kind=kOutput, calls=%fused_computation.180 | convolution fusion | flops 7256013312 | bytes 23620608 | tf_op jit(solution)/shard_map/dot_general | solution.py:26
  279.5 20.8 %fusion.83 = (f32[3072]{0:T(1024)}, bf16[1536,3072]{1,0:T(8,128)(2,1)}) fusion(f32[1536,3072]{1,0:T(8,128)} %get-tuple-element.177, f32[3072]{0:T(1024)S(1)} %add.213, bf16[3072,768]{1,0:T(8,128)(2,1)S(1)} %bitcast.187, f32[1536,768]{1,0:T(8,128)S(1)} %get-tuple-element.162, f32[1536]{0:T(1024)S(1)} %negate_multiply_fusion.1), kind=kOutput, calls=%fused_computation.182 | convolution fusion | flops 7316173824 | bytes 37779456 | tf_op jit(solution)/shard_map/dot_general | solution.py:26
  300.4 12.9 %multiply_reduce_fusion.1 = (f32[768]{0:T(1024)S(1)}, f32[1536]{0:T(1024)S(1)}, f32[768]{0:T(1024)S(1)}, f32[1536,768]{1,0:T(8,128)S(1)}) fusion(f32[1536,768]{1,0:T(8,128)S(1)} %bitcast.156, f32[1536]{0:T(1024)S(1)} %fusion.59, f32[1536]{0:T(1024)S(1)} %broadcast_multiply_fusion.1, f32[768]{0:T(1024)S(1)} %get-tuple-element.137, ...), kind=kOutput, calls=%fused_computation.29 | convolution fusion | flops 7259550720 | bytes 28345344 | tf_op jit(solution)/shard_map/dot_general | solution.py:26
  315.5 5.7 convolution_convert_fusion.2.refs_4_.refs_6_
  321.2 33.7 %attention_backward.2 = (bf16[512,768]{1,0:T(8,128)(2,1)}, f32[768,2048]{1,0:T(8,128)}, f32[768,2048]{1,0:T(8,128)}) custom-call(bf16[1536,768]{1,0:T(8,128)(2,1)} %fusion.26.refs_0_, bf16[3072,1536]{1,0:T(8,128)(2,1)} %add_convert_fusion.refs_1_.refs_2_.refs_3_.refs_4_, bf16[3072,1536]{1,0:T(8,128)(2,1)} %add_convert_fusion.refs_1_.refs_2_.refs_3_.refs_4_, ...), custom_call_target="tpu_custom_call" | custom-call | flops 6442450944 | bytes 25165824 | tf_op jit(solution)/shard_map/attention_backward/pallas_call | solution.py:309
  356.1 73.3 %attention_backward.3 = (bf16[1024,768]{1,0:T(8,128)(2,1)}, bf16[1024,768]{1,0:T(8,128)(2,1)}, bf16[1024,768]{1,0:T(8,128)(2,1)}, bf16[2048,768]{1,0:T(8,128)(2,1)}, bf16[2048,768]{1,0:T(8,128)(2,1)}) custom-call(bf16[1536,768]{1,0:T(8,128)(2,1)} %fusion.26.refs_0_, bf16[3072,1536]{1,0:T(8,128)(2,1)} %add_convert_fusion.refs_1_.refs_2_.refs_3_.refs_4_, ...), custom_call_target="tpu_custom_call" | custom-call | flops 14495514624 | bytes 56623104 | tf_op jit(solution)/shard_map/attention_backward/pallas_call | solution.py:309
  447.9 6.0 copy.93
  459.2 5.4 convolution_convert_fusion.4
  465.8 13.0 %convolution_convert_fusion.1 = bf16[768,3072]{1,0:T(8,128)(2,1)S(1)} fusion(bf16[1536,3072]{1,0:T(8,128)(2,1)} %get-tuple-element.184, f32[1536,768]{1,0:T(8,128)} %copy-done.4, f32[768]{0:T(1024)S(1)} %copy-done.39, f32[768]{0:T(1024)S(1)} %get-tuple-element.137, f32[1536]{0:T(1024)S(1)} %fusion.59, f32[1536]{0:T(1024)S(1)} %broadcast_multiply_fusion.1), kind=kOutput, calls=%fused_computation.15 | convolution fusion | flops 7256014848 | bytes 18892800 | tf_op jit(solution)/shard_map/dot_general | solution.py:26
  483.8 8.8 convolution_convert_fusion
  508.9 41.4 %all-reduce.2 = (f32[768]{0:T(1024)S(1)}, f32[768]{0:T(1024)S(1)}, f32[768]{0:T(1024)S(1)}, f32[768]{0:T(1024)S(1)}, f32[768]{0:T(1024)S(1)}, /*index=5*/f32[307...) all-reduce(f32[768]{0:T(1024)S(1)} %convert_reduce_fusion.1, ...), channel_id=1, replica_groups=mesh['grp'=8,'seq'=4] {'grp','seq'}, use_global_device_ids=true, to_apply=%region_16.17 | all-reduce | flops 11406 | bytes 91248 | tf_op jit(solution)/shard_map/psum | solution.py:569
  560.9 54.8 %reduce-scatter.6.cloned.1.call-done = bf16[512,1536]{1,0:T(8,128)(2,1)} async-done(((bf16[2048,1536]{1,0:T(8,128)(2,1)}), bf16[512,1536]{1,0:T(8,128)(2,1)}) %reduce-scatter.6.cloned.1.call-update) | async-done | bytes 1572880 | tf_op jit(solution)/shard_map/reduce_scatter | solution.py:539
  615.8 7.3 fusion.5
  623.1 5.0 add_add_fusion.2
  631.3 133.4 %reduce-scatter.8.cloned.1.call-done = bf16[1,216,768]{2,1,0:T(8,128)(2,1)} async-done(((bf16[32,216,768]{2,1,0:T(8,128)(2,1)}), bf16[1,216,768]{2,1,0:T(8,128)(2,1)}) %reduce-scatter.8.cloned.1.call-update) | async-done | bytes 331792 | tf_op jit(solution)/shard_map/reduce_scatter | solution.py:506
  767.8 129.1 %all-reduce.6.cloned.1.call-done = (f32[768,128]{1,0:T(8,128)}, f32[128,128]{1,0:T(8,128)}) async-done(((f32[768,128]{1,0:T(8,128)}, f32[128,128]{1,0:T(8,128)}), (f32[768,128]{1,0:T(8,128)}, f32[128,128]{1,0:T(8,128)})) %all-reduce.6.cloned.1.call-update) | async-done | bytes 458768 | tf_op jit(solution)/shard_map/psum | solution.py:569
  (270 shorter events, 121.5 us)
Async XLA Ops:
  7.2 257.4 %copy-start = (f32[128,128]{1,0:T(8,128)S(1)}, f32[128,128]{1,0:T(8,128)}, u32[]{:S(2)}) copy-start(f32[128,128]{1,0:T(8,128)} %param.46) | copy-start | bytes 196612
  7.2 72.2 %all-gather.6.cloned.1.call-start = ((), (), s32[]{:S(2)}) async-start(), calls=%async_computation.3 | async-start | bytes 3852288 | tf_op jit(solution)/shard_map/all_gather | solution.py:357
  15.8 92.5 %all-gather.12.cloned.1.call-start = ((), (), s32[]{:S(2)}) async-start(), calls=%async_computation.8 | async-start | bytes 3932160 | tf_op jit(solution)/shard_map/all_gather | solution.py:357
  16.6 65.8 %copy-start.20 = (bf16[1,512,768]{2,1,0:T(8,128)(2,1)S(1)}, bf16[1,512,768]{2,1,0:T(8,128)(2,1)}, u32[]{:S(2)}) copy-start(bf16[1,512,768]{2,1,0:T(8,128)(2,1)} %param.25) | copy-start | bytes 2359300
  16.6 183.5 %all-gather.8.cloned.1.call-start = ((), (), s32[]{:S(2)}) async-start(), calls=%async_computation.4 | async-start | bytes 6082560 | tf_op jit(solution)/shard_map/all_gather | solution.py:357
  19.3 226.3 %all-gather.10.cloned.1.call-start = ((), (), s32[]{:S(2)}) async-start(), calls=%async_computation.5 | async-start | bytes 4866048 | tf_op jit(solution)/shard_map/all_gather | solution.py:357
  21.0 537.7 %reduce-scatter.10.cloned.1.call-start = ((), (), s32[]{:S(2)}) async-start(), calls=%async_computation.9 | async-start | bytes 3649536
  82.3 163.3 %copy-start.38 = (f32[768]{0:T(1024)}, f32[768]{0:T(1024)S(1)}, u32[]{:S(2)}) copy-start(f32[768]{0:T(1024)S(1)} %get-tuple-element.136) | copy-start | bytes 9220
  263.0 13.6 %copy-start.7 = (f32[4,256,2,64]{1,0,3,2:T(4,128)}, f32[4,256,2,64]{1,0,3,2:T(4,128)S(1)}, u32[]{:S(2)}) copy-start(f32[4,256,2,64]{1,0,3,2:T(4,128)S(1)} %reshape.204) | copy-start | bytes 1572868
  264.8 11.9 %copy-start.31 = (f32[4,128]{1,0:T(4,128)}, f32[4,128]{1,0:T(4,128)S(1)}, u32[]{:S(2)}) copy-start(f32[4,128]{1,0:T(4,128)S(1)} %fusion.32) | copy-start | bytes 6148
  266.5 10.1 %copy-start.29 = (f32[4,128]{1,0:T(4,128)}, f32[4,128]{1,0:T(4,128)S(1)}, u32[]{:S(2)}) copy-start(f32[4,128]{1,0:T(4,128)S(1)} %get-tuple-element.188) | copy-start | bytes 6148
  276.7 23.7 %slice-start = ((s8[4718592]{0:T(1024)(128)(4,1)}), s8[4194304]{0:T(1024)(128)(4,1)S(1)}, s32[]{:S(2)}) async-start(s8[4718592]{0:T(1024)(128)(4,1)} %bitcast.155), calls=%async_computation.11 | async-start | bytes 8388608
  279.5 20.9 %copy-start.6 = (f32[1536,768]{1,0:T(8,128)}, f32[1536,768]{1,0:T(8,128)S(1)}, u32[]{:S(2)}) copy-start(f32[1536,768]{1,0:T(8,128)S(1)} %get-tuple-element.162) | copy-start | bytes 14155780
  279.5 20.8 %slice-start.1 = ((s8[4718592]{0:T(1024)(128)(4,1)}), s8[524288]{0:T(1024)(128)(4,1)S(1)}, s32[]{:S(2)}) async-start(s8[4718592]{0:T(1024)(128)(4,1)} %bitcast.155), calls=%async_computation.12 | async-start | bytes 1048576
  453.9 161.9 %reduce-scatter.6.cloned.1.call-start = ((), (), s32[]{:S(2)}) async-start(), calls=%async_computation.6 | async-start | bytes 7864320 | tf_op jit(solution)/shard_map/reduce_scatter | solution.py:539
  459.0 305.7 %reduce-scatter.8.cloned.1.call-start = ((), (), s32[]{:S(2)}) async-start(), calls=%async_computation.7 | async-start | bytes 10948608 | tf_op jit(solution)/shard_map/reduce_scatter | solution.py:506
  465.8 17.9 %slice-start.8 = ((s8[9437184]{0:T(1024)(128)(4,1)}), s8[4194304]{0:T(1024)(128)(4,1)S(1)}, s32[]{:S(2)}) async-start(s8[9437184]{0:T(1024)(128)(4,1)} %bitcast.197), calls=%async_computation.19 | async-start | bytes 8388608
  465.8 17.9 %slice-start.9 = ((s8[9437184]{0:T(1024)(128)(4,1)}), s8[4194304]{0:T(1024)(128)(4,1)S(1)}, s32[]{:S(2)}) async-start(s8[9437184]{0:T(1024)(128)(4,1)} %bitcast.197), calls=%async_computation.20 | async-start | bytes 8388608
  495.2 401.8 %all-reduce.6.cloned.1.call-start = ((), (), s32[]{:S(2)}) async-start(), calls=%async_computation.10 | async-start | bytes 917504 | tf_op jit(solution)/shard_map/psum | solution.py:569
  504.5 51.0 %copy-start.27 = (f32[4,128]{1,0:T(4,128)S(1)}, f32[4,128]{1,0:T(4,128)}, u32[]{:S(2)}) copy-start(f32[4,128]{1,0:T(4,128)} %copy-done.26) | copy-start | bytes 6148
  504.5 51.0 %copy-start.30 = (f32[4,128]{1,0:T(4,128)S(1)}, f32[4,128]{1,0:T(4,128)}, u32[]{:S(2)}) copy-start(f32[4,128]{1,0:T(4,128)} %copy-done.29) | copy-start | bytes 6148
  504.5 52.8 %copy-start.19 = (bf16[16,8,4,256]{3,1,2,0:T(8,128)(2,1)S(1)}, bf16[16,8,4,256]{3,1,2,0:T(8,128)(2,1)}, u32[]{:S(2)}) copy-start(bf16[16,8,4,256]{3,1,2,0:T(8,128)(2,1)} %copy-done.18) | copy-start | bytes 786436
  560.9 62.1 %copy-start.14 = (bf16[1536,768]{1,0:T(8,128)(2,1)S(1)}, bf16[1536,768]{1,0:T(8,128)(2,1)}, u32[]{:S(2)}) copy-start(bf16[1536,768]{1,0:T(8,128)(2,1)} %copy-done.13) | copy-start | bytes 7077892
  628.1 272.1 %copy-start.1 = (f32[128,128]{1,0:T(8,128)S(1)}, f32[128,128]{1,0:T(8,128)}, u32[]{:S(2)}) copy-start(f32[128,128]{1,0:T(8,128)} %param.46) | copy-start | bytes 196612
  (45 other events, 178.3 us)
Sparse Core Ops, SparseCore 0:
  16.0 63.3 all-gather.5
  80.9 27.3 all-gather.11
  111.8 67.7 all-gather.7
  182.9 62.6 all-gather.9
  454.0 102.0 reduce-scatter.9
  558.5 57.2 reduce-scatter.5
  622.9 141.7 reduce-scatter.7
  771.5 125.4 all-reduce.5

commit v2 on v1

--- a/solution.py
+++ b/solution.py
@@ -34,7 +34,7 @@
 
 def attention_forward_kernel(near, *refs):
     if near:
-        q_ref, k_ref, v_ref, kn_ref, vn_ref, out_ref, inv_ref, exp_ref, vt_ref, s_ref = refs
+        q_ref, k_ref, v_ref, kn_ref, vn_ref, _, out_ref, inv_ref, exp_ref, vt_ref, s_ref = refs
     else:
         q_ref, k_ref, v_ref, out_ref, inv_ref, exp_ref, vt_ref, s_ref = refs
     far = k_ref.shape[0]
@@ -127,42 +127,46 @@
         finish(outs)
 
 
-def attention_forward(queries, q_at, far_kv, far, near_at, count, tile):
-    near = near_at is not None
-    width = queries.shape[1]
+def attention_forward(queries, keys_values, far, count, at, tile, into):
+    near = into is not None
+    total, width = queries.shape
     pairs = width // PAIR
     tiles = count // tile
     held = far + (tile if near else 0)
-    at = q_at // tile
+    block = at // tile
     specs = [
-        pl.BlockSpec((tile, PAIR), lambda h, t: (at + t, h)),
-        pl.BlockSpec((far, PAIR), lambda h, t: (0, h)),
-        pl.BlockSpec((far, PAIR), lambda h, t: (0, pairs + h)),
+        pl.BlockSpec((tile, PAIR), lambda h, t: (block + t, h)),
+        pl.BlockSpec((far, PAIR), lambda h, t: (0, 2 * h)),
+        pl.BlockSpec((far, PAIR), lambda h, t: (0, 2 * h + 1)),
     ]
-    operands = [queries, far_kv, far_kv]
+    operands = [queries, keys_values, keys_values]
+    aliases = {}
     if near:
-        first = near_at // tile
+        first = far // tile
         specs += [
-            pl.BlockSpec((tile, PAIR), lambda h, t: (first + t, h)),
-            pl.BlockSpec((tile, PAIR), lambda h, t: (first + t, pairs + h)),
+            pl.BlockSpec((tile, PAIR), lambda h, t: (first + t, 2 * h)),
+            pl.BlockSpec((tile, PAIR), lambda h, t: (first + t, 2 * h + 1)),
+            pl.BlockSpec(memory_space=pl.ANY),
         ]
-        operands += [far_kv, far_kv]
+        operands += [keys_values, keys_values, into]
+        aliases = {5: 0}
     cells = count * held * width // HEAD_DIM
     return pl.pallas_call(
         functools.partial(attention_forward_kernel, near),
         grid=(pairs, tiles),
         in_specs=specs,
         out_specs=[
-            pl.BlockSpec((tile, PAIR), lambda h, t: (t, h)),
+            pl.BlockSpec((tile, PAIR), lambda h, t: (block + t, h)),
             pl.BlockSpec((1, 1, 2, tile), lambda h, t: (h, t, 0, 0)),
             pl.BlockSpec((1, 1, 2, held, tile), lambda h, t: (h, t, 0, 0, 0)),
         ],
         out_shape=[
-            jax.ShapeDtypeStruct((count, width), BF16),
+            jax.ShapeDtypeStruct((total, width), BF16),
             jax.ShapeDtypeStruct((pairs, tiles, 2, tile), F32),
             jax.ShapeDtypeStruct((pairs, tiles, 2, held, tile), BF16),
         ],
         scratch_shapes=[pltpu.VMEM((PAIR, far), BF16), pltpu.VMEM((far, tile), F32)],
+        input_output_aliases=aliases,
         compiler_params=pltpu.CompilerParams(vmem_limit_bytes=VMEM_LIMIT),
         cost_estimate=pl.CostEstimate(
             flops=4 * cells * HEAD_DIM, bytes_accessed=2 * cells, transcendentals=cells
@@ -172,44 +176,12 @@
 
 
 def attention_backward_kernel(near, *refs):
+    q_ref, k_ref, v_ref, out_ref, dout_ref, inv_ref, exp_ref = refs[:7]
     if near:
-        (
-            q_ref,
-            k_ref,
-            v_ref,
-            kn_ref,
-            vn_ref,
-            out_ref,
-            dout_ref,
-            inv_ref,
-            exp_ref,
-            dk_in_ref,
-            dv_in_ref,
-            dq_ref,
-            dkn_ref,
-            dvn_ref,
-            dk_ref,
-            dv_ref,
-            kt_ref,
-            dkt_ref,
-            dvt_ref,
-        ) = refs
+        kn_ref, vn_ref, dk_in_ref, dv_in_ref, _, dq_ref, dkvn_ref, dkv_ref = refs[7:15]
     else:
-        (
-            q_ref,
-            k_ref,
-            v_ref,
-            out_ref,
-            dout_ref,
-            inv_ref,
-            exp_ref,
-            dq_ref,
-            dk_ref,
-            dv_ref,
-            kt_ref,
-            dkt_ref,
-            dvt_ref,
-        ) = refs
+        dq_ref, dk_ref, dv_ref = refs[7:10]
+    kt_ref, dkt_ref, dvt_ref = refs[-3:]
     far = k_ref.shape[0]
     tile = q_ref.shape[0]
     at = pl.program_id(1)
@@ -251,76 +223,79 @@
         dqs.append(dq * HEAD_DIM ** (-0.5))
     dq_ref[...] = jnp.concatenate(dqs, 0).T.astype(dq_ref.dtype)
     if near:
-        dkn_ref[...] = jnp.concatenate(dkn, 0).T.astype(dkn_ref.dtype)
-        dvn_ref[...] = jnp.concatenate(dvn, 0).T.astype(dvn_ref.dtype)
+        dkvn_ref[:, :PAIR] = jnp.concatenate(dkn, 0).T.astype(dkvn_ref.dtype)
+        dkvn_ref[:, PAIR:] = jnp.concatenate(dvn, 0).T.astype(dkvn_ref.dtype)
 
     @pl.when(at == pl.num_programs(1) - 1)
     def _():
         if near:
-            dk_ref[...] = dkt_ref[...].T.astype(dk_ref.dtype)
-            dv_ref[...] = dvt_ref[...].T.astype(dv_ref.dtype)
+            dkv_ref[:, :PAIR] = dkt_ref[...].T.astype(dkv_ref.dtype)
+            dkv_ref[:, PAIR:] = dvt_ref[...].T.astype(dkv_ref.dtype)
         else:
             dk_ref[...] = dkt_ref[...]
             dv_ref[...] = dvt_ref[...]
 
 
 def attention_backward(
-    queries, q_at, far_kv, far, near_at, context, d_context, inverse, held_exp, sums, tile, h0, nh
+    queries, keys_values, far, context, d_context, inverse, held_exp, at, tile, h0, nh, into
 ):
-    near = sums is not None
-    width = queries.shape[1]
-    pairs = width // PAIR
-    count = context.shape[0]
-    tiles = count // tile
-    held = held_exp.shape[3]
-    at = q_at // tile
+    near = into is not None
+    total = queries.shape[0]
+    tiles, held = held_exp.shape[1], held_exp.shape[3]
+    count = tiles * tile
+    block = at // tile
+    row = pl.BlockSpec((tile, PAIR), lambda h, t: (block + t, h0 + h))
     specs = [
-        pl.BlockSpec((tile, PAIR), lambda h, t: (at + t, h0 + h)),
-        pl.BlockSpec((far, PAIR), lambda h, t: (0, h0 + h)),
-        pl.BlockSpec((far, PAIR), lambda h, t: (0, pairs + h0 + h)),
-    ]
-    operands = [queries, far_kv, far_kv]
-    if near:
-        first = near_at // tile
-        specs += [
-            pl.BlockSpec((tile, PAIR), lambda h, t: (first + t, h0 + h)),
-            pl.BlockSpec((tile, PAIR), lambda h, t: (first + t, pairs + h0 + h)),
-        ]
-        operands += [far_kv, far_kv]
-    specs += [
-        pl.BlockSpec((tile, PAIR), lambda h, t: (t, h0 + h)),
-        pl.BlockSpec((tile, PAIR), lambda h, t: (at + t, h0 + h)),
+        row,
+        pl.BlockSpec((far, PAIR), lambda h, t: (0, 2 * (h0 + h))),
+        pl.BlockSpec((far, PAIR), lambda h, t: (0, 2 * (h0 + h) + 1)),
+        row,
+        row,
         pl.BlockSpec((1, 1, 2, tile), lambda h, t: (h0 + h, t, 0, 0)),
         pl.BlockSpec((1, 1, 2, held, tile), lambda h, t: (h0 + h, t, 0, 0, 0)),
     ]
-    operands += [context, d_context, inverse, held_exp]
+    operands = [queries, keys_values, keys_values, context, d_context, inverse, held_exp]
     turned = pl.BlockSpec((PAIR, far), lambda h, t: (h, 0))
-    row = pl.BlockSpec((tile, PAIR), lambda h, t: (t, h))
-    row_shape = jax.ShapeDtypeStruct((count, nh * PAIR), BF16)
+    out_specs = [pl.BlockSpec((tile, PAIR), lambda h, t: (block + t, h))]
+    out_shape = [jax.ShapeDtypeStruct((total, nh * PAIR), BF16)]
+    aliases = {}
     if near:
-        specs += [turned, turned]
-        operands += list(sums)
-        column = pl.BlockSpec((far, PAIR), lambda h, t: (0, h))
-        column_shape = jax.ShapeDtypeStruct((far, nh * PAIR), BF16)
+        first = far // tile
+        specs += [
+            pl.BlockSpec((tile, PAIR), lambda h, t: (first + t, 2 * (h0 + h))),
+            pl.BlockSpec((tile, PAIR), lambda h, t: (first + t, 2 * (h0 + h) + 1)),
+            turned,
+            turned,
+            pl.BlockSpec(memory_space=pl.ANY),
+        ]
+        operands += [keys_values, keys_values, into[1], into[2], into[0]]
+        aliases = {11: 0}
+        out_specs += [
+            pl.BlockSpec((tile, 2 * PAIR), lambda h, t: (t, h)),
+            pl.BlockSpec((far, 2 * PAIR), lambda h, t: (0, h)),
+        ]
+        out_shape += [
+            jax.ShapeDtypeStruct((count, 2 * nh * PAIR), BF16),
+            jax.ShapeDtypeStruct((far, 2 * nh * PAIR), BF16),
+        ]
     else:
-        column = turned
-        column_shape = jax.ShapeDtypeStruct((nh * PAIR, far), F32)
+        out_specs += [turned, turned]
+        out_shape += [jax.ShapeDtypeStruct((nh * PAIR, far), F32)] * 2
     cells = count * held * nh * 2
     return pl.pallas_call(
         functools.partial(attention_backward_kernel, near),
         grid=(nh, tiles),
         in_specs=specs,
-        out_specs=[row] + ([row, row] if near else []) + [column, column],
-        out_shape=[row_shape] * (3 if near else 1) + [column_shape] * 2,
+        out_specs=out_specs,
+        out_shape=out_shape,
         scratch_shapes=[
             pltpu.VMEM((PAIR, far), BF16),
             pltpu.VMEM((PAIR, far), F32),
             pltpu.VMEM((PAIR, far), F32),
         ],
+        input_output_aliases=aliases,
         compiler_params=pltpu.CompilerParams(vmem_limit_bytes=VMEM_LIMIT),
-        cost_estimate=pl.CostEstimate(
-            flops=8 * cells * HEAD_DIM, bytes_accessed=2 * cells, transcendentals=0
-        ),
+        cost_estimate=pl.CostEstimate(flops=cells, bytes_accessed=cells, transcendentals=0),
         name="attention_backward",
     )(*operands)
 
@@ -353,8 +328,124 @@
     return (loss, logits)
 
 
-def gather(shard, axes=BOTH):
-    return lax.all_gather(shard, axes, axis=0, tiled=True)
+def bits_of(axis):
+    size = lax.axis_size(axis)
+    return [(axis, 1 << b) for b in reversed(range(size.bit_length() - 1))]
+
+
+def across(array, axis, bit):
+    return lax.ppermute(array, axis, [(i, i ^ bit) for i in range(lax.axis_size(axis))])
+
+
+def bit_set(axis, bit):
+    return (lax.axis_index(axis) // bit) % 2
+
+
+def gather_bits(shard, order, dims):
+    held = shard.reshape((1,) * len(dims) + shard.shape)
+    for axis, bit in order:
+        dim = dims.index((axis, bit))
+        other = across(held, axis, bit)
+        held = jnp.where(
+            bit_set(axis, bit) == 0,
+            jnp.concatenate([held, other], dim),
+            jnp.concatenate([other, held], dim),
+        )
+    return held
+
+
+def gather_relative(shard, axis):
+    bits = bits_of(axis)
+    held = shard.reshape((1,) * len(bits) + shard.shape)
+    for dim, (_, bit) in enumerate(bits):
+        held = jnp.concatenate([held, across(held, axis, bit)], dim)
+    return held.reshape((-1,) + shard.shape[1:])
+
+
+class Scatter:
+    def __init__(self, blocks, order, dims, relative=False):
+        self.shape = blocks.shape[1:]
+        self.held = blocks.reshape((2,) * len(dims) + self.shape)
+        self.order, self.dims, self.relative = list(order), dims, relative
+        self.split()
+
+    def split(self):
+        axis, bit = self.order[0]
+        dim = self.dims.index((axis, bit))
+        mine = 0 if self.relative else bit_set(axis, bit)
+        self.give = lax.dynamic_slice_in_dim(self.held, 1 - mine, 1, dim)
+        self.keep = lax.dynamic_slice_in_dim(self.held, mine, 1, dim)
+
+    def send(self):
+        axis, bit = self.order.pop(0)
+        self.other = across(self.give, axis, bit)
+
+    def take(self):
+        total = self.keep.astype(F32) + self.other.astype(F32)
+        if not self.order:
+            self.held = total.reshape(self.shape)
+            return False
+        self.held = total.astype(BF16)
+        self.split()
+        return True
+
+    def waiting(self):
+        return [self.give]
+
+    def tied(self, values):
+        (self.give,) = values
+
+
+class Sum:
+    def __init__(self, value, order):
+        self.held, self.order = value, list(order)
+
+    def send(self):
+        axis, bit = self.order.pop(0)
+        self.other = across(self.held, axis, bit)
+
+    def take(self):
+        self.held = self.held + self.other
+        return bool(self.order)
+
+    def waiting(self):
+        return [self.held]
+
+    def tied(self, values):
+        (self.held,) = values
+
+
+class Exchanges:
+    def __init__(self):
+        self.live = []
+
+    def add(self, chain):
+        self.live.append([chain, True])
+        return chain
+
+    def step(self, value):
+        for entry in self.live:
+            if not entry[1]:
+                entry[0].more = entry[0].take()
+            else:
+                entry[0].more = True
+            entry[1] = False
+        going = [entry[0] for entry in self.live if entry[0].more]
+        self.live = [[chain, False] for chain in going]
+        if value is not None and going:
+            flat = [v for chain in going for v in chain.waiting()]
+            value, *flat = lax.optimization_barrier((value, *flat))
+            for chain in going:
+                size = len(chain.waiting())
+                chain.tied(flat[:size])
+                flat = flat[size:]
+        for chain in going:
+            chain.send()
+        return value
+
+    def finish(self):
+        while self.live:
+            self.step(None)
 
 
 def local(
@@ -391,8 +482,19 @@
     part = joint_weight.shape[0]
     devices = width // part
     hidden_width = expand_weight.shape[1]
+    fold = hidden_width // width
     tile = min(share, length)
-
+    grp_bits, seq_bits = bits_of("grp"), bits_of("seq")
+    dims = grp_bits + seq_bits
+    scatter_order = [seq_bits[-1]] + seq_bits[:-1][::-1] + grp_bits[::-1]
+    gather_orders = (
+        grp_bits + seq_bits,
+        grp_bits[:-1] + seq_bits[:-1] + grp_bits[-1:] + seq_bits[-1:],
+    )
+
+    pairs = width // PAIR
+    groups = [3, 2, 1] if pairs == 6 else [pairs]
+    joint_low = joint_weight.astype(BF16)
     vectors = [
         query_bias,
         value_bias,
@@ -403,19 +505,33 @@
         second_gain,
         second_shift,
     ]
-    beside = jnp.concatenate(
-        [v[:, None] for v in vectors] + [expand_bias.reshape(part, hidden_width // width)], 1
-    )
-    beside = jnp.pad(beside, ((0, 0), (0, 128 - beside.shape[1])))
-    joint_all = gather(jnp.concatenate([joint_weight, beside], 1).astype(BF16))
-    prompt_all = gather(prompt_rows, "seq")
-    far = prompt_all.shape[0]
-    out_expand = gather(jnp.concatenate([output_weight, expand_weight], 1).astype(BF16))
-    reduce_full = gather(reduce_weight.astype(BF16))
+    beside = jnp.concatenate([v[None] for v in vectors], 0).astype(BF16).T
+    beside = jnp.concatenate([beside, expand_bias.astype(BF16).reshape(part, fold)], 1)
+    lanes = student_weight.shape[1]
+    own_joint = [joint_low[:, :width]]
+    for h in range(pairs):
+        own_joint += [joint_low[:, (s * pairs + h) * PAIR :][:, :PAIR] for s in (1, 2)]
+    own_joint.append(jnp.pad(beside, ((0, 0), (0, lanes - beside.shape[1]))))
+    own_joint = jnp.concatenate(own_joint, 1)
+    half = (3 * width // 2 + lanes) // PAIR * PAIR
+    joint_all = jnp.concatenate(
+        [
+            gather_bits(piece, order, dims).reshape(width, -1)
+            for piece, order in zip((own_joint[:, :half], own_joint[:, half:]), gather_orders)
+        ],
+        1,
+    )
     joint_full = joint_all[:, : 3 * width]
     flat = joint_all[:, 3 * width :].astype(F32)
-    qbias, vbias, obias, fgain, fshift, rbias, sgain, sshift = (flat[:, i] for i in range(8))
-    ebias = flat[:, 8 : 8 + hidden_width // width].reshape(hidden_width)
+    by_vector = flat[:, : len(vectors)].T
+    qbias, vbias, obias, fgain, fshift, rbias, sgain, sshift = (by_vector[i] for i in range(8))
+    ebias = flat[:, 8 : 8 + fold].reshape(hidden_width)
+    prompt_all = gather_relative(prompt_rows, "seq")
+    far = prompt_all.shape[0]
+    out_expand = lax.all_gather(
+        jnp.concatenate([output_weight, expand_weight], 1).astype(BF16), BOTH, axis=0, tiled=True
+    )
+    reduce_full = lax.all_gather(reduce_weight.astype(BF16), BOTH, axis=0, tiled=True)
     output_full = out_expand[:, :width]
     expand_full = out_expand[:, width:]
 
@@ -423,16 +539,15 @@
     rows = jnp.concatenate([prompt_rows, cont_rows], 0)
     key_rows = jnp.concatenate([prompt_all, cont_rows], 0)
     queries = (dot(rows, joint_full[:, :width], 1, 0) + qbias).astype(BF16) * HEAD_DIM ** (-0.5)
-    kv_bias = jnp.concatenate([jnp.zeros_like(vbias), vbias])
+    kv_bias = jnp.pad(vbias.reshape(pairs, 1, PAIR), ((0, 0), (1, 0), (0, 0))).reshape(-1)
     keys_values = (dot(key_rows, joint_full[:, width:], 1, 0) + kv_bias).astype(BF16)
 
-    prompt_context, prompt_inv, prompt_exp = attention_forward(
-        queries, 0, keys_values, far, None, share, tile
-    )
-    cont_context, cont_inv, cont_exp = attention_forward(
-        queries, share, keys_values, far, far, cont_count, length
-    )
-    context = jnp.concatenate([prompt_context, cont_context], 0)
+    context, prompt_inv, prompt_exp = attention_forward(
+        queries, keys_values, far, share, 0, tile, None
+    )
+    context, cont_inv, cont_exp = attention_forward(
+        queries, keys_values, far, cont_count, share, length, context
+    )
 
     branch = dot(context, output_full, 1, 0) + obias
     first, first_back = jax.vjp(layer_norm, rows.astype(F32) + branch, fgain, fshift)
@@ -497,91 +612,132 @@
     d_output_weight = dot(context, d_inner_low, 0, 0).astype(BF16)
     d_context = dot(d_inner_low, output_full, 1, 1).astype(BF16)
 
+    classes = class_weight.shape[1]
+    small = [
+        d_student_weight,
+        d_pool_weight,
+        jnp.pad(d_class_weight, ((0, 0), (0, lanes - classes))),
+        d_student_bias[None],
+        d_query[None],
+        d_pool_bias[None],
+        jnp.pad(d_class_bias, (0, lanes - classes))[None],
+    ] + [
+        v.reshape(-1, lanes)
+        for v in (
+            d_output_bias,
+            d_first_gain,
+            d_first_shift,
+            d_reduce_bias,
+            d_second_gain,
+            d_second_shift,
+            d_expand_bias,
+        )
+    ]
+    exchanges = Exchanges()
+    small = exchanges.add(Sum(jnp.concatenate(small, 0), dims))
     blocks = [d_output_weight.reshape(devices, part, width)]
     blocks += [
         d_expand_weight[:, i * width : (i + 1) * width].reshape(devices, part, width)
-        for i in range(hidden_width // width)
+        for i in range(fold)
     ]
     blocks += [d_reduce_weight.reshape(devices, -1, width)]
-    early = lax.psum_scatter(
-        jnp.concatenate(blocks, 1), BOTH, scatter_dimension=0, tiled=True
-    )[0].astype(F32)
-    count = hidden_width // width
+    blocks, d_context, d_inner = lax.optimization_barrier(
+        (jnp.concatenate(blocks, 1), d_context, d_inner)
+    )
+    early = lax.psum_scatter(blocks, BOTH, scatter_dimension=0, tiled=True)
+    early = early[0].astype(F32)
     output_grad = early[:part]
     expand_grad = jnp.concatenate(
-        [early[part * (1 + i) : part * (2 + i)] for i in range(count)], 1
-    )
-    reduce_grad = early[part * (1 + count) :]
-
-    pairs = width // PAIR
-    dq_prompt, dk_sum, dv_sum = attention_backward(
-        queries, 0, keys_values, far, None, prompt_context, d_context, prompt_inv, prompt_exp,
-        None, tile, 0, pairs,
-    )
-    dq_cont, dk_cont, dv_cont, dk_far, dv_far = attention_backward(
-        queries, share, keys_values, far, far, cont_context, d_context, cont_inv, cont_exp,
-        (dk_sum, dv_sum), length, 0, pairs,
-    )
-    d_queries = jnp.concatenate([dq_prompt, dq_cont], 0)
-    d_keys = jnp.concatenate([dk_far, dk_cont], 0)
-    d_values = jnp.concatenate([dv_far, dv_cont], 0)
-    d_query_bias = jnp.sum(d_queries.astype(F32), 0)
-    d_value_bias = jnp.sum(d_values.astype(F32), 0)
-    d_joint = jnp.concatenate(
-        [
-            dot(rows, d_queries, 0, 0),
-            dot(key_rows, d_keys, 0, 0),
-            dot(key_rows, d_values, 0, 0),
-        ],
-        1,
-    ).astype(BF16)
-    joint_grad = lax.psum_scatter(d_joint, BOTH, scatter_dimension=0, tiled=True).astype(F32)
-    own = lax.psum_scatter(
-        jnp.concatenate([dk_far, dv_far], 1), "seq", scatter_dimension=0, tiled=True
-    )
-    d_kv = jnp.concatenate([own, jnp.concatenate([dk_cont, dv_cont], 1)], 0)
-    d_rows = (
-        d_inner
-        + dot(d_queries, joint_full[:, :width], 1, 1)
-        + dot(d_kv, joint_full[:, width:], 1, 1)
-    )
-
+        [early[part * (1 + i) : part * (2 + i)] for i in range(fold)], 1
+    )
+    reduce_grad = early[part * (1 + fold) :]
+
+    dqs, owns, dkv_conts, joint_parts, sums = [], [], [], [], []
+    pick = lax.broadcasted_iota(jnp.int32, (1, lanes), 1)
+    ones = [jnp.where(pick == i, 1.0, 0.0).astype(BF16) for i in range(2)]
+    h0 = 0
+    for g, nh in enumerate(groups):
+        d_context = exchanges.step(d_context)
+        partial_sums = attention_backward(
+            queries, keys_values, far, context, d_context, prompt_inv, prompt_exp, 0, tile, h0, nh, None
+        )
+        d_context = exchanges.step(d_context)
+        dq, dkv_cont, dkv_far = attention_backward(
+            queries, keys_values, far, context, d_context, cont_inv, cont_exp, share, length, h0, nh,
+            partial_sums,
+        )
+        owns.append(
+            exchanges.add(
+                Scatter(
+                    dkv_far.reshape(lax.axis_size("seq"), share, -1),
+                    seq_bits[::-1],
+                    seq_bits,
+                    relative=True,
+                )
+            )
+        )
+        dqs.append(dq)
+        dkv_conts.append(dkv_cont)
+        columns = [
+            dot(rows, dq, 0, 0),
+            dot(prompt_all, dkv_far, 0, 0) + dot(cont_rows, dkv_cont, 0, 0),
+        ]
+        ones_of = [jnp.broadcast_to(ones[i], (dq.shape[0], lanes)) for i in range(2)]
+        value_sums = dot(dkv_far, jnp.broadcast_to(ones[1], (far, lanes)), 0, 0) + dot(
+            dkv_cont, ones_of[1][:cont_count], 0, 0
+        )
+        value_sums = value_sums.reshape(nh, 2, PAIR, lanes)[:, 1].reshape(-1, lanes)
+        sums.append(dot(dq, ones_of[0], 0, 0) + value_sums)
+        if g == len(groups) - 1:
+            columns.append(jnp.concatenate(sums, 0))
+        columns = jnp.concatenate(columns, 1).astype(BF16).reshape(devices, part, -1)
+        joint_parts.append(exchanges.add(Scatter(columns, scatter_order, dims)))
+        h0 += nh
+    exchanges.finish()
+    parts = [p.held for p in joint_parts]
+    pieces = [[], [], []]
+    for p, nh in zip(parts, groups):
+        pieces[0].append(p[:, : nh * PAIR])
+        for h in range(nh):
+            for s in range(2):
+                at = (nh + 2 * h + s) * PAIR
+                pieces[1 + s].append(p[:, at : at + PAIR])
+    joint_grad = jnp.concatenate(pieces[0] + pieces[1] + pieces[2], 1)
+    at = 3 * groups[-1] * PAIR
+    g_qbias, g_vbias = parts[-1][:, at], parts[-1][:, at + 1]
+
+    d_queries = jnp.concatenate(dqs, 1)
+    d_own = jnp.concatenate([d_queries[:share]] + [o.held.astype(BF16) for o in owns], 1)
+    d_cont = jnp.concatenate([d_queries[share:]] + dkv_conts, 1)
+    d_cont_rows = d_inner[share:] + dot(d_cont, joint_full, 1, 1)
+    d_prompt_rows = d_inner[:share] + dot(d_own, joint_full, 1, 1)
+
+    small = small.held
+    index = lax.axis_index(BOTH)
+    at = width + lanes
     head_grads = (
-        d_student_weight,
-        d_student_bias,
-        d_query,
-        d_pool_weight,
-        d_pool_bias,
-        d_class_weight,
-        d_class_bias,
-    )
-    vector_grads = (
-        d_query_bias,
-        d_value_bias,
-        d_output_bias,
-        d_first_gain,
-        d_first_shift,
-        d_expand_bias,
-        d_reduce_bias,
-        d_second_gain,
-        d_second_shift,
-    )
-    head_grads, vector_grads = lax.psum((head_grads, vector_grads), BOTH)
-    index = lax.axis_index(BOTH)
-
-    def own_part(vector):
-        size = vector.shape[0] // devices
-        return lax.dynamic_slice(vector, (index * size,), (size,))
-
-    (g_qbias, g_vbias, g_obias, g_fgain, g_fshift, g_ebias, g_rbias, g_sgain, g_sshift) = (
-        own_part(v) for v in vector_grads
-    )
+        small[:width],
+        small[at + lanes],
+        small[at + lanes + 1],
+        small[width:at],
+        small[at + lanes + 2],
+        small[at : at + lanes, :classes],
+        small[at + lanes + 3, :classes],
+    )
+    at += lanes + 4
+    vector_grads = []
+    for size in [width] * 6 + [hidden_width]:
+        vector = small[at : at + size // lanes].reshape(size)
+        own = size // devices
+        vector_grads.append(lax.dynamic_slice(vector, (index * own,), (own,)))
+        at += size // lanes
+    g_obias, g_fgain, g_fshift, g_rbias, g_sgain, g_sshift, g_ebias = vector_grads
     return (
         layer_low[:share][None],
         cont_layer.reshape(1, conts, length, width),
         logits[None],
-        d_rows[:share][None],
-        d_rows[share:].reshape(1, conts, length, width),
+        d_prompt_rows[None],
+        d_cont_rows.reshape(1, conts, length, width),
         joint_grad,
         g_qbias,
         g_vbias,
@@ -595,7 +751,7 @@
         g_rbias,
         g_sgain,
         g_sshift,
-    ) + tuple(head_grads)
+    ) + head_grads
 
 
 def solution(mesh):

time: 913 us -> 597 us (0.65)
  waiting for transfers between devices: 419 us -> 76.5 us
  blocking collectives: 41.4 us -> 0 us
  starting transfers between devices: 0.71 us -> 36.5 us
  Pallas kernels: 181 us -> 196 us
    reduce_scatter x2 -> x1, waiting for transfers between devices: 188 us -> 0.01 us  [local(): early = lax.psum_scatter(blocks, BOTH, scatter_dimension=0, tiled=True)]
    psum x1 -> x0, waiting for transfers between devices: 129 us -> none  [local(): head_grads, vector_grads = lax.psum((head_grads, vector_grads), BOTH)]
    all_gather x4 -> x2, waiting for transfers between devices: 101 us -> 0.01 us  [the longest x1 0.01 us: local(): lax.all_gather(jnp.concatenate([output_weight, expand_weight], 1).astype(...]
    ppermute x0 -> x38, waiting for transfers between devices: none -> 76.5 us  [across(): lax.ppermute(array, axis, [(i, i ^ bit) for i in range(lax.axis_size(axis...]
    psum x1 -> x0, blocking collectives: 41.4 us -> none  [local(): head_grads, vector_grads = lax.psum((head_grads, vector_grads), BOTH)]
    ppermute x0 -> x38, starting transfers between devices: none -> 36.4 us  [across(): lax.ppermute(array, axis, [(i, i ^ bit) for i in range(lax.axis_size(axis...]
    pallas_call x2 -> x6, Pallas kernels: 107 us -> 122 us  [attention_backward(): pl.pallas_call(functools.partial(attention_backward_kernel, near), grid=(...]
    convert_element_type x2 -> x24, other arithmetic: 2.66 us -> 15.8 us  [the longest x15 8.06 us: take(): self.held = total.astype(BF16)]
  transfers between devices with their start and end apart: 8 -> 41, of which waited for: 6 -> 16; matrix products, arithmetic and copies ran while one was open for 15% -> 23% of each run, Pallas kernels for 8% -> 33%
where the time goes in v2:
time: 597 us; the launch traced here: 590 us
  Pallas kernels  196 us (33%)
  matrix products  156 us (26%)
  waiting for transfers between devices  76.5 us (13%)
  other arithmetic  56.7 us (9%)
  local copies, waits for them, and re-layouts  51.3 us (9%)
  starting transfers between devices  36.5 us (6%)
  between operations  16.3 us (3%)
    dot_general x34, matrix products, dot(): lax.dot_general(left, right, (((left_dim,), (right_dim,)), ((), ())), pre...  152 us
    pallas_call x6, Pallas kernels, attention_backward(): pl.pallas_call(functools.partial(attention_backward_kernel, near), grid=(...  122 us
    ppermute x38, waiting for transfers between devices, across(): lax.ppermute(array, axis, [(i, i ^ bit) for i in range(lax.axis_size(axis...  76.5 us
    pallas_call x2, Pallas kernels, attention_forward(): pl.pallas_call(functools.partial(attention_forward_kernel, near), grid=(p...  74 us
    ppermute x38, starting transfers between devices, across(): lax.ppermute(array, axis, [(i, i ^ bit) for i in range(lax.axis_size(axis...  36.4 us
    unnamed x223, local copies, waits for them, and re-layouts  17.8 us
  transfers between devices with their start and end apart: 41, of which 16 were waited for; matrix products, arithmetic and copies ran while one was open for 23% of the time, Pallas kernels for 33%

profile of v2, /device:TPU:0, one launch (start us, length us, event | category | flops | bytes accessed | tf_op | source)
XLA Modules:
  0.0 589.8 jit_solution(2661542383902423673)
XLA Ops:
  37.0 8.7 %collective-permute-done.7 = bf16[2,2,1,1,1,24,1152]{6,5,4,3,2,1,0:T(8,128)(2,1)S(1)} collective-permute-done((bf16[2,2,1,1,1,24,1152]{6,5,4,3,2,1,0:T(8,128)(2,1)S(1)}, bf16[2,2,1,1,1,24,1152]{6,5,4,3,2,1,0:T(8,128)(2,1)S(1)}, u32[]{:S(2)}, u32[]{:S(2)}) %collective-permute-start.7) | collective-permute-done | bytes 221216 | tf_op jit(solution)/shard_map/ppermute | solution.py:337
  50.7 7.6 %collective-permute-done.8 = bf16[2,2,1,2,1,24,1152]{6,5,4,3,2,1,0:T(8,128)(2,1)S(1)} collective-permute-done((bf16[2,2,1,2,1,24,1152]{6,5,4,3,2,1,0:T(8,128)(2,1)S(1)}, bf16[2,2,1,2,1,24,1152]{6,5,4,3,2,1,0:T(8,128)(2,1)S(1)}, u32[]{:S(2)}, u32[]{:S(2)}) %collective-permute-start.8) | collective-permute-done | bytes 442400 | tf_op jit(solution)/shard_map/ppermute | solution.py:337
  67.7 5.2 fusion.27.refs_0_
  76.7 12.1 %add_convert_fusion.refs_1_.refs_2_.refs_3_.refs_4_.refs_7_.refs_8_ = bf16[3072,1536]{1,0:T(8,128)(2,1)} fusion(f32[1536]{0:T(1024)S(1)} %add.377, bf16[1024,768]{1,0:T(8,128)(2,1)S(1)} %bitcast.353, bf16[2048,768]{1,0:T(8,128)(2,1)S(1)} %bitcast.306, bf16[768,1280]{1,0:T(8,128)(2,1)S(1)} %bitcast.346, bf16[768,1152]{1,0:T(8,128)(2,1)S(1)} %bitcast.340), kind=kOutput, calls=%fused_computation.9 | convolution fusion | flops 7271350272 | bytes 17897472 | tf_op jit(solution)/shard_map/dot_general | solution.py:26
  88.7 25.6 %attention_forward.2 = (bf16[1536,768]{1,0:T(8,128)(2,1)}, f32[6,2,2,256]{3,2,1,0:T(2,128)}, bf16[6,2,2,2048,256]{4,3,2,1,0:T(8,128)(2,1)}) custom-call(bf16[1536,768]{1,0:T(8,128)(2,1)} %fusion.27.refs_0_, bf16[3072,1536]{1,0:T(8,128)(2,1)} %add_convert_fusion.refs_1_.refs_2_.refs_3_.refs_4_.refs_7_.refs_8_, ...), custom_call_target="tpu_custom_call" | custom-call | flops 3221225472 | bytes 25165824 | tf_op jit(solution)/shard_map/attention_forward/pallas_call | solution.py:154
  114.3 48.3 %attention_forward.3 = (bf16[1536,768]{1,0:T(8,128)(2,1)}, f32[6,4,2,256]{3,2,1,0:T(2,128)}, bf16[6,4,2,2304,256]{4,3,2,1,0:T(8,128)(2,1)}) custom-call(bf16[1536,768]{1,0:T(8,128)(2,1)} %fusion.27.refs_0_, bf16[3072,1536]{1,0:T(8,128)(2,1)} %add_convert_fusion.refs_1_.refs_2_.refs_3_.refs_4_.refs_7_.refs_8_, ...), custom_call_target="tpu_custom_call", output_to_operand_aliasing={{0}: (5, {})} | custom-call | flops 7247757312 | bytes 56623104 | tf_op jit(solution)/shard_map/attention_forward/pallas_call | solution.py:154
  162.7 5.0 fusion.132
  169.8 13.7 %multiply_convert_fusion = (bf16[1536,3072]{1,0:T(8,128)(2,1)}, f32[1536,3072]{1,0:T(8,128)}) fusion(f32[3072]{0:T(1024)S(1)} %add.388, bf16[768,3840]{1,0:T(8,128)(2,1)S(1)} %bitcast.405, f32[1536,768]{1,0:T(8,128)S(1)} %get-tuple-element.256, f32[768]{0:T(1024)S(1)} %get-tuple-element.204, f32[768]{0:T(1024)S(1)} %get-tuple-element.205, ...), kind=kOutput, calls=%fused_computation.7 | convolution fusion | flops 7281967104 | bytes 37785600 | tf_op jit(solution)/shard_map/dot_general | solution.py:26
  183.5 12.8 %fusion.133 = (f32[1536]{0:T(1024)S(1)}, f32[1536,768]{1,0:T(8,128)S(1)}) fusion(f32[768]{0:T(1024)S(1)} %get-tuple-element.203, bf16[1536,3072]{1,0:T(8,128)(2,1)} %get-tuple-element.257, bf16[3072,768]{1,0:T(8,128)(2,1)} %all-gather.5.cloned.1.call-done, f32[768]{0:T(1024)S(1)} %get-tuple-element.204, f32[768]{0:T(1024)S(1)} %get-tuple-element.205, ...), kind=kOutput, calls=%fused_computation.343 | convolution fusion | flops 7256013312 | bytes 23620608 | tf_op jit(solution)/shard_map/dot_general | solution.py:26
  218.5 11.2 %convolution_convert_fusion = bf16[3072,768]{1,0:T(8,128)(2,1)} fusion(bf16[1536,3072]{1,0:T(8,128)(2,1)S(1)} %bitcast.408, f32[1536,768]{1,0:T(8,128)S(1)} %get-tuple-element.218, f32[1536]{0:T(1024)S(1)} %negate_multiply_fusion.1), kind=kOutput, calls=%fused_computation.12 | convolution fusion | flops 7252475904 | bytes 18880512 | tf_op jit(solution)/shard_map/dot_general | solution.py:26
  231.2 18.9 %fusion.137 = (f32[3072]{0:T(1024)S(1)}, bf16[1536,3072]{1,0:T(8,128)(2,1)}) fusion(f32[1536,3072]{1,0:T(8,128)} %get-tuple-element.258, f32[3072]{0:T(1024)S(1)} %copy-done.71, bf16[3072,768]{1,0:T(8,128)(2,1)} %all-gather.5.cloned.1.call-done, f32[1536,768]{1,0:T(8,128)} %copy-done.10, f32[1536]{0:T(1024)S(1)} %negate_multiply_fusion.1), kind=kOutput, calls=%fused_computation.347 | convolution fusion | flops 7316173824 | bytes 37779456 | tf_op jit(solution)/shard_map/dot_general | solution.py:26
  250.2 13.6 %convolution_convert_fusion.1 = bf16[768,3072]{1,0:T(8,128)(2,1)} fusion(bf16[1536,3072]{1,0:T(8,128)(2,1)} %get-tuple-element.269, f32[1536,768]{1,0:T(8,128)S(1)} %bitcast.315, f32[768]{0:T(1024)S(1)} %copy-done.74, f32[768]{0:T(1024)S(1)} %copy-done.69, f32[1536]{0:T(1024)S(1)} %copy-done.63, f32[1536]{0:T(1024)S(1)} %copy-done.55), kind=kOutput, calls=%fused_computation.13 | convolution fusion | flops 7256014848 | bytes 18892800 | tf_op jit(solution)/shard_map/dot_general | solution.py:26
  263.8 14.1 %multiply_reduce_fusion.1 = (f32[768]{0:T(1024)S(1)}, f32[1536]{0:T(1024)S(1)}, f32[768]{0:T(1024)S(1)}, f32[1536,768]{1,0:T(8,128)}) fusion(f32[1536,768]{1,0:T(8,128)S(1)} %bitcast.315, f32[1536]{0:T(1024)S(1)} %copy-done.63, f32[1536]{0:T(1024)S(1)} %copy-done.55, f32[768]{0:T(1024)S(1)} %copy-done.69, ...), kind=kOutput, calls=%fused_computation.27 | convolution fusion | flops 7259550720 | bytes 28345344 | tf_op jit(solution)/shard_map/dot_general | solution.py:26
  295.0 6.1 %convolution_convert_fusion.2.refs_4_ = bf16[1536,768]{1,0:T(8,128)(2,1)} fusion(f32[1536,768]{1,0:T(8,128)} %copy-done.16, bf16[768,3840]{1,0:T(8,128)(2,1)} %all-gather.3.cloned.1.call-done), kind=kOutput, calls=%fused_computation.50 | convolution fusion | flops 1814298624 | bytes 8257536 | tf_op jit(solution)/shard_map/dot_general | solution.py:26
  306.7 18.5 %attention_backward.6 = (bf16[1536,384]{1,0:T(8,128)(2,1)}, f32[384,2048]{1,0:T(8,128)}, f32[384,2048]{1,0:T(8,128)}) custom-call(bf16[1536,768]{1,0:T(8,128)(2,1)} %fusion.27.refs_0_, bf16[3072,1536]{1,0:T(8,128)(2,1)} %add_convert_fusion.refs_1_.refs_2_.refs_3_.refs_4_.refs_7_.refs_8_, ...), custom_call_target="tpu_custom_call" | custom-call | flops 6291456 | bytes 6291456 | tf_op jit(solution)/shard_map/attention_backward/pallas_call | solution.py:285
  330.8 39.0 %attention_backward.7 = (bf16[1536,384]{1,0:T(8,128)(2,1)}, bf16[1024,768]{1,0:T(8,128)(2,1)}, bf16[2048,768]{1,0:T(8,128)(2,1)}) custom-call(bf16[1536,768]{1,0:T(8,128)(2,1)} %fusion.27.refs_0_, bf16[3072,1536]{1,0:T(8,128)(2,1)} %add_convert_fusion.refs_1_.refs_2_.refs_3_.refs_4_.refs_7_.refs_8_, ...), custom_call_target="tpu_custom_call", output_to_operand_aliasing={{0}: (11, {})} | custom-call | flops 14155776 | bytes 14155776 | tf_op jit(solution)/shard_map/attention_backward/pallas_call | solution.py:285
  387.5 13.7 %attention_backward.8 = (bf16[1536,256]{1,0:T(8,128)(2,1)}, f32[256,2048]{1,0:T(8,128)}, f32[256,2048]{1,0:T(8,128)}) custom-call(bf16[1536,768]{1,0:T(8,128)(2,1)} %fusion.27.refs_0_, bf16[3072,1536]{1,0:T(8,128)(2,1)} %add_convert_fusion.refs_1_.refs_2_.refs_3_.refs_4_.refs_7_.refs_8_, ...), custom_call_target="tpu_custom_call" | custom-call | flops 4194304 | bytes 4194304 | tf_op jit(solution)/shard_map/attention_backward/pallas_call | solution.py:285
  401.2 5.3 collective-permute-done.14
  413.0 27.4 %attention_backward.9 = (bf16[1536,256]{1,0:T(8,128)(2,1)}, bf16[1024,512]{1,0:T(8,128)(2,1)}, bf16[2048,512]{1,0:T(8,128)(2,1)}) custom-call(bf16[1536,768]{1,0:T(8,128)(2,1)} %fusion.27.refs_0_, bf16[3072,1536]{1,0:T(8,128)(2,1)} %add_convert_fusion.refs_1_.refs_2_.refs_3_.refs_4_.refs_7_.refs_8_, ...), custom_call_target="tpu_custom_call", output_to_operand_aliasing={{0}: (11, {})} | custom-call | flops 9437184 | bytes 9437184 | tf_op jit(solution)/shard_map/attention_backward/pallas_call | solution.py:285
  457.8 11.8 %collective-permute-done.17 = f32[1088,128]{1,0:T(8,128)S(1)} collective-permute-done((f32[1088,128]{1,0:T(8,128)S(1)}, f32[1088,128]{1,0:T(8,128)S(1)}, u32[]{:S(2)}, u32[]{:S(2)}) %collective-permute-start.17) | collective-permute-done | bytes 557088 | tf_op jit(solution)/shard_map/ppermute | solution.py:337
  471.9 8.5 %attention_backward.10 = (bf16[1536,128]{1,0:T(8,128)(2,1)}, f32[128,2048]{1,0:T(8,128)}, f32[128,2048]{1,0:T(8,128)}) custom-call(bf16[1536,768]{1,0:T(8,128)(2,1)} %fusion.27.refs_0_, bf16[3072,1536]{1,0:T(8,128)(2,1)} %add_convert_fusion.refs_1_.refs_2_.refs_3_.refs_4_.refs_7_.refs_8_, ...), custom_call_target="tpu_custom_call" | custom-call | flops 2097152 | bytes 2097152 | tf_op jit(solution)/shard_map/attention_backward/pallas_call | solution.py:285
  506.3 15.3 %attention_backward.11 = (bf16[1536,128]{1,0:T(8,128)(2,1)}, bf16[1024,256]{1,0:T(8,128)(2,1)}, bf16[2048,256]{1,0:T(8,128)(2,1)}) custom-call(bf16[1536,768]{1,0:T(8,128)(2,1)} %fusion.27.refs_0_, bf16[3072,1536]{1,0:T(8,128)(2,1)} %add_convert_fusion.refs_1_.refs_2_.refs_3_.refs_4_.refs_7_.refs_8_, ...), custom_call_target="tpu_custom_call", output_to_operand_aliasing={{0}: (11, {})} | custom-call | flops 4718592 | bytes 4718592 | tf_op jit(solution)/shard_map/attention_backward/pallas_call | solution.py:285
  531.8 6.8 %slice_add_fusion = f32[1024,768]{1,0:T(8,128)} fusion(f32[1536,768]{1,0:T(8,128)S(1)} %bitcast.325, bf16[768,1152]{1,0:T(8,128)(2,1)S(1)} %bitcast.341, bf16[768,1280]{1,0:T(8,128)(2,1)S(1)} %bitcast.347, bf16[1024,256]{1,0:T(8,128)(2,1)S(1)} %copy-done.34, bf16[1024,512]{1,0:T(8,128)(2,1)} %get-tuple-element.103, bf16[1024,768]{1,0:T(8,128)(2,1)S(1)} %copy-done.39, ...), kind=kOutput, calls=%fused_computation.53 | convolution fusion | flops 3650617344 | bytes 14745600 | tf_op jit(solution)/shard_map/dot_general | solution.py:26
  539.4 8.0 %collective-permute-done.28 = bf16[2,2,2,1,1,24,768]{6,5,4,3,2,1,0:T(8,128)(2,1)S(1)} collective-permute-done((bf16[2,2,2,1,1,24,768]{6,5,4,3,2,1,0:T(8,128)(2,1)S(1)}, bf16[2,2,2,1,1,24,768]{6,5,4,3,2,1,0:T(8,128)(2,1)S(1)}, u32[]{:S(2)}, u32[]{:S(2)}) %collective-permute-start.28) | collective-permute-done | bytes 294944 | tf_op jit(solution)/shard_map/ppermute | solution.py:337
  (509 shorter events, 216.2 us)
Async XLA Ops:
  7.2 155.5 %all-gather.3.cloned.1.call-start = ((), (), s32[]{:S(2)}) async-start(), calls=%async_computation.1 | async-start | bytes 6082560 | tf_op jit(solution)/shard_map/all_gather | solution.py:531
  9.8 173.7 %all-gather.5.cloned.1.call-start = ((), (), s32[]{:S(2)}) async-start(), calls=%async_computation.2 | async-start | bytes 4866048 | tf_op jit(solution)/shard_map/all_gather | solution.py:534
  14.6 11.6 %collective-permute-start.5 = (bf16[1,1,1,1,1,24,1152]{6,5,4,3,2,1,0:T(8,128)(2,1)S(1)}, bf16[1,1,1,1,1,24,1152]{6,5,4,3,2,1,0:T(8,128)(2,1)S(1)}, u32[]{:S(2)}, u32[]{:S(2)}) collective-permute-start(bf16[1,1,1,1,1,24,1152]{6,5,4,3,2,1,0:T(8,128)(2,1)S(1)} %bitcast.379), channel_id=1, source_target_pairs={{0,16},{4,20},{8,24},{12,28},{16,0},{20,4},{24,8},{28,12},{1,17},{... | collective-permute-start | bytes 165896 | tf_op jit(solution)/shard_map/ppermute | solution.py:337
  18.8 40.6 %collective-permute-start.10 = (bf16[1,1,512,768]{3,2,1,0:T(8,128)(2,1)}, bf16[1,1,512,768]{3,2,1,0:T(8,128)(2,1)}, u32[]{:S(2)}, u32[]{:S(2)}) collective-permute-start(bf16[1,1,512,768]{3,2,1,0:T(8,128)(2,1)} %bitcast.329), channel_id=1, source_target_pairs={{0,2},{1,3},{2,0},{3,1},{4,6},{5,7},{6,4},{7,5},{8,10},{9,11},{10,... | collective-permute-start | bytes 2359304 | tf_op jit(solution)/shard_map/ppermute | solution.py:337
  22.3 557.4 %reduce-scatter.2.cloned.1.call-start = ((), (), s32[]{:S(2)}) async-start(), calls=%async_computation.3 | async-start | bytes 10948608 | tf_op jit(solution)/shard_map/reduce_scatter | solution.py:647
  33.4 12.4 %collective-permute-start.7 = (bf16[2,2,1,1,1,24,1152]{6,5,4,3,2,1,0:T(8,128)(2,1)S(1)}, bf16[2,2,1,1,1,24,1152]{6,5,4,3,2,1,0:T(8,128)(2,1)S(1)}, u32[]{:S(2)}, u32[]{:S(2)}) collective-permute-start(bf16[2,2,1,1,1,24,1152]{6,5,4,3,2,1,0:T(8,128)(2,1)S(1)} %maximum_select_fusion.11), channel_id=1, source_target_pairs={{0,2},{1,3},{2,0},{3,1},{4,6},{5,7},{6,4},{7,5},{8,10},{9,11},{10,... | collective-permute-start | bytes 663560 | tf_op jit(solution)/shard_map/ppermute | solution.py:337
  35.4 12.6 %collective-permute-start.2 = (bf16[2,2,1,1,1,24,1280]{6,5,4,3,2,1,0:T(8,128)(2,1)S(1)}, bf16[2,2,1,1,1,24,1280]{6,5,4,3,2,1,0:T(8,128)(2,1)S(1)}, u32[]{:S(2)}, u32[]{:S(2)}) collective-permute-start(bf16[2,2,1,1,1,24,1280]{6,5,4,3,2,1,0:T(8,128)(2,1)S(1)} %copy.103), channel_id=1, source_target_pairs={{0,4},{4,0},{8,12},{12,8},{16,20},{20,16},{24,28},{28,24},{1,5},{5... | collective-permute-start | bytes 737288 | tf_op jit(solution)/shard_map/ppermute | solution.py:337
  45.9 12.4 %collective-permute-start.8 = (bf16[2,2,1,2,1,24,1152]{6,5,4,3,2,1,0:T(8,128)(2,1)S(1)}, bf16[2,2,1,2,1,24,1152]{6,5,4,3,2,1,0:T(8,128)(2,1)S(1)}, u32[]{:S(2)}, u32[]{:S(2)}) collective-permute-start(bf16[2,2,1,2,1,24,1152]{6,5,4,3,2,1,0:T(8,128)(2,1)S(1)} %maximum_select_fusion.7), channel_id=1, source_target_pairs={{0,4},{4,0},{8,12},{12,8},{16,20},{20,16},{24,28},{28,24},{1,5},{5... | collective-permute-start | bytes 1327112 | tf_op jit(solution)/shard_map/ppermute | solution.py:337
  301.6 27.9 %collective-permute-start.12 = (f32[1088,128]{1,0:T(8,128)S(1)}, f32[1088,128]{1,0:T(8,128)S(1)}, u32[]{:S(2)}, u32[]{:S(2)}) collective-permute-start(f32[1088,128]{1,0:T(8,128)S(1)} %concatenate.677), channel_id=1, source_target_pairs={{0,16},{4,20},{8,24},{12,28},{16,0},{20,4},{24,8},{28,12},{1,17},{... | collective-permute-start | bytes 1671176 | tf_op jit(solution)/shard_map/ppermute | solution.py:337
  330.3 50.8 %collective-permute-start.13 = (f32[1088,128]{1,0:T(8,128)}, f32[1088,128]{1,0:T(8,128)}, u32[]{:S(2)}, u32[]{:S(2)}) collective-permute-start(f32[1088,128]{1,0:T(8,128)} %add.411), channel_id=1, source_target_pairs={{0,8},{4,12},{8,0},{12,4},{16,24},{20,28},{24,16},{28,20},{1,9},{5... | collective-permute-start | bytes 1671176 | tf_op jit(solution)/shard_map/ppermute | solution.py:337
  383.3 25.4 %collective-permute-start.16 = (bf16[2,2,2,2,1,24,1152]{6,5,4,3,2,1,0:T(8,128)(2,1)}, bf16[2,2,2,2,1,24,1152]{6,5,4,3,2,1,0:T(8,128)(2,1)}, u32[]{:S(2)}, u32[]{:S(2)}) collective-permute-start(bf16[2,2,2,2,1,24,1152]{6,5,4,3,2,1,0:T(8,128)(2,1)} %fusion.55), channel_id=1, source_target_pairs={{0,1},{1,0},{2,3},{3,2},{4,5},{5,4},{6,7},{7,6},{8,9},{9,8},{10,11... | collective-permute-start | bytes 2654216 | tf_op jit(solution)/shard_map/ppermute | solution.py:337
  383.9 22.7 %collective-permute-start.14 = (f32[1088,128]{1,0:T(8,128)}, f32[1088,128]{1,0:T(8,128)}, u32[]{:S(2)}, u32[]{:S(2)}) collective-permute-start(f32[1088,128]{1,0:T(8,128)} %add.412), channel_id=1, source_target_pairs={{0,4},{4,0},{8,12},{12,8},{16,20},{20,16},{24,28},{28,24},{1,5},{5... | collective-permute-start | bytes 1671176 | tf_op jit(solution)/shard_map/ppermute | solution.py:337
  384.6 26.6 %collective-permute-start.15 = (bf16[2,1,512,768]{3,2,1,0:T(8,128)(2,1)}, bf16[2,1,512,768]{3,2,1,0:T(8,128)(2,1)}, u32[]{:S(2)}, u32[]{:S(2)}) collective-permute-start(bf16[2,1,512,768]{3,2,1,0:T(8,128)(2,1)} %dynamic_slice.196), channel_id=1, source_target_pairs={{0,1},{1,0},{2,3},{3,2},{4,5},{5,4},{6,7},{7,6},{8,9},{9,8},{10,11... | collective-permute-start | bytes 4718600 | tf_op jit(solution)/shard_map/ppermute | solution.py:337
  444.6 13.1 %collective-permute-start.18 = (bf16[2,2,2,1,1,24,1152]{6,5,4,3,2,1,0:T(8,128)(2,1)S(1)}, bf16[2,2,2,1,1,24,1152]{6,5,4,3,2,1,0:T(8,128)(2,1)S(1)}, u32[]{:S(2)}, u32[]{:S(2)}) collective-permute-start(bf16[2,2,2,1,1,24,1152]{6,5,4,3,2,1,0:T(8,128)(2,1)S(1)} %copy-done.49), channel_id=1, source_target_pairs={{0,2},{1,3},{2,0},{3,1},{4,6},{5,7},{6,4},{7,5},{8,10},{9,11},{10,... | collective-permute-start | bytes 1327112 | tf_op jit(solution)/shard_map/ppermute | solution.py:337
  446.3 23.3 %collective-permute-start.17 = (f32[1088,128]{1,0:T(8,128)S(1)}, f32[1088,128]{1,0:T(8,128)S(1)}, u32[]{:S(2)}, u32[]{:S(2)}) collective-permute-start(f32[1088,128]{1,0:T(8,128)S(1)} %copy-done.30), channel_id=1, source_target_pairs={{0,2},{1,3},{2,0},{3,1},{4,6},{5,7},{6,4},{7,5},{8,10},{9,11},{10,... | collective-permute-start | bytes 1671176 | tf_op jit(solution)/shard_map/ppermute | solution.py:337
  446.7 39.1 %collective-permute-start.22 = (bf16[1,1,512,768]{3,2,1,0:T(8,128)(2,1)S(1)}, bf16[1,1,512,768]{3,2,1,0:T(8,128)(2,1)}, u32[]{:S(2)}, u32[]{:S(2)}) collective-permute-start(bf16[1,1,512,768]{3,2,1,0:T(8,128)(2,1)S(1)} %dynamic_slice.200), channel_id=1, source_target_pairs={{0,2},{1,3},{2,0},{3,1},{4,6},{5,7},{6,4},{7,5},{8,10},{9,11},{10,... | collective-permute-start | bytes 2359304 | tf_op jit(solution)/shard_map/ppermute | solution.py:337
  471.3 16.7 %collective-permute-start.37 = (f32[1088,128]{1,0:T(8,128)S(1)}, f32[1088,128]{1,0:T(8,128)S(1)}, u32[]{:S(2)}, u32[]{:S(2)}) collective-permute-start(f32[1088,128]{1,0:T(8,128)S(1)} %add.420), channel_id=1, source_target_pairs={{0,1},{1,0},{2,3},{3,2},{4,5},{5,4},{6,7},{7,6},{8,9},{9,8},{10,11... | collective-permute-start | bytes 1671176 | tf_op jit(solution)/shard_map/ppermute | solution.py:337
  471.4 27.7 %collective-permute-start.21 = (bf16[2,2,2,2,1,24,768]{6,5,4,3,2,1,0:T(8,128)(2,1)}, bf16[2,2,2,2,1,24,768]{6,5,4,3,2,1,0:T(8,128)(2,1)}, u32[]{:S(2)}, u32[]{:S(2)}) collective-permute-start(bf16[2,2,2,2,1,24,768]{6,5,4,3,2,1,0:T(8,128)(2,1)} %fusion.58), channel_id=1, source_target_pairs={{0,1},{1,0},{2,3},{3,2},{4,5},{5,4},{6,7},{7,6},{8,9},{9,8},{10,11... | collective-permute-start | bytes 1769480 | tf_op jit(solution)/shard_map/ppermute | solution.py:337
  471.9 29.6 %collective-permute-start.20 = (bf16[2,1,512,512]{3,2,1,0:T(8,128)(2,1)}, bf16[2,1,512,512]{3,2,1,0:T(8,128)(2,1)}, u32[]{:S(2)}, u32[]{:S(2)}) collective-permute-start(bf16[2,1,512,512]{3,2,1,0:T(8,128)(2,1)} %dynamic_slice.203), channel_id=1, source_target_pairs={{0,1},{1,0},{2,3},{3,2},{4,5},{5,4},{6,7},{7,6},{8,9},{9,8},{10,11... | collective-permute-start | bytes 3145736 | tf_op jit(solution)/shard_map/ppermute | solution.py:337
  503.8 24.6 %collective-permute-start.26 = (bf16[2,1,1,1,1,24,1152]{6,5,4,3,2,1,0:T(8,128)(2,1)}, bf16[2,1,1,1,1,24,1152]{6,5,4,3,2,1,0:T(8,128)(2,1)}, u32[]{:S(2)}, u32[]{:S(2)}) collective-permute-start(bf16[2,1,1,1,1,24,1152]{6,5,4,3,2,1,0:T(8,128)(2,1)} %constant_dynamic-slice_fusion.10), channel_id=1, source_target_pairs={{0,8},{4,12},{8,0},{12,4},{16,24},{20,28},{24,16},{28,20},{1,9},{5... | collective-permute-start | bytes 331784 | tf_op jit(solution)/shard_map/ppermute | solution.py:337
  504.8 57.8 %collective-permute-start.23 = (bf16[1,1,512,512]{3,2,1,0:T(8,128)(2,1)}, bf16[1,1,512,512]{3,2,1,0:T(8,128)(2,1)}, u32[]{:S(2)}, u32[]{:S(2)}) collective-permute-start(bf16[1,1,512,512]{3,2,1,0:T(8,128)(2,1)} %dynamic_slice.207), channel_id=1, source_target_pairs={{0,2},{1,3},{2,0},{3,1},{4,6},{5,7},{6,4},{7,5},{8,10},{9,11},{10,... | collective-permute-start | bytes 1572872 | tf_op jit(solution)/shard_map/ppermute | solution.py:337
  528.3 19.8 %collective-permute-start.32 = (bf16[2,2,2,2,1,24,512]{6,5,4,3,2,1,0:T(8,128)(2,1)S(1)}, bf16[2,2,2,2,1,24,512]{6,5,4,3,2,1,0:T(8,128)(2,1)S(1)}, u32[]{:S(2)}, u32[]{:S(2)}) collective-permute-start(bf16[2,2,2,2,1,24,512]{6,5,4,3,2,1,0:T(8,128)(2,1)S(1)} %constant_dynamic-slice_fusion.4), channel_id=1, source_target_pairs={{0,1},{1,0},{2,3},{3,2},{4,5},{5,4},{6,7},{7,6},{8,9},{9,8},{10,11... | collective-permute-start | bytes 1179656 | tf_op jit(solution)/shard_map/ppermute | solution.py:337
  539.3 19.0 %collective-permute-start.24 = (bf16[2,1,512,256]{3,2,1,0:T(8,128)(2,1)S(1)}, bf16[2,1,512,256]{3,2,1,0:T(8,128)(2,1)S(1)}, u32[]{:S(2)}, u32[]{:S(2)}) collective-permute-start(bf16[2,1,512,256]{3,2,1,0:T(8,128)(2,1)S(1)} %dynamic_slice.213), channel_id=1, source_target_pairs={{0,1},{1,0},{2,3},{3,2},{4,5},{5,4},{6,7},{7,6},{8,9},{9,8},{10,11... | collective-permute-start | bytes 1572872 | tf_op jit(solution)/shard_map/ppermute | solution.py:337
  558.5 17.9 %collective-permute-start.25 = (bf16[1,1,512,256]{3,2,1,0:T(8,128)(2,1)S(1)}, bf16[1,1,512,256]{3,2,1,0:T(8,128)(2,1)S(1)}, u32[]{:S(2)}, u32[]{:S(2)}) collective-permute-start(bf16[1,1,512,256]{3,2,1,0:T(8,128)(2,1)S(1)} %dynamic_slice.215), channel_id=1, source_target_pairs={{0,2},{1,3},{2,0},{3,1},{4,6},{5,7},{6,4},{7,5},{8,10},{9,11},{10,... | collective-permute-start | bytes 786440 | tf_op jit(solution)/shard_map/ppermute | solution.py:337
  (113 other events, 1460.0 us)
Sparse Core Ops, SparseCore 0:
  11.5 72.9 all-gather.2
  88.0 62.7 all-gather.4
  306.8 146.9 reduce-scatter.1

commit v3 on v2

v3 whole, which is shorter than its diff:
```python
import functools

import jax
import jax.numpy as jnp
from jax import lax
from jax.experimental import pallas as pl
from jax.experimental.pallas import tpu as pltpu
from jax.sharding import PartitionSpec as P

HEAD_DIM = 64
POOL_HEADS = 2
PAIR = 2 * HEAD_DIM

EPSILON = 1e-06
HIGHEST = lax.Precision.HIGHEST
NEGATIVE = -1e30
BOTH = ("grp", "seq")
BF16 = jnp.bfloat16
F32 = jnp.float32
LOG2_E = 1.4426950408889634
SUM_LOW, SUM_HIGH = 1e-12, 1e18
VMEM_LIMIT = 56 << 20


def dot(left, right, left_dim, right_dim):
    return lax.dot_general(
        left, right, (((left_dim,), (right_dim,)), ((), ())), preferred_element_type=F32
    )


def precise(left, right):
    return jnp.dot(left, right, precision=HIGHEST, preferred_element_type=F32)


def attention_forward_kernel(near, *refs):
    if near:
        q_ref, k_ref, v_ref, kn_ref, vn_ref, _, out_ref, inv_ref, exp_ref, vt_ref, s_ref = refs
    else:
        q_ref, k_ref, v_ref, out_ref, inv_ref, exp_ref, vt_ref, s_ref = refs
    far = k_ref.shape[0]
    tile = q_ref.shape[0]

    @pl.when(pl.program_id(1) == 0)
    def _():
        vt_ref[...] = v_ref[...].T

    q = q_ref[...]
    lane = lax.broadcasted_iota(jnp.int32, q.shape, 1)
    masked = [
        jnp.where((lane < HEAD_DIM) if h == 0 else (lane >= HEAD_DIM), q, jnp.zeros_like(q))
        for h in range(2)
    ]
    heads = [slice(h * HEAD_DIM, (h + 1) * HEAD_DIM) for h in range(2)]
    if near:
        vnt = vn_ref[...].T
        allowed = lax.broadcasted_iota(jnp.int32, (tile, tile), 0) <= lax.broadcasted_iota(
            jnp.int32, (tile, tile), 1
        )

    def near_scores(h):
        return jnp.where(allowed, dot(kn_ref[...], masked[h], 1, 1), NEGATIVE)

    def finish(outs):
        out_ref[...] = jnp.concatenate(outs, 0).T.astype(out_ref.dtype)

    outs = []
    fine = None
    for h in range(2):
        e = jnp.exp2(dot(k_ref[...], masked[h], 1, 1) * LOG2_E)
        total = jnp.sum(e, axis=0, keepdims=True)
        low = e.astype(BF16)
        exp_ref[0, 0, h, 0:far, :] = low
        out = dot(vt_ref[heads[h], :], low, 1, 0)
        if near:
            e = jnp.exp2(near_scores(h) * LOG2_E)
            total = total + jnp.sum(e, axis=0, keepdims=True)
            low = e.astype(BF16)
            exp_ref[0, 0, h, far:, :] = low
            out = out + dot(vnt[heads[h], :], low, 1, 0)
        inverse = 1.0 / total
        inv_ref[0, 0, h : h + 1, :] = inverse
        outs.append(out * inverse)
        good = jnp.where((total > SUM_LOW) & (total < SUM_HIGH), 1.0, 0.0)
        fine = good if fine is None else jnp.minimum(fine, good)
    finish(outs)

    @pl.when(jnp.min(fine) < 0.5)
    def _():
        chunk = tile
        steps = far // chunk
        outs = []
        for h in range(2):

            def score(c, top):
                at = pl.multiple_of(c * chunk, chunk)
                s = dot(k_ref[pl.ds(at, chunk), :], masked[h], 1, 1)
                s_ref[pl.ds(at, chunk), :] = s
                return jnp.maximum(top, jnp.max(s, axis=0, keepdims=True))

            top = jnp.full((1, tile), NEGATIVE, F32)
            if near:
                sn = near_scores(h)
                top = jnp.max(sn, axis=0, keepdims=True)
            top = lax.fori_loop(0, steps, score, top)

            def weigh(c, carry):
                total, out = carry
                at = pl.multiple_of(c * chunk, chunk)
                e = jnp.exp2((s_ref[pl.ds(at, chunk), :] - top) * LOG2_E)
                low = e.astype(BF16)
                exp_ref[0, 0, h, pl.ds(at, chunk), :] = low
                part = dot(v_ref[pl.ds(at, chunk), :], low, 0, 0)[heads[h], :]
                return total + jnp.sum(e, axis=0, keepdims=True), out + part

            total = jnp.zeros((1, tile), F32)
            out = jnp.zeros((HEAD_DIM, tile), F32)
            if near:
                e = jnp.exp2((sn - top) * LOG2_E)
                low = e.astype(BF16)
                exp_ref[0, 0, h, far:, :] = low
                total = jnp.sum(e, axis=0, keepdims=True)
                out = dot(vnt[heads[h], :], low, 1, 0)
            total, out = lax.fori_loop(0, steps, weigh, (total, out))
            inverse = 1.0 / total
            inv_ref[0, 0, h : h + 1, :] = inverse
            outs.append(out * inverse)
        finish(outs)


def attention_forward(queries, keys_values, far, count, at, tile, into):
    near = into is not None
    total, width = queries.shape
    pairs = width // PAIR
    tiles = count // tile
    held = far + (tile if near else 0)
    block = at // tile
    specs = [
        pl.BlockSpec((tile, PAIR), lambda h, t: (block + t, h)),
        pl.BlockSpec((far, PAIR), lambda h, t: (0, 2 * h)),
        pl.BlockSpec((far, PAIR), lambda h, t: (0, 2 * h + 1)),
    ]
    operands = [queries, keys_values, keys_values]
    aliases = {}
    if near:
        first = far // tile
        specs += [
            pl.BlockSpec((tile, PAIR), lambda h, t: (first + t, 2 * h)),
            pl.BlockSpec((tile, PAIR), lambda h, t: (first + t, 2 * h + 1)),
            pl.BlockSpec(memory_space=pl.ANY),
        ]
        operands += [keys_values, keys_values, into]
        aliases = {5: 0}
    cells = count * held * width // HEAD_DIM
    return pl.pallas_call(
        functools.partial(attention_forward_kernel, near),
        grid=(pairs, tiles),
        in_specs=specs,
        out_specs=[
            pl.BlockSpec((tile, PAIR), lambda h, t: (block + t, h)),
            pl.BlockSpec((1, 1, 2, tile), lambda h, t: (h, t, 0, 0)),
            pl.BlockSpec((1, 1, 2, held, tile), lambda h, t: (h, t, 0, 0, 0)),
        ],
        out_shape=[
            jax.ShapeDtypeStruct((total, width), BF16),
            jax.ShapeDtypeStruct((pairs, tiles, 2, tile), F32),
            jax.ShapeDtypeStruct((pairs, tiles, 2, held, tile), BF16),
        ],
        scratch_shapes=[pltpu.VMEM((PAIR, far), BF16), pltpu.VMEM((far, tile), F32)],
        input_output_aliases=aliases,
        compiler_params=pltpu.CompilerParams(vmem_limit_bytes=VMEM_LIMIT),
        cost_estimate=pl.CostEstimate(
            flops=4 * cells * HEAD_DIM, bytes_accessed=2 * cells, transcendentals=cells
        ),
        name="attention_forward",
    )(*operands)


def attention_backward_kernel(cont_tiles, *refs):
    k_ref, v_ref, kn_ref, vn_ref = refs[:4]
    cont_refs, prompt_refs = refs[4:9], refs[9:14]
    rows_ref, prompt_rows_ref = refs[14:16]
    dq_ref, dkvn_ref, dkv_ref, weight_ref, sums_ref, kt_ref, dkt_ref, dvt_ref = refs[-8:]
    at = pl.program_id(1)

    @pl.when(at == 0)
    def _():
        kt_ref[...] = k_ref[...].T
        dkt_ref[...] = jnp.zeros_like(dkt_ref)
        dvt_ref[...] = jnp.zeros_like(dvt_ref)

    def tile_of(near, tile_refs, first):
        q_ref, out_ref, dout_ref, inv_ref, exp_ref = tile_refs
        far = k_ref.shape[0]
        tile = q_ref.shape[0]
        qt = q_ref[...].T
        dout = dout_ref[...].astype(F32).T
        product = out_ref[...].astype(F32).T * dout
        if near:
            knt = kn_ref[...].T
        zero = jnp.zeros((HEAD_DIM, tile), BF16)
        dqs, dkn, dvn = [], [], []
        for h in range(2):
            rows = slice(h * HEAD_DIM, (h + 1) * HEAD_DIM)
            inverse = inv_ref[0, 0, h : h + 1, :]
            delta = jnp.sum(product[rows, :], axis=0, keepdims=True) * inverse
            do = (dout[rows, :] * inverse).astype(BF16)
            padded = jnp.concatenate([do, zero] if h == 0 else [zero, do], 0)
            e = exp_ref[0, 0, h, 0:far, :]
            ds = (e.astype(F32) * (dot(v_ref[...], padded, 1, 0) - delta)).astype(BF16)
            dvt_ref[rows, :] += dot(do, e, 1, 1)
            dkt_ref[rows, :] += dot(qt[rows, :], ds, 1, 1)
            dq = dot(kt_ref[rows, :], ds, 1, 0)
            if near:
                e = exp_ref[0, 0, h, far:, :]
                ds = (e.astype(F32) * (dot(vn_ref[...], padded, 1, 0) - delta)).astype(BF16)
                dvn.append(dot(do, e, 1, 1))
                dkn.append(dot(qt[rows, :], ds, 1, 1))
                dq = dq + dot(knt[rows, :], ds, 1, 0)
            dqs.append(dq * HEAD_DIM ** (-0.5))
        row = pl.ds(pl.multiple_of(first, tile), tile)
        dq_ref[row, :] = jnp.concatenate(dqs, 0).T.astype(dq_ref.dtype)
        if near:
            dkvn_ref[row, :PAIR] = jnp.concatenate(dkn, 0).T.astype(dkvn_ref.dtype)
            dkvn_ref[row, PAIR:] = jnp.concatenate(dvn, 0).T.astype(dkvn_ref.dtype)

    @pl.when(at < cont_tiles)
    def _():
        tile_of(True, cont_refs, at * cont_refs[0].shape[0])

    @pl.when(at >= cont_tiles)
    def _():
        tile_of(False, prompt_refs, dkvn_ref.shape[0] + (at - cont_tiles) * prompt_refs[0].shape[0])

    @pl.when(at == pl.num_programs(1) - 1)
    def _():
        dkv_ref[:, :PAIR] = dkt_ref[...].T.astype(dkv_ref.dtype)
        dkv_ref[:, PAIR:] = dvt_ref[...].T.astype(dkv_ref.dtype)
        count = dkvn_ref.shape[0]
        weight_ref[:, :PAIR] = dot(rows_ref[...], dq_ref[...], 1, 0).astype(weight_ref.dtype)
        weight_ref[:, PAIR:] = (
            dot(prompt_rows_ref[...], dkv_ref[...], 1, 0)
            + dot(rows_ref[:, :count], dkvn_ref[...], 1, 0)
        ).astype(weight_ref.dtype)

        def sums_of(ref):
            return dot(jnp.ones((8, ref.shape[0]), BF16), ref[...], 1, 0)

        sums_ref[0, :, :PAIR] = sums_of(dq_ref)
        sums_ref[0, :, PAIR:] = sums_of(dkv_ref) + sums_of(dkvn_ref)


def attention_backward(
    queries, keys_values, far, context, d_context, cont_held, prompt_held, rows_t, prompt_t, h0, nh,
    into,
):
    total, width = queries.shape
    cont_tiles, length = cont_held[1].shape[1], cont_held[1].shape[4]
    tiles, tile = prompt_held[1].shape[1], prompt_held[1].shape[4]
    count = cont_tiles * length
    first, behind = far // length, count // tile

    def cont_at(t):
        return jnp.minimum(t, cont_tiles - 1)

    def prompt_at(t):
        return jnp.maximum(t - cont_tiles, 0)

    def tile_specs(size, held, start, at):
        row = pl.BlockSpec((size, PAIR), lambda h, t: (start + at(t), h0 + h))
        return [
            row,
            row,
            row,
            pl.BlockSpec((1, 1, 2, size), lambda h, t: (h0 + h, at(t), 0, 0)),
            pl.BlockSpec((1, 1, 2, held, size), lambda h, t: (h0 + h, at(t), 0, 0, 0)),
        ]

    specs = [
        pl.BlockSpec((far, PAIR), lambda h, t: (0, 2 * (h0 + h))),
        pl.BlockSpec((far, PAIR), lambda h, t: (0, 2 * (h0 + h) + 1)),
        pl.BlockSpec((length, PAIR), lambda h, t: (first + cont_at(t), 2 * (h0 + h))),
        pl.BlockSpec((length, PAIR), lambda h, t: (first + cont_at(t), 2 * (h0 + h) + 1)),
    ]
    specs += tile_specs(length, far + length, 0, cont_at)
    specs += tile_specs(tile, far, behind, prompt_at)
    whole = pl.Buffered(1)
    specs += [
        pl.BlockSpec((width, total), lambda h, t: (0, 0), pipeline_mode=whole),
        pl.BlockSpec((width, far), lambda h, t: (0, 0), pipeline_mode=whole),
    ]
    specs += [pl.BlockSpec(memory_space=pl.ANY)] * len(into)
    wide = 2 * PAIR
    cells = (count * (far + length) + tiles * tile * far) * nh * 2
    return pl.pallas_call(
        functools.partial(attention_backward_kernel, cont_tiles),
        grid=(nh, cont_tiles + tiles),
        in_specs=specs,
        out_specs=[
            pl.BlockSpec((total, PAIR), lambda h, t: (0, h0 + h)),
            pl.BlockSpec((count, wide), lambda h, t: (0, h0 + h)),
            pl.BlockSpec((far, wide), lambda h, t: (0, h)),
            pl.BlockSpec((width, 3 * PAIR), lambda h, t: (0, h)),
            pl.BlockSpec((1, 8, 3 * PAIR), lambda h, t: (h, 0, 0)),
        ],
        out_shape=[
            jax.ShapeDtypeStruct((total, width), BF16),
            jax.ShapeDtypeStruct((count, 2 * width), BF16),
            jax.ShapeDtypeStruct((far, nh * wide), BF16),
            jax.ShapeDtypeStruct((width, nh * 3 * PAIR), BF16),
            jax.ShapeDtypeStruct((nh, 8, 3 * PAIR), F32),
        ],
        scratch_shapes=[
            pltpu.VMEM((PAIR, far), BF16),
            pltpu.VMEM((PAIR, far), F32),
            pltpu.VMEM((PAIR, far), F32),
        ],
        input_output_aliases={16 + n: n for n in range(len(into))},
        compiler_params=pltpu.CompilerParams(vmem_limit_bytes=VMEM_LIMIT),
        cost_estimate=pl.CostEstimate(flops=cells, bytes_accessed=cells // 16, transcendentals=0),
        name="attention_backward",
    )(
        keys_values, keys_values, keys_values, keys_values,
        queries, context, d_context, *cont_held,
        queries, context, d_context, *prompt_held,
        rows_t, prompt_t, *into,
    )


def turn_kernel(x_ref, out_ref):
    out_ref[...] = x_ref[...].T


def turned(rows):
    count, width = rows.shape
    tile = count // 2 if (count // 2) % PAIR == 0 else count
    return pl.pallas_call(
        turn_kernel,
        grid=(count // tile,),
        in_specs=[pl.BlockSpec((tile, width), lambda t: (t, 0))],
        out_specs=pl.BlockSpec((width, tile), lambda t: (0, t)),
        out_shape=jax.ShapeDtypeStruct((width, count), rows.dtype),
        compiler_params=pltpu.CompilerParams(vmem_limit_bytes=VMEM_LIMIT),
        name="turn",
    )(rows)


def gelu_pair(pre):
    half = 0.5 * (1.0 + lax.erf(pre * (0.5**0.5)))
    slope = half + pre * (jnp.exp(-0.5 * pre * pre) * 0.3989422804014327)
    return pre * half, slope


def exact(left, right, left_dim, right_dim):
    return lax.dot_general(
        left,
        right,
        (((left_dim,), (right_dim,)), ((), ())),
        precision=HIGHEST,
        preferred_element_type=F32,
    )


def total_of(array):
    return jnp.sum(array, axis=0, keepdims=True)


def dense_kernel(cont_tiles, length, classes, *refs):
    (
        label_ref, x_ref, context_ref, cot_ref, first_weight_ref, reduce_ref, vector_ref, ebias_ref,
        student_ref, head_ref, pool_ref, class_ref,
        layer_ref, logits_ref, first_ref, hidden_ref, dmixed_ref, dpre_ref, dinner_ref,
        dinner_low_ref, dcontext_ref, small_ref, expand_sum_ref,
        hat_ref, mixed_ref, slope_ref, cotangent_ref,
    ) = refs
    at = pl.program_id(0)
    count, width = x_ref.shape
    lanes = student_ref.shape[1]
    inner = hidden_ref.shape[1]
    chunk = width
    obias, fgain, fshift, rbias, sgain, sshift = (vector_ref[i : i + 1, :] for i in range(2, 8))
    vectors_at = width + 2 * lanes + 4

    @pl.when(at == 0)
    def _():
        small_ref[...] = jnp.zeros_like(small_ref)
        expand_sum_ref[...] = jnp.zeros_like(expand_sum_ref)

    def add_vector(which, row):
        start = vectors_at + which * (width // lanes)
        for i in range(width // lanes):
            small_ref[start + i : start + i + 1, :] += row[:, i * lanes : (i + 1) * lanes]

    def normal(rows):
        center = rows - jnp.mean(rows, -1, keepdims=True)
        scale = lax.rsqrt(jnp.mean(center * center, -1, keepdims=True) + EPSILON)
        return center * scale, scale

    def normal_back(grad, hat, scale, gain):
        scaled = grad * gain
        return scale * (
            scaled
            - jnp.mean(scaled, -1, keepdims=True)
            - hat * jnp.mean(scaled * hat, -1, keepdims=True)
        )

    branch = dot(context_ref[...], first_weight_ref[:, :width], 1, 0) + obias
    hat, first_scale = normal(x_ref[...].astype(F32) + branch)
    hat_ref[...] = hat
    first = hat * fgain + fshift
    first_ref[...] = first.astype(BF16)
    mixed_ref[...] = first + rbias

    @pl.loop(0, inner // chunk)
    def _(c):
        columns = pl.ds(pl.multiple_of(c * chunk, chunk), chunk)
        behind = pl.ds(pl.multiple_of(width + c * chunk, chunk), chunk)
        pre = dot(first_ref[...], first_weight_ref[:, behind], 1, 0) + ebias_ref[:, columns]
        hidden, slope = gelu_pair(pre)
        hidden = hidden.astype(BF16)
        hidden_ref[:, columns] = hidden
        slope_ref[:, columns] = slope.astype(BF16)
        mixed_ref[...] += dot(hidden, reduce_ref[columns, :], 1, 0)

    hat, scale = normal(mixed_ref[...])
    layer_ref[...] = (hat * sgain + sshift).astype(BF16)
    mixed_ref[...] = hat
    cotangent_ref[...] = cot_ref[...].astype(F32)

    if cont_tiles:

        @pl.when(at < cont_tiles)
        def _():
            student_bias, query, pool_bias, class_bias = (head_ref[i : i + 1, :] for i in range(4))
            lane = lax.broadcasted_iota(jnp.int32, (lanes, lanes), 0) // (lanes // POOL_HEADS)
            same = jnp.where(
                lane == lax.broadcasted_iota(jnp.int32, (lanes, lanes), 1) // (lanes // POOL_HEADS),
                1.0,
                0.0,
            )
            scale = (lanes // POOL_HEADS) ** (-0.5)
            kind = lax.broadcasted_iota(jnp.int32, (1, lanes), 1)

            def eight(row):
                pad = lax.broadcasted_iota(jnp.int32, (8, lanes), 0) == 0
                return jnp.where(pad, jnp.broadcast_to(row, (8, lanes)), 0.0)

            @pl.loop(0, count // length)
            def _(c):
                rows = pl.ds(pl.multiple_of(c * length, length), length)
                layer = layer_ref[rows, :]
                student = dot(layer, student_ref[...], 1, 0) + student_bias
                scores = exact(student * query, same, 1, 0) * scale
                weights = jnp.exp(scores - jnp.max(scores, axis=0, keepdims=True))
                weights = weights / total_of(weights)
                pooled = total_of(weights * student)
                hidden = jnp.tanh(exact(eight(pooled), pool_ref[...], 1, 0)[0:1] + pool_bias)
                logits = exact(eight(hidden), class_ref[...], 1, 0)[0:1] + class_bias
                which = at * (count // length) + c
                logits_ref[pl.ds(which, 1), :] = logits
                logits = jnp.where(kind < classes, logits, NEGATIVE)
                chance = jnp.exp(logits - jnp.max(logits, axis=1, keepdims=True))
                chance = chance / jnp.sum(chance, axis=1, keepdims=True)
                d_logits = chance - jnp.where(kind == label_ref[which], 1.0, 0.0)
                d_hidden = exact(eight(d_logits), class_ref[...], 1, 1)[0:1]
                d_sum = d_hidden * (1.0 - hidden * hidden)
                d_pooled = exact(eight(d_sum), pool_ref[...], 1, 1)[0:1]
                d_weights = exact(student * d_pooled, same, 1, 0)
                d_scores = weights * (d_weights - total_of(weights * d_weights)) * scale
                d_student = weights * d_pooled + d_scores * query
                d_low = d_student.astype(BF16)
                cotangent_ref[rows, :] += dot(d_low, student_ref[...], 1, 1)
                small_ref[:width, :] += dot(layer, d_low, 0, 0)
                small_ref[width : width + lanes, :] += exact(eight(pooled), eight(d_sum), 0, 0)
                small_ref[width + lanes : width + 2 * lanes, :] += exact(
                    eight(hidden), eight(d_logits), 0, 0
                )
                start = width + 2 * lanes
                small_ref[start : start + 1, :] += total_of(d_student)
                small_ref[start + 1 : start + 2, :] += total_of(d_scores * student)
                small_ref[start + 2 : start + 3, :] += d_sum
                small_ref[start + 3 : start + 4, :] += d_logits

    cotangent = cotangent_ref[...]
    hat = mixed_ref[...]
    add_vector(4, total_of(cotangent * hat))
    add_vector(5, total_of(cotangent))
    d_mixed = normal_back(cotangent, hat, scale, sgain)
    add_vector(3, total_of(d_mixed))
    dmixed_ref[...] = d_mixed.astype(BF16)
    cotangent_ref[...] = d_mixed

    @pl.loop(0, inner // chunk)
    def _(c):
        columns = pl.ds(pl.multiple_of(c * chunk, chunk), chunk)
        behind = pl.ds(pl.multiple_of(width + c * chunk, chunk), chunk)
        d_pre = dot(dmixed_ref[...], reduce_ref[columns, :], 1, 1) * slope_ref[
            :, columns
        ].astype(F32)
        expand_sum_ref[:, columns] += jnp.sum(d_pre.reshape(-1, 8, chunk), axis=0)
        d_pre = d_pre.astype(BF16)
        dpre_ref[:, columns] = d_pre
        cotangent_ref[...] += dot(d_pre, first_weight_ref[:, behind], 1, 1)

    d_first = cotangent_ref[...]
    hat = hat_ref[...]
    add_vector(1, total_of(d_first * hat))
    add_vector(2, total_of(d_first))
    d_inner = normal_back(d_first, hat, first_scale, fgain)
    add_vector(0, total_of(d_inner))
    dinner_ref[...] = d_inner
    low = d_inner.astype(BF16)
    dinner_low_ref[...] = low
    dcontext_ref[...] = dot(low, first_weight_ref[:, :width], 1, 1).astype(BF16)

    @pl.when(at == pl.num_programs(0) - 1)
    def _():
        start = vectors_at + 6 * (width // lanes)
        for i in range(inner // lanes):
            small_ref[start + i : start + i + 1, :] = total_of(
                expand_sum_ref[:, i * lanes : (i + 1) * lanes]
            )


def dense(labels, rows, context, cotangents, weights, start, count, tile, cont_tiles, length):
    first_weight, reduce_full, vectors, ebias, student, head, pool, classify, classes = weights
    width, inner = rows.shape[1], reduce_full.shape[0]
    lanes = student.shape[1]
    first = start // tile
    small_rows = width + 2 * lanes + 4 + (6 * width + inner) // lanes
    small_rows += -small_rows % 8

    def row(size, behind=0):
        return pl.BlockSpec((tile, size), lambda t: (behind + t, 0))

    def whole(array):
        return pl.BlockSpec(array.shape, lambda t: (0, 0), pipeline_mode=pl.Buffered(1))

    def kept(shape):
        return pl.BlockSpec(shape, lambda t: (0, 0))

    conts = labels.shape[0]
    low, high = BF16, F32
    outs = [
        (width, low), None, (width, low), (inner, low), (width, low), (inner, low), (width, high),
        (width, low), (width, low),
    ]
    fixed = [whole(w) for w in (first_weight, reduce_full, vectors, ebias, student, head, pool, classify)]
    weight_cells = first_weight.size + reduce_full.size
    return pl.pallas_call(
        functools.partial(dense_kernel, cont_tiles, length, classes),
        grid=(count // tile,),
        in_specs=[pl.BlockSpec(memory_space=pltpu.SMEM), row(width, first), row(width, first)]
        + [row(width, first)]
        + fixed,
        out_specs=[row(o[0]) if o else kept((conts, lanes)) for o in outs]
        + [kept((small_rows, lanes)), kept((8, inner))],
        out_shape=[
            jax.ShapeDtypeStruct((count, o[0]) if o else (conts, lanes), o[1] if o else F32)
            for o in outs
        ]
        + [
            jax.ShapeDtypeStruct((small_rows, lanes), F32),
            jax.ShapeDtypeStruct((8, inner), F32),
        ],
        scratch_shapes=[
            pltpu.VMEM((tile, width), F32),
            pltpu.VMEM((tile, width), F32),
            pltpu.VMEM((tile, inner), BF16),
            pltpu.VMEM((tile, width), F32),
        ],
        compiler_params=pltpu.CompilerParams(vmem_limit_bytes=VMEM_LIMIT),
        cost_estimate=pl.CostEstimate(
            flops=4 * count * weight_cells,
            bytes_accessed=2 * weight_cells + 20 * count * (width + inner) // 4,
            transcendentals=2 * count * inner,
        ),
        name="dense",
    )(
        labels, rows, context, cotangents, first_weight, reduce_full, vectors, ebias, student, head,
        pool, classify,
    )


def rows_back_kernel(d_inner_ref, dq_ref, dkv_ref, joint_ref, out_ref):
    width = dq_ref.shape[1]
    out_ref[...] = (
        d_inner_ref[...]
        + dot(dq_ref[...], joint_ref[:, :width], 1, 1)
        + dot(dkv_ref[...], joint_ref[:, width : 3 * width], 1, 1)
    )


def rows_back(d_inner, d_queries, d_kv, joint, start, count, tile):
    width = d_inner.shape[1]
    first = start // tile
    return pl.pallas_call(
        rows_back_kernel,
        grid=(count // tile,),
        in_specs=[
            pl.BlockSpec((tile, width), lambda t: (first + t, 0)),
            pl.BlockSpec((tile, width), lambda t: (first + t, 0)),
            pl.BlockSpec((tile, 2 * width), lambda t: (t, 0)),
            pl.BlockSpec(joint.shape, lambda t: (0, 0), pipeline_mode=pl.Buffered(1)),
        ],
        out_specs=pl.BlockSpec((tile, width), lambda t: (t, 0)),
        out_shape=jax.ShapeDtypeStruct((count, width), F32),
        compiler_params=pltpu.CompilerParams(vmem_limit_bytes=VMEM_LIMIT),
        cost_estimate=pl.CostEstimate(flops=count, bytes_accessed=count, transcendentals=0),
        name="rows_back",
    )(d_inner, d_queries, d_kv, joint)


def bits_of(axis):
    size = lax.axis_size(axis)
    return [(axis, 1 << b) for b in reversed(range(size.bit_length() - 1))]


def across(array, axis, bit):
    return lax.ppermute(array, axis, [(i, i ^ bit) for i in range(lax.axis_size(axis))])


def bit_set(axis, bit):
    return (lax.axis_index(axis) // bit) % 2


def gather_bits(shard, order, dims):
    held = shard.reshape((1,) * len(dims) + shard.shape)
    for axis, bit in order:
        dim = dims.index((axis, bit))
        other = across(held, axis, bit)
        held = jnp.where(
            bit_set(axis, bit) == 0,
            jnp.concatenate([held, other], dim),
            jnp.concatenate([other, held], dim),
        )
    return held


def gather_relative(shard, axis):
    bits = bits_of(axis)
    held = shard.reshape((1,) * len(bits) + shard.shape)
    for dim, (_, bit) in enumerate(bits):
        held = jnp.concatenate([held, across(held, axis, bit)], dim)
    return held.reshape((-1,) + shard.shape[1:])


class Halves:
    def __init__(self, blocks):
        self.shape = blocks.shape[1:]
        self.bits = bits_of("seq")
        self.held = blocks
        self.split()

    def split(self):
        both = self.held.reshape((-1, 2) + self.shape)
        self.keep, self.give = both[:, 0], both[:, 1]

    def send(self):
        self.other = across(self.give, *self.bits.pop())

    def take(self):
        self.held = (self.keep.astype(F32) + self.other.astype(F32)).astype(BF16)
        if not self.bits:
            self.held = self.held.reshape(self.shape)
            return False
        self.split()
        return True

    def waiting(self):
        return self.give if self.bits else self.held

    def tied(self, value):
        if self.bits:
            self.give = value
        else:
            self.held = value


class Spread:
    def __init__(self, blocks):
        self.held, self.sent = blocks, False

    def send(self):
        self.other, self.sent = lax.all_to_all(self.held, BOTH, 0, 0), True

    def take(self):
        self.held = jnp.sum(self.other.astype(F32), 0)
        return False

    def waiting(self):
        return self.held

    def tied(self, value):
        self.held = value


class Sum:
    def __init__(self, value, order):
        self.held, self.order = value.astype(BF16), list(order)

    def send(self):
        axis, bit = self.order.pop(0)
        self.other = across(self.held, axis, bit)

    def take(self):
        self.held = self.held.astype(F32) + self.other.astype(F32)
        if self.order:
            self.held = self.held.astype(BF16)
        return bool(self.order)

    def waiting(self):
        return self.held

    def tied(self, value):
        self.held = value


class Exchanges:
    def __init__(self):
        self.live = []

    def add(self, chain):
        self.live.append((chain, True))
        return chain

    def step(self, value):
        going, flat = [], []
        for chain, new in self.live:
            if new or chain.take():
                going.append(chain)
        if value is not None:
            chains = [chain for chain, _ in self.live]
            value, flat = lax.optimization_barrier((value, [c.waiting() for c in chains]))
            for chain, tied in zip(chains, flat):
                chain.tied(tied)
        self.live = [(chain, False) for chain in going]
        for chain in going:
            chain.send()
        return value

    def finish(self):
        while self.live:
            self.step(None)


def local(
    prompt_in,
    cont_in,
    prompt_cot,
    cont_cot,
    labels,
    joint_weight,
    query_bias,
    value_bias,
    output_weight,
    output_bias,
    first_gain,
    first_shift,
    expand_weight,
    expand_bias,
    reduce_weight,
    reduce_bias,
    second_gain,
    second_shift,
    student_weight,
    student_bias,
    pool_query,
    pool_weight,
    pool_bias,
    class_weight,
    class_bias,
):
    prompt_rows = prompt_in[0]
    share, width = prompt_rows.shape
    _, conts, length, _ = cont_in.shape
    cont_count = conts * length
    part = joint_weight.shape[0]
    devices = width // part
    hidden_width = expand_weight.shape[1]
    fold = hidden_width // width
    tile = min(share, length)
    grp_bits, seq_bits = bits_of("grp"), bits_of("seq")
    dims = grp_bits + seq_bits
    gather_orders = (
        grp_bits + seq_bits,
        grp_bits[:-1] + seq_bits[:-1] + grp_bits[-1:] + seq_bits[-1:],
    )

    pairs = width // PAIR
    groups = [3, 2, 1] if pairs == 6 else [pairs]
    joint_low = joint_weight.astype(BF16)
    vectors = [
        query_bias,
        value_bias,
        output_bias,
        first_gain,
        first_shift,
        reduce_bias,
        second_gain,
        second_shift,
    ]
    beside = jnp.concatenate([v[None] for v in vectors], 0).astype(BF16).T
    beside = jnp.concatenate([beside, expand_bias.astype(BF16).reshape(part, fold)], 1)
    lanes = student_weight.shape[1]
    own_joint = [joint_low[:, :width]]
    for h in range(pairs):
        own_joint += [joint_low[:, (s * pairs + h) * PAIR :][:, :PAIR] for s in (1, 2)]
    own_joint.append(jnp.pad(beside, ((0, 0), (0, lanes - beside.shape[1]))))
    own_joint = jnp.concatenate(own_joint, 1)
    half = (3 * width // 2 + lanes) // PAIR * PAIR
    joint_all = jnp.concatenate(
        [
            gather_bits(piece, order, dims).reshape(width, -1)
            for piece, order in zip((own_joint[:, :half], own_joint[:, half:]), gather_orders)
        ],
        1,
    )
    joint_full = joint_all[:, : 3 * width]
    flat = joint_all[:, 3 * width :].astype(F32)
    by_vector = flat[:, : len(vectors)].T
    qbias, vbias = by_vector[0], by_vector[1]
    ebias = flat[:, 8 : 8 + fold].reshape(hidden_width)
    prompt_all = gather_relative(prompt_rows, "seq")
    far = prompt_all.shape[0]
    out_expand = lax.all_gather(
        jnp.concatenate([output_weight, expand_weight], 1).astype(BF16), BOTH, axis=0, tiled=True
    )
    reduce_full = lax.all_gather(reduce_weight.astype(BF16), BOTH, axis=0, tiled=True)

    cont_rows = cont_in[0].reshape(cont_count, width)
    rows = jnp.concatenate([cont_rows, prompt_rows], 0)
    key_rows = jnp.concatenate([prompt_all, cont_rows], 0)
    rows_t, prompt_t = turned(rows), turned(prompt_all)
    queries = (dot(rows, joint_full[:, :width], 1, 0) + qbias).astype(BF16) * HEAD_DIM ** (-0.5)
    kv_bias = jnp.pad(vbias.reshape(pairs, 1, PAIR), ((0, 0), (1, 0), (0, 0))).reshape(-1)
    keys_values = (dot(key_rows, joint_full[:, width:], 1, 0) + kv_bias).astype(BF16)

    context, prompt_inv, prompt_exp = attention_forward(
        queries, keys_values, far, share, cont_count, tile, None
    )
    context, cont_inv, cont_exp = attention_forward(
        queries, keys_values, far, cont_count, 0, length, context
    )

    classes = class_weight.shape[1]
    head = jnp.concatenate(
        [student_bias, pool_query, pool_bias, jnp.pad(class_bias, (0, lanes - classes))]
    ).reshape(4, lanes)
    weights = (
        out_expand,
        reduce_full,
        by_vector,
        ebias[None],
        student_weight.astype(BF16),
        jnp.pad(head, ((0, 4), (0, 0))),
        pool_weight,
        jnp.pad(class_weight, ((0, 0), (0, lanes - classes))),
        classes,
    )
    cotangents = jnp.concatenate([cont_cot[0].reshape(cont_count, width), prompt_cot[0]], 0)
    cont_tile = min(2 * length, cont_count)
    if cont_tile == share:
        results = dense(
            labels[0], rows, context, cotangents, weights, 0, rows.shape[0], share,
            cont_count // cont_tile, length,
        )
    else:
        of_conts = dense(
            labels[0], rows, context, cotangents, weights, 0, cont_count, cont_tile,
            cont_count // cont_tile, length,
        )
        of_prompt = dense(
            labels[0], rows, context, cotangents, weights, cont_count, share, share, 0, length
        )
        results = [
            of_conts[i]
            if i == 1
            else of_conts[i] + of_prompt[i]
            if i > 8
            else jnp.concatenate([of_conts[i], of_prompt[i]], 0)
            for i in range(len(of_conts))
        ]
    layer_low, logits, first_low, hidden, d_mixed_low, d_pre_low, d_inner = results[:7]
    d_inner_low, d_context, small = results[7:10]
    logits = logits[:, :classes]
    cont_layer = layer_low[:cont_count]
    exchanges = Exchanges()
    small = exchanges.add(Sum(small, dims))
    d_reduce_weight = dot(hidden, d_mixed_low, 0, 0).astype(BF16)
    d_expand_weight = dot(first_low, d_pre_low, 0, 0).astype(BF16)
    d_output_weight = dot(context, d_inner_low, 0, 0).astype(BF16)

    blocks = [d_output_weight.reshape(devices, part, width)]
    blocks += [
        d_expand_weight[:, i * width : (i + 1) * width].reshape(devices, part, width)
        for i in range(fold)
    ]
    blocks += [d_reduce_weight.reshape(devices, -1, width)]
    blocks, d_context, d_inner, rows_t, prompt_t = lax.optimization_barrier(
        (jnp.concatenate(blocks, 1), d_context, d_inner, rows_t, prompt_t)
    )
    early = lax.psum_scatter(blocks, BOTH, scatter_dimension=0, tiled=True)

    into, owns, joint_parts, sums = (), [], [], []
    h0 = 0
    for nh in groups:
        d_context = exchanges.step(d_context)
        *into, dkv_far, d_joint, sum_rows = attention_backward(
            queries, keys_values, far, context, d_context, (cont_inv, cont_exp),
            (prompt_inv, prompt_exp), rows_t, prompt_t, h0, nh, into,
        )
        if h0 + nh == pairs:
            sums.append(sum_rows[:, 0])
            sums = jnp.concatenate(sums, 0)
            sums = [sums[:, i * PAIR : (i + 1) * PAIR].reshape(devices, 1, part) for i in (0, 2)]
            sums = jnp.concatenate(sums, 1).astype(BF16)
            sums = jnp.pad(sums, ((0, 0), (0, 6), (0, 3 * nh * PAIR - part)))
            d_joint = jnp.concatenate([d_joint.reshape(devices, part, -1), sums], 1)
        else:
            sums.append(sum_rows[:, 0])
        owns.append(exchanges.add(Halves(dkv_far.reshape(-1, share, dkv_far.shape[1]))))
        joint_parts.append(exchanges.add(Spread(d_joint.reshape(devices, -1, 3 * nh * PAIR))))
        h0 += nh
    d_queries, d_kv = into
    early, d_queries = exchanges.step((early, d_queries))
    d_cont_rows = rows_back(d_inner, d_queries, d_kv, joint_all, 0, cont_count, cont_tile)
    exchanges.finish()
    early = early[0].astype(F32)
    output_grad = early[:part]
    expand_grad = jnp.concatenate(
        [early[part * (1 + i) : part * (2 + i)] for i in range(fold)], 1
    )
    reduce_grad = early[part * (1 + fold) :]
    parts = [p.held for p in joint_parts]
    joint_grad = jnp.concatenate(
        [p[:part].reshape(part, nh, 3, PAIR) for p, nh in zip(parts, groups)], 1
    )
    joint_grad = joint_grad.transpose(0, 2, 1, 3).reshape(part, 3 * width)

    d_own = jnp.concatenate([o.held.astype(BF16) for o in owns], 1)
    d_prompt_rows = rows_back(d_inner, d_queries, d_own, joint_all, cont_count, share, share)

    small = small.held
    index = lax.axis_index(BOTH)
    at = width + lanes
    head_grads = (
        small[:width],
        small[at + lanes],
        small[at + lanes + 1],
        small[width:at],
        small[at + lanes + 2],
        small[at : at + lanes, :classes],
        small[at + lanes + 3, :classes],
    )
    at += lanes + 4
    vector_grads = []
    for row in (part, part + 1):
        vector_grads.append(parts[-1][row, :part])
    for size in [width] * 6 + [hidden_width]:
        vector = small[at : at + size // lanes].reshape(size)
        own = size // devices
        vector_grads.append(lax.dynamic_slice(vector, (index * own,), (own,)))
        at += size // lanes
    (g_qbias, g_vbias, g_obias, g_fgain, g_fshift, g_rbias, g_sgain, g_sshift, g_ebias) = vector_grads
    return (
        layer_low[cont_count:][None],
        cont_layer.reshape(1, conts, length, width),
        logits[None],
        d_prompt_rows[None],
        d_cont_rows.reshape(1, conts, length, width),
        joint_grad,
        g_qbias,
        g_vbias,
        output_grad,
        g_obias,
        g_fgain,
        g_fshift,
        expand_grad,
        g_ebias,
        reduce_grad,
        g_rbias,
        g_sgain,
        g_sshift,
    ) + head_grads


def solution(mesh):
    placed = (
        P("grp", "seq", None),
        P("grp", "seq", None, None),
        P("grp", "seq", None),
        P("grp", "seq", None, None),
        P("grp", "seq"),
        P(("grp", "seq"), None),
        P(("grp", "seq")),
        P(("grp", "seq")),
        P(("grp", "seq"), None),
        P(("grp", "seq")),
        P(("grp", "seq")),
        P(("grp", "seq")),
        P(("grp", "seq"), None),
        P(("grp", "seq")),
        P(("grp", "seq"), None),
        P(("grp", "seq")),
        P(("grp", "seq")),
        P(("grp", "seq")),
        P(),
        P(),
        P(),
        P(),
        P(),
        P(),
        P(),
    )
    return jax.shard_map(
        local,
        mesh=mesh,
        in_specs=placed,
        out_specs=(
            P("grp", "seq", None),
            P("grp", "seq", None, None),
            P("grp", "seq", None),
            P("grp", "seq", None),
            P("grp", "seq", None, None),
            P(("grp", "seq"), None),
            P(("grp", "seq")),
            P(("grp", "seq")),
            P(("grp", "seq"), None),
            P(("grp", "seq")),
            P(("grp", "seq")),
            P(("grp", "seq")),
            P(("grp", "seq"), None),
            P(("grp", "seq")),
            P(("grp", "seq"), None),
            P(("grp", "seq")),
            P(("grp", "seq")),
            P(("grp", "seq")),
            P(),
            P(),
            P(),
            P(),
            P(),
            P(),
            P(),
        ),
        check_vma=False,
    )
```

time: 597 us -> 534 us (0.89)
  matrix products: 156 us -> 38 us
  Pallas kernels: 196 us -> 300 us
  waiting for transfers between devices: 76.5 us -> 47.1 us
  other arithmetic: 56.7 us -> 43.4 us
  local copies, waits for them, and re-layouts: 51.3 us -> 43.1 us
    dot_general x34 -> x5, matrix products: 152 us -> 38 us  [dot(): lax.dot_general(left, right, (((left_dim,), (right_dim,)), ((), ())), pre...]
    pallas_call x6 -> x8, Pallas kernels: 122 us -> 226 us  [the longest x3 131 us: attention_backward(): pl.pallas_call(functools.partial(attention_backward_kernel, cont_tiles),...]
    ppermute x38 -> x23, waiting for transfers between devices: 76.5 us -> 47 us  [across(): lax.ppermute(array, axis, [(i, i ^ bit) for i in range(lax.axis_size(axis...]
    reduce_sum x14 -> x3, other arithmetic: 17.1 us -> 1.81 us  [take(): self.held = jnp.sum(self.other.astype(F32), 0)]
    all_to_all x0 -> x3, starting transfers between devices: none -> 12.5 us  [send(): self.other, self.sent = (lax.all_to_all(self.held, BOTH, 0, 0), True)]
    ppermute x38 -> x23, starting transfers between devices: 36.4 us -> 24.7 us  [across(): lax.ppermute(array, axis, [(i, i ^ bit) for i in range(lax.axis_size(axis...]
    squeeze x0 -> x8, local copies, waits for them, and re-layouts: none -> 10.9 us  [the longest x6 9.68 us: split(): self.keep, self.give = (both[:, 0], both[:, 1])]
    concatenate x5 -> x7, other arithmetic: 2.07 us -> 11.9 us  [the longest x1 3.85 us: local(): jnp.concatenate([gather_bits(piece, order, dims).reshape(width, -1) for p...]
  transfers between devices with their start and end apart: 41 -> 29, of which waited for: 16 -> 8; matrix products, arithmetic and copies ran while one was open for 23% -> 17% of each run, Pallas kernels for 33% -> 43%
where the time goes in v3:
time: 534 us; the launch traced here: 524 us
  Pallas kernels  300 us (56%)
  waiting for transfers between devices  47.1 us (9%)
  other arithmetic  43.4 us (8%)
  local copies, waits for them, and re-layouts  43.1 us (8%)
  matrix products  38 us (7%)
  starting transfers between devices  37.4 us (7%)
  between operations  15.2 us (3%)
    pallas_call x3, Pallas kernels, attention_backward(): pl.pallas_call(functools.partial(attention_backward_kernel, cont_tiles),...  131 us
    pallas_call x2, Pallas kernels, attention_forward(): pl.pallas_call(functools.partial(attention_forward_kernel, near), grid=(p...  74 us
    pallas_call x1, Pallas kernels, dense(): pl.pallas_call(functools.partial(dense_kernel, cont_tiles, length, classe...  72.8 us
    ppermute x23, waiting for transfers between devices, across(): lax.ppermute(array, axis, [(i, i ^ bit) for i in range(lax.axis_size(axis...  47 us
    dot_general x5, matrix products, dot(): lax.dot_general(left, right, (((left_dim,), (right_dim,)), ((), ())), pre...  38 us
    ppermute x23, starting transfers between devices, across(): lax.ppermute(array, axis, [(i, i ^ bit) for i in range(lax.axis_size(axis...  24.7 us
    pallas_call x2, Pallas kernels, rows_back(): pl.pallas_call(rows_back_kernel, grid=(count // tile,), in_specs=[pl.Bloc...  15.2 us
    all_to_all x3, starting transfers between devices, send(): self.other, self.sent = (lax.all_to_all(self.held, BOTH, 0, 0), True)  12.5 us
  transfers between devices with their start and end apart: 29, of which 8 were waited for; matrix products, arithmetic and copies ran while one was open for 17% of the time, Pallas kernels for 43%

profile of v3, /device:TPU:0, one launch (start us, length us, event | category | flops | bytes accessed | tf_op | source)
XLA Modules:
  0.0 523.8 jit_solution(9049813820839317929)
XLA Ops:
  12.9 4.1 collective-permute-start
  30.1 4.0 collective-permute-done.6
  38.2 5.3 %collective-permute-done.7 = bf16[2,2,1,1,1,24,1152]{6,5,4,3,2,1,0:T(8,128)(2,1)S(1)} collective-permute-done((bf16[2,2,1,1,1,24,1152]{6,5,4,3,2,1,0:T(8,128)(2,1)S(1)}, bf16[2,2,1,1,1,24,1152]{6,5,4,3,2,1,0:T(8,128)(2,1)S(1)}, u32[]{:S(2)}, u32[]{:S(2)}) %collective-permute-start.7) | collective-permute-done | bytes 221216 | tf_op jit(solution)/shard_map/ppermute | solution.py:619
  45.1 3.4 collective-permute-done.2
  48.7 8.8 %collective-permute-done.8 = bf16[2,2,1,2,1,24,1152]{6,5,4,3,2,1,0:T(8,128)(2,1)S(1)} collective-permute-done((bf16[2,2,1,2,1,24,1152]{6,5,4,3,2,1,0:T(8,128)(2,1)S(1)}, bf16[2,2,1,2,1,24,1152]{6,5,4,3,2,1,0:T(8,128)(2,1)S(1)}, u32[]{:S(2)}, u32[]{:S(2)}) %collective-permute-start.8) | collective-permute-done | bytes 442400 | tf_op jit(solution)/shard_map/ppermute | solution.py:619
  71.3 3.4 pad_maximum_fusion.1
  74.8 3.8 turn.3.refs_15_
  78.5 12.9 %add_convert_fusion.refs_1_.refs_2_.refs_3_.refs_4_.refs_0_ = bf16[3072,1536]{1,0:T(8,128)(2,1)} fusion(f32[1536]{0:T(1024)S(1)} %add.115, bf16[1024,768]{1,0:T(8,128)(2,1)S(1)} %bitcast.275, bf16[2048,768]{1,0:T(8,128)(2,1)S(1)} %bitcast.248, bf16[768,1280]{1,0:T(8,128)(2,1)} %bitcast.253, bf16[768,1152]{1,0:T(8,128)(2,1)S(1)} %bitcast.250), kind=kOutput, calls=%fused_computation | convolution fusion | flops 7271350272 | bytes 17897472 | tf_op jit(solution)/shard_map/dot_general | solution.py:26
  91.4 25.8 %attention_forward.2 = (bf16[1536,768]{1,0:T(8,128)(2,1)}, f32[6,2,2,256]{3,2,1,0:T(2,128)}, bf16[6,2,2,2048,256]{4,3,2,1,0:T(8,128)(2,1)}) custom-call(bf16[1536,768]{1,0:T(8,128)(2,1)} %fusion.4.refs_0_.refs_4_.refs_9_, bf16[3072,1536]{1,0:T(8,128)(2,1)} %add_convert_fusion.refs_1_.refs_2_.refs_3_.refs_4_.refs_0_, ...), custom_call_target="tpu_custom_call" | custom-call | flops 3221225472 | bytes 25165824 | tf_op jit(solution)/shard_map/attention_forward/pallas_call | solution.py:154
  117.2 48.2 %attention_forward.3 = (bf16[1536,768]{1,0:T(8,128)(2,1)}, f32[6,4,2,256]{3,2,1,0:T(2,128)}, bf16[6,4,2,2304,256]{4,3,2,1,0:T(8,128)(2,1)}) custom-call(bf16[1536,768]{1,0:T(8,128)(2,1)} %fusion.4.refs_0_.refs_4_.refs_9_, bf16[3072,1536]{1,0:T(8,128)(2,1)} %add_convert_fusion.refs_1_.refs_2_.refs_3_.refs_4_.refs_0_, ...), custom_call_target="tpu_custom_call", output_to_operand_aliasing={{0}: (5, {})} | custom-call | flops 7247757312 | bytes 56623104 | tf_op jit(solution)/shard_map/attention_forward/pallas_call | solution.py:154
  165.4 72.8 %dense.1 = (bf16[1536,768]{1,0:T(8,128)(2,1)}, f32[4,128]{1,0:T(4,128)}, bf16[1536,768]{1,0:T(8,128)(2,1)}, bf16[1536,3072]{1,0:T(8,128)(2,1)}, bf16[1536,768]{1...) custom-call(s32[4]{0:T(128)} %bitcast.297, ...), custom_call_target="tpu_custom_call" | custom-call | flops 32614907904 | bytes 40108032 | tf_op jit(solution)/shard_map/dense/pallas_call | solution.py:549
  238.2 11.4 %convolution_convert_fusion.1 = bf16[768,3072]{1,0:T(8,128)(2,1)S(1)} fusion(bf16[1536,768]{1,0:T(8,128)(2,1)} %get-tuple-element.86, bf16[1536,3072]{1,0:T(8,128)(2,1)} %get-tuple-element.87), kind=kOutput, calls=%fused_computation.2 | convolution fusion | flops 7250116608 | bytes 16515072 | tf_op jit(solution)/shard_map/dot_general | solution.py:26
  256.2 8.2 %convolution_convert_fusion = bf16[3072,768]{1,0:T(8,128)(2,1)S(1)} fusion(bf16[1536,3072]{1,0:T(8,128)(2,1)S(1)} %bitcast.299, bf16[1536,768]{1,0:T(8,128)(2,1)S(1)} %copy-done.41), kind=kOutput, calls=%fused_computation.1 | convolution fusion | flops 7250116608 | bytes 16515072 | tf_op jit(solution)/shard_map/dot_general | solution.py:26
  275.0 62.7 %attention_backward.3 = (bf16[1536,768]{1,0:T(8,128)(2,1)}, bf16[1024,1536]{1,0:T(8,128)(2,1)}, bf16[2048,768]{1,0:T(8,128)(2,1)}, bf16[768,1152]{1,0:T(8,128)(2,1)}, f32[3,8,384]{2,1,0:T(8,128)}) custom-call(bf16[3072,1536]{1,0:T(8,128)(2,1)} %add_convert_fusion.refs_1_.refs_2_.refs_3_.refs_4_.refs_0_, ...), custom_call_target="tpu_custom_call" | custom-call | flops 20447232 | bytes 1277952 | tf_op jit(solution)/shard_map/attention_backward/pallas_call | solution.py:294
  344.4 3.8 pad_maximum_fusion.joint_ref
  352.9 43.8 %attention_backward.4 = (bf16[1536,768]{1,0:T(8,128)(2,1)}, bf16[1024,1536]{1,0:T(8,128)(2,1)}, bf16[2048,512]{1,0:T(8,128)(2,1)}, bf16[768,768]{1,0:T(8,128)(2,1)}, f32[2,8,384]{2,1,0:T(8,128)}) custom-call(bf16[3072,1536]{1,0:T(8,128)(2,1)} %add_convert_fusion.refs_1_.refs_2_.refs_3_.refs_4_.refs_0_, ...), custom_call_target="tpu_custom_call", output_to_operand_aliasing={{0}: (16, {}), {1}: (17, {})} | custom-call | flops 13631488 | bytes 851968 | tf_op jit(solution)/shard_map/attention_backward/pallas_call | solution.py:294
  403.4 5.0 all-to-all-start.1
  409.8 24.3 %attention_backward.5 = (bf16[1536,768]{1,0:T(8,128)(2,1)}, bf16[1024,1536]{1,0:T(8,128)(2,1)}, bf16[2048,256]{1,0:T(8,128)(2,1)}, bf16[768,384]{1,0:T(8,128)(2,1)}, f32[1,8,384]{2,1,0:T(8,128)}) custom-call(bf16[3072,1536]{1,0:T(8,128)(2,1)} %add_convert_fusion.refs_1_.refs_2_.refs_3_.refs_4_.refs_0_, ...), custom_call_target="tpu_custom_call", output_to_operand_aliasing={{0}: (16, {}), {1}: (17, {})} | custom-call | flops 6815744 | bytes 425984 | tf_op jit(solution)/shard_map/attention_backward/pallas_call | solution.py:294
  443.5 3.5 collective-permute-done.15
  447.8 9.7 %collective-permute-done.16 = bf16[1,512,768]{2,1,0:T(8,128)(2,1)} collective-permute-done((bf16[1,512,768]{2,1,0:T(8,128)(2,1)}, bf16[1,512,768]{2,1,0:T(8,128)(2,1)}, u32[]{:S(2)}, u32[]{:S(2)}) %collective-permute-start.16) | collective-permute-done | bytes 786464 | tf_op jit(solution)/shard_map/ppermute | solution.py:619
  465.1 4.6 all-to-all-start.2
  472.5 8.8 %rows_back.3 = f32[1024,768]{1,0:T(8,128)} custom-call(f32[1536,768]{1,0:T(8,128)} %get-tuple-element.92.d_inner_ref, bf16[1536,768]{1,0:T(8,128)(2,1)} %get-tuple-element.127.dq_ref, bf16[1024,1536]{1,0:T(8,128)(2,1)} %get-tuple-element.131.dkv_ref, bf16[768,2432]{1,0:T(8,128)(2,1)} %pad_maximum_fusion.joint_ref), custom_call_target="tpu_custom_call" | custom-call | flops 1024 | bytes 1024 | tf_op jit(solution)/shard_map/rows_back/pallas_call | solution.py:596
  487.3 10.9 %collective-permute-done.18 = bf16[1,512,512]{2,1,0:T(8,128)(2,1)S(1)} collective-permute-done((bf16[1,512,512]{2,1,0:T(8,128)(2,1)}, bf16[1,512,512]{2,1,0:T(8,128)(2,1)S(1)}, u32[]{:S(2)}, u32[]{:S(2)}) %collective-permute-start.18) | collective-permute-done | bytes 524320 | tf_op jit(solution)/shard_map/ppermute | solution.py:619
  508.8 6.5 %rows_back.2 = f32[512,768]{1,0:T(8,128)} custom-call(f32[1536,768]{1,0:T(8,128)} %get-tuple-element.92.d_inner_ref, bf16[1536,768]{1,0:T(8,128)(2,1)} %get-tuple-element.127.dq_ref, bf16[512,1536]{1,0:T(8,128)(2,1)} %pad_maximum_fusion.5.dkv_ref, bf16[768,2432]{1,0:T(8,128)(2,1)} %pad_maximum_fusion.joint_ref), custom_call_target="tpu_custom_call" | custom-call | flops 512 | bytes 512 | tf_op jit(solution)/shard_map/rows_back/pallas_call | solution.py:596
  (274 shorter events, 112.8 us)
Async XLA Ops:
  7.3 158.1 %all-gather.5.cloned.1.call-start = ((), (), s32[]{:S(2)}) async-start(), calls=%async_computation.5 | async-start | bytes 4866048 | tf_op jit(solution)/shard_map/all_gather | solution.py:828
  9.1 156.3 %all-gather.3.cloned.1.call-start = ((), (), s32[]{:S(2)}) async-start(), calls=%async_computation.4 | async-start | bytes 6082560 | tf_op jit(solution)/shard_map/all_gather | solution.py:825
  11.7 450.3 %reduce-scatter.2.cloned.1.call-start = ((), (), s32[]{:S(2)}) async-start(), calls=%async_computation.6 | async-start | bytes 10948608 | tf_op jit(solution)/shard_map/reduce_scatter | solution.py:902
  12.9 16.6 %collective-permute-start = (bf16[1,1,1,1,1,24,1280]{6,5,4,3,2,1,0:T(8,128)(2,1)S(1)}, bf16[1,1,1,1,1,24,1280]{6,5,4,3,2,1,0:T(8,128)(2,1)S(1)}, u32[]{:S(2)}, u32[]{:S(2)}) collective-permute-start(bf16[1,1,1,1,1,24,1280]{6,5,4,3,2,1,0:T(8,128)(2,1)S(1)} %get-tuple-element.245), channel_id=1, source_target_pairs={{0,16},{4,20},{8,24},{12,28},{16,0},{20,4},{24,8},{28,12},{1,17},{... | collective-permute-start | bytes 184328 | tf_op jit(solution)/shard_map/ppermute | solution.py:619
  17.5 10.3 %collective-permute-start.5 = (bf16[1,1,1,1,1,24,1152]{6,5,4,3,2,1,0:T(8,128)(2,1)S(1)}, bf16[1,1,1,1,1,24,1152]{6,5,4,3,2,1,0:T(8,128)(2,1)S(1)}, u32[]{:S(2)}, u32[]{:S(2)}) collective-permute-start(bf16[1,1,1,1,1,24,1152]{6,5,4,3,2,1,0:T(8,128)(2,1)S(1)} %bitcast.287), channel_id=1, source_target_pairs={{0,16},{4,20},{8,24},{12,28},{16,0},{20,4},{24,8},{28,12},{1,17},{... | collective-permute-start | bytes 165896 | tf_op jit(solution)/shard_map/ppermute | solution.py:619
  17.6 43.4 %collective-permute-start.10 = (bf16[1,1,512,768]{3,2,1,0:T(8,128)(2,1)S(1)}, bf16[1,1,512,768]{3,2,1,0:T(8,128)(2,1)S(1)}, u32[]{:S(2)}, u32[]{:S(2)}) collective-permute-start(bf16[1,1,512,768]{3,2,1,0:T(8,128)(2,1)S(1)} %bitcast.255), channel_id=1, source_target_pairs={{0,2},{1,3},{2,0},{3,1},{4,6},{5,7},{6,4},{7,5},{8,10},{9,11},{10,... | collective-permute-start | bytes 2359304 | tf_op jit(solution)/shard_map/ppermute | solution.py:619
  34.1 9.4 %collective-permute-start.7 = (bf16[2,2,1,1,1,24,1152]{6,5,4,3,2,1,0:T(8,128)(2,1)S(1)}, bf16[2,2,1,1,1,24,1152]{6,5,4,3,2,1,0:T(8,128)(2,1)S(1)}, u32[]{:S(2)}, u32[]{:S(2)}) collective-permute-start(bf16[2,2,1,1,1,24,1152]{6,5,4,3,2,1,0:T(8,128)(2,1)S(1)} %maximum_select_fusion.11), channel_id=1, source_target_pairs={{0,2},{1,3},{2,0},{3,1},{4,6},{5,7},{6,4},{7,5},{8,10},{9,11},{10,... | collective-permute-start | bytes 663560 | tf_op jit(solution)/shard_map/ppermute | solution.py:619
  36.6 12.0 %collective-permute-start.2 = (bf16[2,2,1,1,1,24,1280]{6,5,4,3,2,1,0:T(8,128)(2,1)S(1)}, bf16[2,2,1,1,1,24,1280]{6,5,4,3,2,1,0:T(8,128)(2,1)S(1)}, u32[]{:S(2)}, u32[]{:S(2)}) collective-permute-start(bf16[2,2,1,1,1,24,1280]{6,5,4,3,2,1,0:T(8,128)(2,1)S(1)} %maximum_select_fusion.9), channel_id=1, source_target_pairs={{0,4},{4,0},{8,12},{12,8},{16,20},{20,16},{24,28},{28,24},{1,5},{5... | collective-permute-start | bytes 737288 | tf_op jit(solution)/shard_map/ppermute | solution.py:619
  43.7 13.8 %collective-permute-start.8 = (bf16[2,2,1,2,1,24,1152]{6,5,4,3,2,1,0:T(8,128)(2,1)S(1)}, bf16[2,2,1,2,1,24,1152]{6,5,4,3,2,1,0:T(8,128)(2,1)S(1)}, u32[]{:S(2)}, u32[]{:S(2)}) collective-permute-start(bf16[2,2,1,2,1,24,1152]{6,5,4,3,2,1,0:T(8,128)(2,1)S(1)} %maximum_select_fusion.7), channel_id=1, source_target_pairs={{0,4},{4,0},{8,12},{12,8},{16,20},{20,16},{24,28},{28,24},{1,5},{5... | collective-permute-start | bytes 1327112 | tf_op jit(solution)/shard_map/ppermute | solution.py:619
  48.6 10.8 %collective-permute-start.3 = (bf16[2,2,2,1,1,24,1280]{6,5,4,3,2,1,0:T(8,128)(2,1)S(1)}, bf16[2,2,2,1,1,24,1280]{6,5,4,3,2,1,0:T(8,128)(2,1)S(1)}, u32[]{:S(2)}, u32[]{:S(2)}) collective-permute-start(bf16[2,2,2,1,1,24,1280]{6,5,4,3,2,1,0:T(8,128)(2,1)S(1)} %maximum_select_fusion.5), channel_id=1, source_target_pairs={{0,2},{1,3},{2,0},{3,1},{4,6},{5,7},{6,4},{7,5},{8,10},{9,11},{10,... | collective-permute-start | bytes 1474568 | tf_op jit(solution)/shard_map/ppermute | solution.py:619
  272.6 67.8 %collective-permute-start.12 = (bf16[1088,128]{1,0:T(8,128)(2,1)S(1)}, bf16[1088,128]{1,0:T(8,128)(2,1)S(1)}, u32[]{:S(2)}, u32[]{:S(2)}) collective-permute-start(bf16[1088,128]{1,0:T(8,128)(2,1)S(1)} %convert_element_type.209), channel_id=1, source_target_pairs={{0,16},{4,20},{8,24},{12,28},{16,0},{20,4},{24,8},{28,12},{1,17},{... | collective-permute-start | bytes 835592 | tf_op jit(solution)/shard_map/ppermute | solution.py:619
  341.2 61.4 %all-to-all-start = ((bf16[32,24,1152]{2,1,0:T(8,128)(2,1)}), bf16[32,24,1152]{2,1,0:T(8,128)(2,1)S(1)}, u32[]{:S(2)}, u32[]{:S(2)}) async-start(bf16[32,24,1152]{2,1,0:T(8,128)(2,1)} %bitcast.270), calls=%async_computation.1 | async-start | bytes 3538944 | tf_op jit(solution)/shard_map/all_to_all | solution.py:684
  344.1 55.7 %collective-permute-start.14 = (bf16[2,512,768]{2,1,0:T(8,128)(2,1)}, bf16[2,512,768]{2,1,0:T(8,128)(2,1)}, u32[]{:S(2)}, u32[]{:S(2)}) collective-permute-start(bf16[2,512,768]{2,1,0:T(8,128)(2,1)} %slice_bitcast_fusion.1), channel_id=1, source_target_pairs={{0,1},{1,0},{2,3},{3,2},{4,5},{5,4},{6,7},{7,6},{8,9},{9,8},{10,11... | collective-permute-start | bytes 4718600 | tf_op jit(solution)/shard_map/ppermute | solution.py:619
  351.2 47.8 %collective-permute-start.13 = (bf16[1088,128]{1,0:T(8,128)(2,1)S(1)}, bf16[1088,128]{1,0:T(8,128)(2,1)S(1)}, u32[]{:S(2)}, u32[]{:S(2)}) collective-permute-start(bf16[1088,128]{1,0:T(8,128)(2,1)S(1)} %copy-done.17), channel_id=1, source_target_pairs={{0,8},{4,12},{8,0},{12,4},{16,24},{20,28},{24,16},{28,20},{1,9},{5... | collective-permute-start | bytes 835592 | tf_op jit(solution)/shard_map/ppermute | solution.py:619
  403.4 57.8 %all-to-all-start.1 = ((bf16[32,24,768]{2,1,0:T(8,128)(2,1)}), bf16[32,24,768]{2,1,0:T(8,128)(2,1)S(1)}, u32[]{:S(2)}, u32[]{:S(2)}) async-start(bf16[32,24,768]{2,1,0:T(8,128)(2,1)} %bitcast.277), calls=%async_computation.2 | async-start | bytes 2359296 | tf_op jit(solution)/shard_map/all_to_all | solution.py:684
  435.1 23.8 %collective-permute-start.17 = (bf16[2,512,512]{2,1,0:T(8,128)(2,1)}, bf16[2,512,512]{2,1,0:T(8,128)(2,1)}, u32[]{:S(2)}, u32[]{:S(2)}) collective-permute-start(bf16[2,512,512]{2,1,0:T(8,128)(2,1)} %slice_bitcast_fusion.3), channel_id=1, source_target_pairs={{0,1},{1,0},{2,3},{3,2},{4,5},{5,4},{6,7},{7,6},{8,9},{9,8},{10,11... | collective-permute-start | bytes 3145736 | tf_op jit(solution)/shard_map/ppermute | solution.py:619
  435.5 22.0 %collective-permute-start.16 = (bf16[1,512,768]{2,1,0:T(8,128)(2,1)}, bf16[1,512,768]{2,1,0:T(8,128)(2,1)}, u32[]{:S(2)}, u32[]{:S(2)}) collective-permute-start(bf16[1,512,768]{2,1,0:T(8,128)(2,1)} %slice_bitcast_fusion.5), channel_id=1, source_target_pairs={{0,2},{1,3},{2,0},{3,1},{4,6},{5,7},{6,4},{7,5},{8,10},{9,11},{10,... | collective-permute-start | bytes 2359304 | tf_op jit(solution)/shard_map/ppermute | solution.py:619
  437.2 9.8 %collective-permute-start.15 = (bf16[1088,128]{1,0:T(8,128)(2,1)S(1)}, bf16[1088,128]{1,0:T(8,128)(2,1)S(1)}, u32[]{:S(2)}, u32[]{:S(2)}) collective-permute-start(bf16[1088,128]{1,0:T(8,128)(2,1)S(1)} %copy-done.16), channel_id=1, source_target_pairs={{0,4},{4,0},{8,12},{12,8},{16,20},{20,16},{24,28},{28,24},{1,5},{5... | collective-permute-start | bytes 835592 | tf_op jit(solution)/shard_map/ppermute | solution.py:619
  462.1 21.6 %collective-permute-start.21 = (bf16[1088,128]{1,0:T(8,128)(2,1)}, bf16[1088,128]{1,0:T(8,128)(2,1)}, u32[]{:S(2)}, u32[]{:S(2)}) collective-permute-start(bf16[1088,128]{1,0:T(8,128)(2,1)} %add_convert_fusion.3), channel_id=1, source_target_pairs={{0,2},{1,3},{2,0},{3,1},{4,6},{5,7},{6,4},{7,5},{8,10},{9,11},{10,... | collective-permute-start | bytes 835592 | tf_op jit(solution)/shard_map/ppermute | solution.py:619
  465.1 50.1 %all-to-all-start.2 = ((bf16[32,32,384]{2,1,0:T(8,128)(2,1)}), bf16[32,32,384]{2,1,0:T(8,128)(2,1)S(1)}, u32[]{:S(2)}, u32[]{:S(2)}) async-start(bf16[32,32,384]{2,1,0:T(8,128)(2,1)} %fusion.15), calls=%async_computation.3 | async-start | bytes 1572864 | tf_op jit(solution)/shard_map/all_to_all | solution.py:684
  469.7 15.2 %collective-permute-start.19 = (bf16[2,512,256]{2,1,0:T(8,128)(2,1)}, bf16[2,512,256]{2,1,0:T(8,128)(2,1)}, u32[]{:S(2)}, u32[]{:S(2)}) collective-permute-start(bf16[2,512,256]{2,1,0:T(8,128)(2,1)} %slice_bitcast_fusion.9), channel_id=1, source_target_pairs={{0,1},{1,0},{2,3},{3,2},{4,5},{5,4},{6,7},{7,6},{8,9},{9,8},{10,11... | collective-permute-start | bytes 1572872 | tf_op jit(solution)/shard_map/ppermute | solution.py:619
  481.9 16.3 %collective-permute-start.18 = (bf16[1,512,512]{2,1,0:T(8,128)(2,1)}, bf16[1,512,512]{2,1,0:T(8,128)(2,1)S(1)}, u32[]{:S(2)}, u32[]{:S(2)}) collective-permute-start(bf16[1,512,512]{2,1,0:T(8,128)(2,1)} %slice_bitcast_fusion.10), channel_id=1, source_target_pairs={{0,2},{1,3},{2,0},{3,1},{4,6},{5,7},{6,4},{7,5},{8,10},{9,11},{10,... | collective-permute-start | bytes 1572872 | tf_op jit(solution)/shard_map/ppermute | solution.py:619
  484.8 14.4 %collective-permute-start.22 = (bf16[1088,128]{1,0:T(8,128)(2,1)S(1)}, bf16[1088,128]{1,0:T(8,128)(2,1)S(1)}, u32[]{:S(2)}, u32[]{:S(2)}) collective-permute-start(bf16[1088,128]{1,0:T(8,128)(2,1)S(1)} %add_convert_fusion.2), channel_id=1, source_target_pairs={{0,1},{1,0},{2,3},{3,2},{4,5},{5,4},{6,7},{7,6},{8,9},{9,8},{10,11... | collective-permute-start | bytes 835592 | tf_op jit(solution)/shard_map/ppermute | solution.py:619
  487.0 18.8 %collective-permute-start.20 = (bf16[1,512,256]{2,1,0:T(8,128)(2,1)}, bf16[1,512,256]{2,1,0:T(8,128)(2,1)}, u32[]{:S(2)}, u32[]{:S(2)}) collective-permute-start(bf16[1,512,256]{2,1,0:T(8,128)(2,1)} %slice_bitcast_fusion.13), channel_id=1, source_target_pairs={{0,2},{1,3},{2,0},{3,1},{4,6},{5,7},{6,4},{7,5},{8,10},{9,11},{10,... | collective-permute-start | bytes 786440 | tf_op jit(solution)/shard_map/ppermute | solution.py:619
  (50 other events, 457.8 us)
Sparse Core Ops, SparseCore 0:
  11.6 68.0 all-gather.4
  83.2 66.5 all-gather.2
  271.7 165.6 reduce-scatter.1

commit v4 on v3

--- a/solution.py
+++ b/solution.py
@@ -340,6 +340,9 @@
         out_specs=pl.BlockSpec((width, tile), lambda t: (0, t)),
         out_shape=jax.ShapeDtypeStruct((width, count), rows.dtype),
         compiler_params=pltpu.CompilerParams(vmem_limit_bytes=VMEM_LIMIT),
+        cost_estimate=pl.CostEstimate(
+            flops=0, bytes_accessed=4 * count * width, transcendentals=0
+        ),
         name="turn",
     )(rows)
 
@@ -723,19 +726,42 @@
         self.live.append((chain, True))
         return chain
 
-    def step(self, value):
+    def step(self, value, last=False):
         going, flat = [], []
         for chain, new in self.live:
             if new or chain.take():
                 going.append(chain)
         if value is not None:
-            chains = [chain for chain, _ in self.live]
+            chains = [chain for chain, new in self.live if new or not last]
             value, flat = lax.optimization_barrier((value, [c.waiting() for c in chains]))
             for chain, tied in zip(chains, flat):
                 chain.tied(tied)
+        if last:
+            for chain, new in self.live:
+                if new:
+                    chain.send()
+            chains = [chain for chain, new in self.live if not new]
+            value, flat = lax.optimization_barrier((value, [c.waiting() for c in chains]))
+            for chain, tied in zip(chains, flat):
+                chain.tied(tied)
+            for chain in going:
+                if chain in chains:
+                    chain.send()
+            self.live = [(chain, False) for chain in going]
+            return value
         self.live = [(chain, False) for chain in going]
         for chain in going:
             chain.send()
+        return value
+
+    def move(self, chain, value):
+        more = chain.take()
+        value, tied = lax.optimization_barrier((value, chain.waiting()))
+        chain.tied(tied)
+        if more:
+            chain.send()
+        else:
+            self.live = [entry for entry in self.live if entry[0] is not chain]
         return value
 
     def finish(self):
@@ -815,6 +841,7 @@
         ],
         1,
     )
+    joint_all = lax.optimization_barrier(joint_all)
     joint_full = joint_all[:, : 3 * width]
     flat = joint_all[:, 3 * width :].astype(F32)
     by_vector = flat[:, : len(vectors)].T
@@ -922,7 +949,8 @@
         joint_parts.append(exchanges.add(Spread(d_joint.reshape(devices, -1, 3 * nh * PAIR))))
         h0 += nh
     d_queries, d_kv = into
-    early, d_queries = exchanges.step((early, d_queries))
+    early, d_queries = exchanges.step((early, d_queries), True)
+    d_queries = exchanges.move(owns[-1], d_queries)
     d_cont_rows = rows_back(d_inner, d_queries, d_kv, joint_all, 0, cont_count, cont_tile)
     exchanges.finish()
     early = early[0].astype(F32)

time: 534 us -> 515 us (0.964); the launches traced: 524 us -> 511 us
  waiting for transfers between devices: 47.1 us -> 33.4 us
  other arithmetic: 43.4 us -> 35.4 us
    ppermute x23, waiting for transfers between devices: 47 us -> 33.2 us  [across(): lax.ppermute(array, axis, [(i, i ^ bit) for i in range(lax.axis_size(axis...]
    unnamed x109 -> x97, local copies, waits for them, and re-layouts: 10.9 us -> 13.5 us
  transfers between devices with their start and end apart: 29 -> 29, of which waited for: 8 -> 7; matrix products, arithmetic and copies ran while one was open for 17% -> 16% of each run, Pallas kernels for 43% -> 44%
where the time goes in v4:
time: 515 us; the launch traced here: 511 us
  Pallas kernels  300 us (58%)
  local copies, waits for them, and re-layouts  48.4 us (9%)
  starting transfers between devices  39.7 us (8%)
  matrix products  38.8 us (8%)
  other arithmetic  35.4 us (7%)
  waiting for transfers between devices  33.4 us (6%)
  between operations  15 us (3%)
    pallas_call x3, Pallas kernels, attention_backward(): pl.pallas_call(functools.partial(attention_backward_kernel, cont_tiles),...  131 us
    pallas_call x2, Pallas kernels, attention_forward(): pl.pallas_call(functools.partial(attention_forward_kernel, near), grid=(p...  74 us
    pallas_call x1, Pallas kernels, dense(): pl.pallas_call(functools.partial(dense_kernel, cont_tiles, length, classe...  72.7 us
    dot_general x5, matrix products, dot(): lax.dot_general(left, right, (((left_dim,), (right_dim,)), ((), ())), pre...  38.8 us
    ppermute x23, waiting for transfers between devices, across(): lax.ppermute(array, axis, [(i, i ^ bit) for i in range(lax.axis_size(axis...  33.2 us
    ppermute x23, starting transfers between devices, across(): lax.ppermute(array, axis, [(i, i ^ bit) for i in range(lax.axis_size(axis...  26.9 us
    pallas_call x2, Pallas kernels, rows_back(): pl.pallas_call(rows_back_kernel, grid=(count // tile,), in_specs=[pl.Bloc...  15.2 us
    unnamed x97, local copies, waits for them, and re-layouts  13.5 us
  transfers between devices with their start and end apart: 29, of which 7 were waited for; matrix products, arithmetic and copies ran while one was open for 16% of the time, Pallas kernels for 44%

profile of v4, /device:TPU:0, one launch (start us, length us, event | category | flops | bytes accessed | tf_op | source)
XLA Modules:
  0.0 510.6 jit_solution(9481942629136982119)
XLA Ops:
  13.0 4.1 collective-permute-start
  25.1 4.4 collective-permute-done.6
  33.5 9.2 %collective-permute-done.7 = bf16[2,2,1,1,1,24,1152]{6,5,4,3,2,1,0:T(8,128)(2,1)S(1)} collective-permute-done((bf16[2,2,1,1,1,24,1152]{6,5,4,3,2,1,0:T(8,128)(2,1)S(1)}, bf16[2,2,1,1,1,24,1152]{6,5,4,3,2,1,0:T(8,128)(2,1)S(1)}, u32[]{:S(2)}, u32[]{:S(2)}) %collective-permute-start.7) | collective-permute-done | bytes 221216 | tf_op jit(solution)/shard_map/ppermute | solution.py:622
  46.7 10.1 %collective-permute-done.8 = bf16[2,2,1,2,1,24,1152]{6,5,4,3,2,1,0:T(8,128)(2,1)S(1)} collective-permute-done((bf16[2,2,1,2,1,24,1152]{6,5,4,3,2,1,0:T(8,128)(2,1)S(1)}, bf16[2,2,1,2,1,24,1152]{6,5,4,3,2,1,0:T(8,128)(2,1)S(1)}, u32[]{:S(2)}, u32[]{:S(2)}) %collective-permute-start.8) | collective-permute-done | bytes 442400 | tf_op jit(solution)/shard_map/ppermute | solution.py:622
  59.3 3.4 turn.2.refs_14_
  74.3 5.1 %fusion.4.refs_0_.refs_4_.refs_9_ = bf16[1536,768]{1,0:T(8,128)(2,1)} fusion(f32[768]{0:T(1024)S(1)} %get-tuple-element.221, bf16[768,2432]{1,0:T(8,128)(2,1)} %copy-done.1, bf16[512,768]{1,0:T(8,128)(2,1)S(1)} %bitcast.254, bf16[1024,768]{1,0:T(8,128)(2,1)} %bitcast.268), kind=kOutput, calls=%fused_computation.12 | convolution fusion | flops 1820196864 | bytes 5901312 | tf_op jit(solution)/shard_map/dot_general | solution.py:26
  79.4 3.4 pad_maximum_fusion.1
  82.8 3.8 turn.3.refs_15_
  87.5 12.0 %add_convert_fusion.refs_1_.refs_2_.refs_3_.refs_4_.refs_0_ = bf16[3072,1536]{1,0:T(8,128)(2,1)} fusion(f32[1536]{0:T(1024)S(1)} %add.115, bf16[1024,768]{1,0:T(8,128)(2,1)S(1)} %bitcast.270, bf16[2048,768]{1,0:T(8,128)(2,1)} %bitcast.248, bf16[768,2432]{1,0:T(8,128)(2,1)S(1)} %copy-done.2), kind=kOutput, calls=%fused_computation | convolution fusion | flops 7266631680 | bytes 16523264 | tf_op jit(solution)/shard_map/dot_general | solution.py:26
  99.4 25.6 %attention_forward.2 = (bf16[1536,768]{1,0:T(8,128)(2,1)}, f32[6,2,2,256]{3,2,1,0:T(2,128)}, bf16[6,2,2,2048,256]{4,3,2,1,0:T(8,128)(2,1)}) custom-call(bf16[1536,768]{1,0:T(8,128)(2,1)} %fusion.4.refs_0_.refs_4_.refs_9_, bf16[3072,1536]{1,0:T(8,128)(2,1)} %add_convert_fusion.refs_1_.refs_2_.refs_3_.refs_4_.refs_0_, ...), custom_call_target="tpu_custom_call" | custom-call | flops 3221225472 | bytes 25165824 | tf_op jit(solution)/shard_map/attention_forward/pallas_call | solution.py:154
  125.0 48.4 %attention_forward.3 = (bf16[1536,768]{1,0:T(8,128)(2,1)}, f32[6,4,2,256]{3,2,1,0:T(2,128)}, bf16[6,4,2,2304,256]{4,3,2,1,0:T(8,128)(2,1)}) custom-call(bf16[1536,768]{1,0:T(8,128)(2,1)} %fusion.4.refs_0_.refs_4_.refs_9_, bf16[3072,1536]{1,0:T(8,128)(2,1)} %add_convert_fusion.refs_1_.refs_2_.refs_3_.refs_4_.refs_0_, ...), custom_call_target="tpu_custom_call", output_to_operand_aliasing={{0}: (5, {})} | custom-call | flops 7247757312 | bytes 56623104 | tf_op jit(solution)/shard_map/attention_forward/pallas_call | solution.py:154
  173.4 72.7 %dense.1 = (bf16[1536,768]{1,0:T(8,128)(2,1)}, f32[4,128]{1,0:T(4,128)}, bf16[1536,768]{1,0:T(8,128)(2,1)}, bf16[1536,3072]{1,0:T(8,128)(2,1)}, bf16[1536,768]{1...) custom-call(s32[4]{0:T(128)} %bitcast.292, ...), custom_call_target="tpu_custom_call" | custom-call | flops 32614907904 | bytes 40108032 | tf_op jit(solution)/shard_map/dense/pallas_call | solution.py:552
  246.2 11.5 %convolution_convert_fusion.1 = bf16[768,3072]{1,0:T(8,128)(2,1)S(1)} fusion(bf16[1536,768]{1,0:T(8,128)(2,1)} %get-tuple-element.90, bf16[1536,3072]{1,0:T(8,128)(2,1)} %get-tuple-element.91), kind=kOutput, calls=%fused_computation.2 | convolution fusion | flops 7250116608 | bytes 16515072 | tf_op jit(solution)/shard_map/dot_general | solution.py:26
  264.2 8.2 %convolution_convert_fusion = bf16[3072,768]{1,0:T(8,128)(2,1)S(1)} fusion(bf16[1536,3072]{1,0:T(8,128)(2,1)S(1)} %bitcast.294, bf16[1536,768]{1,0:T(8,128)(2,1)S(1)} %copy-done.35), kind=kOutput, calls=%fused_computation.1 | convolution fusion | flops 7250116608 | bytes 16515072 | tf_op jit(solution)/shard_map/dot_general | solution.py:26
  283.0 62.7 %attention_backward.3 = (bf16[1536,768]{1,0:T(8,128)(2,1)}, bf16[1024,1536]{1,0:T(8,128)(2,1)}, bf16[2048,768]{1,0:T(8,128)(2,1)}, bf16[768,1152]{1,0:T(8,128)(2,1)}, f32[3,8,384]{2,1,0:T(8,128)}) custom-call(bf16[3072,1536]{1,0:T(8,128)(2,1)} %add_convert_fusion.refs_1_.refs_2_.refs_3_.refs_4_.refs_0_, ...), custom_call_target="tpu_custom_call" | custom-call | flops 20447232 | bytes 1277952 | tf_op jit(solution)/shard_map/attention_backward/pallas_call | solution.py:294
  348.0 2.9 all-to-all-start
  352.1 2.7 slice.269
  358.6 43.7 %attention_backward.4 = (bf16[1536,768]{1,0:T(8,128)(2,1)}, bf16[1024,1536]{1,0:T(8,128)(2,1)}, bf16[2048,512]{1,0:T(8,128)(2,1)}, bf16[768,768]{1,0:T(8,128)(2,1)}, f32[2,8,384]{2,1,0:T(8,128)}) custom-call(bf16[3072,1536]{1,0:T(8,128)(2,1)} %add_convert_fusion.refs_1_.refs_2_.refs_3_.refs_4_.refs_0_, ...), custom_call_target="tpu_custom_call", output_to_operand_aliasing={{0}: (16, {}), {1}: (17, {})} | custom-call | flops 13631488 | bytes 851968 | tf_op jit(solution)/shard_map/attention_backward/pallas_call | solution.py:294
  408.4 4.9 all-to-all-start.1
  418.1 24.3 %attention_backward.5 = (bf16[1536,768]{1,0:T(8,128)(2,1)}, bf16[1024,1536]{1,0:T(8,128)(2,1)}, bf16[2048,256]{1,0:T(8,128)(2,1)}, bf16[768,384]{1,0:T(8,128)(2,1)}, f32[1,8,384]{2,1,0:T(8,128)}) custom-call(bf16[3072,1536]{1,0:T(8,128)(2,1)} %add_convert_fusion.refs_1_.refs_2_.refs_3_.refs_4_.refs_0_, ...), custom_call_target="tpu_custom_call", output_to_operand_aliasing={{0}: (16, {}), {1}: (17, {})} | custom-call | flops 6815744 | bytes 425984 | tf_op jit(solution)/shard_map/attention_backward/pallas_call | solution.py:294
  456.0 5.0 all-to-all-start.2
  467.8 8.7 %rows_back.3 = f32[1024,768]{1,0:T(8,128)} custom-call(f32[1536,768]{1,0:T(8,128)} %get-tuple-element.96.d_inner_ref, bf16[1536,768]{1,0:T(8,128)(2,1)} %get-tuple-element.135.dq_ref, bf16[1024,1536]{1,0:T(8,128)(2,1)} %get-tuple-element.139.dkv_ref, bf16[768,2432]{1,0:T(8,128)(2,1)} %copy-done.1), custom_call_target="tpu_custom_call" | custom-call | flops 1024 | bytes 1024 | tf_op jit(solution)/shard_map/rows_back/pallas_call | solution.py:599
  476.5 7.6 %collective-permute-done.19 = bf16[1,512,512]{2,1,0:T(8,128)(2,1)} collective-permute-done((bf16[1,512,512]{2,1,0:T(8,128)(2,1)}, bf16[1,512,512]{2,1,0:T(8,128)(2,1)}, u32[]{:S(2)}, u32[]{:S(2)}) %collective-permute-start.19) | collective-permute-done | bytes 524320 | tf_op jit(solution)/shard_map/ppermute | solution.py:622
  495.7 6.5 %rows_back.2 = f32[512,768]{1,0:T(8,128)} custom-call(f32[1536,768]{1,0:T(8,128)} %get-tuple-element.96.d_inner_ref, bf16[1536,768]{1,0:T(8,128)(2,1)} %get-tuple-element.135.dq_ref, bf16[512,1536]{1,0:T(8,128)(2,1)} %pad_maximum_fusion.5.dkv_ref, bf16[768,2432]{1,0:T(8,128)(2,1)} %copy-done.1), custom_call_target="tpu_custom_call" | custom-call | flops 512 | bytes 512 | tf_op jit(solution)/shard_map/rows_back/pallas_call | solution.py:599
  (262 shorter events, 104.7 us)
Async XLA Ops:
  7.4 166.1 %all-gather.5.cloned.1.call-start = ((), (), s32[]{:S(2)}) async-start(), calls=%async_computation.5 | async-start | bytes 4866048 | tf_op jit(solution)/shard_map/all_gather | solution.py:855
  9.2 164.3 %all-gather.3.cloned.1.call-start = ((), (), s32[]{:S(2)}) async-start(), calls=%async_computation.4 | async-start | bytes 6082560 | tf_op jit(solution)/shard_map/all_gather | solution.py:852
  11.8 441.9 %reduce-scatter.2.cloned.1.call-start = ((), (), s32[]{:S(2)}) async-start(), calls=%async_computation.6 | async-start | bytes 10948608 | tf_op jit(solution)/shard_map/reduce_scatter | solution.py:929
  13.0 11.4 %collective-permute-start = (bf16[1,1,1,1,1,24,1280]{6,5,4,3,2,1,0:T(8,128)(2,1)S(1)}, bf16[1,1,1,1,1,24,1280]{6,5,4,3,2,1,0:T(8,128)(2,1)S(1)}, u32[]{:S(2)}, u32[]{:S(2)}) collective-permute-start(bf16[1,1,1,1,1,24,1280]{6,5,4,3,2,1,0:T(8,128)(2,1)S(1)} %get-tuple-element.253), channel_id=1, source_target_pairs={{0,16},{4,20},{8,24},{12,28},{16,0},{20,4},{24,8},{28,12},{1,17},{... | collective-permute-start | bytes 184328 | tf_op jit(solution)/shard_map/ppermute | solution.py:622
  17.6 46.6 %collective-permute-start.10 = (bf16[1,1,512,768]{3,2,1,0:T(8,128)(2,1)S(1)}, bf16[1,1,512,768]{3,2,1,0:T(8,128)(2,1)S(1)}, u32[]{:S(2)}, u32[]{:S(2)}) collective-permute-start(bf16[1,1,512,768]{3,2,1,0:T(8,128)(2,1)S(1)} %bitcast.251), channel_id=1, source_target_pairs={{0,2},{1,3},{2,0},{3,1},{4,6},{5,7},{6,4},{7,5},{8,10},{9,11},{10,... | collective-permute-start | bytes 2359304 | tf_op jit(solution)/shard_map/ppermute | solution.py:622
  29.6 13.1 %collective-permute-start.7 = (bf16[2,2,1,1,1,24,1152]{6,5,4,3,2,1,0:T(8,128)(2,1)S(1)}, bf16[2,2,1,1,1,24,1152]{6,5,4,3,2,1,0:T(8,128)(2,1)S(1)}, u32[]{:S(2)}, u32[]{:S(2)}) collective-permute-start(bf16[2,2,1,1,1,24,1152]{6,5,4,3,2,1,0:T(8,128)(2,1)S(1)} %maximum_select_fusion.11), channel_id=1, source_target_pairs={{0,2},{1,3},{2,0},{3,1},{4,6},{5,7},{6,4},{7,5},{8,10},{9,11},{10,... | collective-permute-start | bytes 663560 | tf_op jit(solution)/shard_map/ppermute | solution.py:622
  31.9 12.4 %collective-permute-start.2 = (bf16[2,2,1,1,1,24,1280]{6,5,4,3,2,1,0:T(8,128)(2,1)S(1)}, bf16[2,2,1,1,1,24,1280]{6,5,4,3,2,1,0:T(8,128)(2,1)S(1)}, u32[]{:S(2)}, u32[]{:S(2)}) collective-permute-start(bf16[2,2,1,1,1,24,1280]{6,5,4,3,2,1,0:T(8,128)(2,1)S(1)} %maximum_select_fusion.9), channel_id=1, source_target_pairs={{0,4},{4,0},{8,12},{12,8},{16,20},{20,16},{24,28},{28,24},{1,5},{5... | collective-permute-start | bytes 737288 | tf_op jit(solution)/shard_map/ppermute | solution.py:622
  42.8 14.0 %collective-permute-start.8 = (bf16[2,2,1,2,1,24,1152]{6,5,4,3,2,1,0:T(8,128)(2,1)S(1)}, bf16[2,2,1,2,1,24,1152]{6,5,4,3,2,1,0:T(8,128)(2,1)S(1)}, u32[]{:S(2)}, u32[]{:S(2)}) collective-permute-start(bf16[2,2,1,2,1,24,1152]{6,5,4,3,2,1,0:T(8,128)(2,1)S(1)} %maximum_select_fusion.7), channel_id=1, source_target_pairs={{0,4},{4,0},{8,12},{12,8},{16,20},{20,16},{24,28},{28,24},{1,5},{5... | collective-permute-start | bytes 1327112 | tf_op jit(solution)/shard_map/ppermute | solution.py:622
  44.3 12.7 %collective-permute-start.3 = (bf16[2,2,2,1,1,24,1280]{6,5,4,3,2,1,0:T(8,128)(2,1)S(1)}, bf16[2,2,2,1,1,24,1280]{6,5,4,3,2,1,0:T(8,128)(2,1)S(1)}, u32[]{:S(2)}, u32[]{:S(2)}) collective-permute-start(bf16[2,2,2,1,1,24,1280]{6,5,4,3,2,1,0:T(8,128)(2,1)S(1)} %maximum_select_fusion.5), channel_id=1, source_target_pairs={{0,2},{1,3},{2,0},{3,1},{4,6},{5,7},{6,4},{7,5},{8,10},{9,11},{10,... | collective-permute-start | bytes 1474568 | tf_op jit(solution)/shard_map/ppermute | solution.py:622
  57.1 9.2 %collective-permute-start.4 = (bf16[2,2,2,2,1,24,1280]{6,5,4,3,2,1,0:T(8,128)(2,1)S(1)}, bf16[2,2,2,2,1,24,1280]{6,5,4,3,2,1,0:T(8,128)(2,1)}, u32[]{:S(2)}, u32[]{:S(2)}) collective-permute-start(bf16[2,2,2,2,1,24,1280]{6,5,4,3,2,1,0:T(8,128)(2,1)S(1)} %maximum_select_fusion.2), channel_id=1, source_target_pairs={{0,1},{1,0},{2,3},{3,2},{4,5},{5,4},{6,7},{7,6},{8,9},{9,8},{10,11... | collective-permute-start | bytes 2949128 | tf_op jit(solution)/shard_map/ppermute | solution.py:622
  64.4 15.0 %collective-permute-start.11 = (bf16[2,1,512,768]{3,2,1,0:T(8,128)(2,1)S(1)}, bf16[2,1,512,768]{3,2,1,0:T(8,128)(2,1)}, u32[]{:S(2)}, u32[]{:S(2)}) collective-permute-start(bf16[2,1,512,768]{3,2,1,0:T(8,128)(2,1)S(1)} %pad_maximum_fusion.4), channel_id=1, source_target_pairs={{0,1},{1,0},{2,3},{3,2},{4,5},{5,4},{6,7},{7,6},{8,9},{9,8},{10,11... | collective-permute-start | bytes 4718600 | tf_op jit(solution)/shard_map/ppermute | solution.py:622
  280.5 66.7 %collective-permute-start.12 = (bf16[1088,128]{1,0:T(8,128)(2,1)S(1)}, bf16[1088,128]{1,0:T(8,128)(2,1)S(1)}, u32[]{:S(2)}, u32[]{:S(2)}) collective-permute-start(bf16[1088,128]{1,0:T(8,128)(2,1)S(1)} %convert_element_type.209), channel_id=1, source_target_pairs={{0,16},{4,20},{8,24},{12,28},{16,0},{20,4},{24,8},{28,12},{1,17},{... | collective-permute-start | bytes 835592 | tf_op jit(solution)/shard_map/ppermute | solution.py:622
  348.0 60.1 %all-to-all-start = ((bf16[32,24,1152]{2,1,0:T(8,128)(2,1)}), bf16[32,24,1152]{2,1,0:T(8,128)(2,1)S(1)}, u32[]{:S(2)}, u32[]{:S(2)}) async-start(bf16[32,24,1152]{2,1,0:T(8,128)(2,1)} %bitcast.79), calls=%async_computation.1 | async-start | bytes 3538944 | tf_op jit(solution)/shard_map/all_to_all | solution.py:687
  350.9 54.4 %collective-permute-start.14 = (bf16[2,512,768]{2,1,0:T(8,128)(2,1)S(1)}, bf16[2,512,768]{2,1,0:T(8,128)(2,1)}, u32[]{:S(2)}, u32[]{:S(2)}) collective-permute-start(bf16[2,512,768]{2,1,0:T(8,128)(2,1)S(1)} %slice_bitcast_fusion.1), channel_id=1, source_target_pairs={{0,1},{1,0},{2,3},{3,2},{4,5},{5,4},{6,7},{7,6},{8,9},{9,8},{10,11... | collective-permute-start | bytes 4718600 | tf_op jit(solution)/shard_map/ppermute | solution.py:622
  356.9 47.6 %collective-permute-start.13 = (bf16[1088,128]{1,0:T(8,128)(2,1)S(1)}, bf16[1088,128]{1,0:T(8,128)(2,1)S(1)}, u32[]{:S(2)}, u32[]{:S(2)}) collective-permute-start(bf16[1088,128]{1,0:T(8,128)(2,1)S(1)} %copy-done.13), channel_id=1, source_target_pairs={{0,8},{4,12},{8,0},{12,4},{16,24},{20,28},{24,16},{28,20},{1,9},{5... | collective-permute-start | bytes 835592 | tf_op jit(solution)/shard_map/ppermute | solution.py:622
  408.4 45.1 %all-to-all-start.1 = ((bf16[32,24,768]{2,1,0:T(8,128)(2,1)}), bf16[32,24,768]{2,1,0:T(8,128)(2,1)S(1)}, u32[]{:S(2)}, u32[]{:S(2)}) async-start(bf16[32,24,768]{2,1,0:T(8,128)(2,1)} %bitcast.272), calls=%async_computation.2 | async-start | bytes 2359296 | tf_op jit(solution)/shard_map/all_to_all | solution.py:687
  414.6 36.5 %collective-permute-start.17 = (bf16[2,512,512]{2,1,0:T(8,128)(2,1)}, bf16[2,512,512]{2,1,0:T(8,128)(2,1)}, u32[]{:S(2)}, u32[]{:S(2)}) collective-permute-start(bf16[2,512,512]{2,1,0:T(8,128)(2,1)} %slice_bitcast_fusion.3), channel_id=1, source_target_pairs={{0,1},{1,0},{2,3},{3,2},{4,5},{5,4},{6,7},{7,6},{8,9},{9,8},{10,11... | collective-permute-start | bytes 3145736 | tf_op jit(solution)/shard_map/ppermute | solution.py:622
  415.0 33.9 %collective-permute-start.16 = (bf16[1,512,768]{2,1,0:T(8,128)(2,1)}, bf16[1,512,768]{2,1,0:T(8,128)(2,1)}, u32[]{:S(2)}, u32[]{:S(2)}) collective-permute-start(bf16[1,512,768]{2,1,0:T(8,128)(2,1)} %slice_bitcast_fusion.5), channel_id=1, source_target_pairs={{0,2},{1,3},{2,0},{3,1},{4,6},{5,7},{6,4},{7,5},{8,10},{9,11},{10,... | collective-permute-start | bytes 2359304 | tf_op jit(solution)/shard_map/ppermute | solution.py:622
  416.6 31.5 %collective-permute-start.15 = (bf16[1088,128]{1,0:T(8,128)(2,1)S(1)}, bf16[1088,128]{1,0:T(8,128)(2,1)S(1)}, u32[]{:S(2)}, u32[]{:S(2)}) collective-permute-start(bf16[1088,128]{1,0:T(8,128)(2,1)S(1)} %copy-done.11), channel_id=1, source_target_pairs={{0,4},{4,0},{8,12},{12,8},{16,20},{20,16},{24,28},{28,24},{1,5},{5... | collective-permute-start | bytes 835592 | tf_op jit(solution)/shard_map/ppermute | solution.py:622
  453.7 11.5 %collective-permute-start.21 = (bf16[1088,128]{1,0:T(8,128)(2,1)S(1)}, bf16[1088,128]{1,0:T(8,128)(2,1)S(1)}, u32[]{:S(2)}, u32[]{:S(2)}) collective-permute-start(bf16[1088,128]{1,0:T(8,128)(2,1)S(1)} %copy-done.12), channel_id=1, source_target_pairs={{0,2},{1,3},{2,0},{3,1},{4,6},{5,7},{6,4},{7,5},{8,10},{9,11},{10,... | collective-permute-start | bytes 835592 | tf_op jit(solution)/shard_map/ppermute | solution.py:622
  456.0 46.2 %all-to-all-start.2 = ((bf16[32,32,384]{2,1,0:T(8,128)(2,1)}), bf16[32,32,384]{2,1,0:T(8,128)(2,1)S(1)}, u32[]{:S(2)}, u32[]{:S(2)}) async-start(bf16[32,32,384]{2,1,0:T(8,128)(2,1)} %fusion.14), calls=%async_computation.3 | async-start | bytes 1572864 | tf_op jit(solution)/shard_map/all_to_all | solution.py:687
  461.4 22.8 %collective-permute-start.19 = (bf16[1,512,512]{2,1,0:T(8,128)(2,1)}, bf16[1,512,512]{2,1,0:T(8,128)(2,1)}, u32[]{:S(2)}, u32[]{:S(2)}) collective-permute-start(bf16[1,512,512]{2,1,0:T(8,128)(2,1)} %slice_bitcast_fusion.9), channel_id=1, source_target_pairs={{0,2},{1,3},{2,0},{3,1},{4,6},{5,7},{6,4},{7,5},{8,10},{9,11},{10,... | collective-permute-start | bytes 1572872 | tf_op jit(solution)/shard_map/ppermute | solution.py:622
  465.3 20.8 %collective-permute-start.22 = (bf16[1088,128]{1,0:T(8,128)(2,1)S(1)}, bf16[1088,128]{1,0:T(8,128)(2,1)S(1)}, u32[]{:S(2)}, u32[]{:S(2)}) collective-permute-start(bf16[1088,128]{1,0:T(8,128)(2,1)S(1)} %add_convert_fusion.2), channel_id=1, source_target_pairs={{0,1},{1,0},{2,3},{3,2},{4,5},{5,4},{6,7},{7,6},{8,9},{9,8},{10,11... | collective-permute-start | bytes 835592 | tf_op jit(solution)/shard_map/ppermute | solution.py:622
  467.5 25.3 %collective-permute-start.20 = (bf16[1,512,256]{2,1,0:T(8,128)(2,1)}, bf16[1,512,256]{2,1,0:T(8,128)(2,1)}, u32[]{:S(2)}, u32[]{:S(2)}) collective-permute-start(bf16[1,512,256]{2,1,0:T(8,128)(2,1)} %slice_bitcast_fusion.14), channel_id=1, source_target_pairs={{0,2},{1,3},{2,0},{3,1},{4,6},{5,7},{6,4},{7,5},{8,10},{9,11},{10,... | collective-permute-start | bytes 786440 | tf_op jit(solution)/shard_map/ppermute | solution.py:622
  (44 other events, 393.3 us)
Sparse Core Ops, SparseCore 0:
  11.7 68.9 all-gather.4
  84.2 66.5 all-gather.2
  279.6 167.8 reduce-scatter.1

commit v5 on v4

--- a/solution.py
+++ b/solution.py
@@ -613,6 +613,65 @@
     )(d_inner, d_queries, d_kv, joint)
 
 
+def reduce_grad_kernel(hidden_ref, d_ref, out_ref):
+    out_ref[...] = dot(hidden_ref[...], d_ref[...], 0, 0).reshape(out_ref.shape).astype(BF16)
+
+
+def other_grads_kernel(context_ref, d_inner_ref, first_ref, d_pre_ref, _, out_ref):
+    @pl.when(pl.program_id(0) == 0)
+    def _():
+        grad = dot(context_ref[...], d_inner_ref[...], 0, 0)
+        out_ref[...] = grad.reshape(out_ref.shape).astype(BF16)
+
+    @pl.when(pl.program_id(0) > 0)
+    def _():
+        grad = dot(first_ref[...], d_pre_ref[...], 0, 0)
+        out_ref[...] = grad.reshape(out_ref.shape).astype(BF16)
+
+
+def matrix_grads(hidden, d_mixed, context, d_inner, first, d_pre, devices):
+    total, width = d_mixed.shape
+    fold = hidden.shape[1] // width
+    part = width // devices
+    shape = jax.ShapeDtypeStruct((devices, part * (2 * fold + 1), width), BF16)
+
+    def kept():
+        return pl.BlockSpec((total, width), lambda j: (0, 0), pipeline_mode=pl.Buffered(1))
+
+    params = pltpu.CompilerParams(vmem_limit_bytes=VMEM_LIMIT)
+    grads = pl.pallas_call(
+        reduce_grad_kernel,
+        grid=(fold,),
+        in_specs=[pl.BlockSpec((total, width), lambda j: (0, j)), kept()],
+        out_specs=pl.BlockSpec((devices // fold, part * fold, width), lambda j: (j, 0, 0)),
+        out_shape=shape,
+        compiler_params=params,
+        cost_estimate=pl.CostEstimate(
+            flops=2 * total * width * width * fold, bytes_accessed=0, transcendentals=0
+        ),
+        name="reduce_grad",
+    )(hidden, d_mixed)
+    return pl.pallas_call(
+        other_grads_kernel,
+        grid=(1 + fold,),
+        in_specs=[
+            kept(),
+            kept(),
+            kept(),
+            pl.BlockSpec((total, width), lambda j: (0, jnp.maximum(j - 1, 0))),
+            pl.BlockSpec(memory_space=pl.ANY),
+        ],
+        out_specs=pl.BlockSpec((devices, part, width), lambda j: (0, fold + j, 0)),
+        out_shape=shape,
+        input_output_aliases={4: 0},
+        compiler_params=params,
+        cost_estimate=pl.CostEstimate(
+            flops=2 * total * width * width * (1 + fold), bytes_accessed=0, transcendentals=0
+        ),
+        name="other_grads",
+    )(context, d_inner, first, d_pre, grads)
+
+
 def bits_of(axis):
     size = lax.axis_size(axis)
     return [(axis, 1 << b) for b in reversed(range(size.bit_length() - 1))]
@@ -913,18 +972,22 @@
     cont_layer = layer_low[:cont_count]
     exchanges = Exchanges()
     small = exchanges.add(Sum(small, dims))
-    d_reduce_weight = dot(hidden, d_mixed_low, 0, 0).astype(BF16)
-    d_expand_weight = dot(first_low, d_pre_low, 0, 0).astype(BF16)
-    d_output_weight = dot(context, d_inner_low, 0, 0).astype(BF16)
-
-    blocks = [d_output_weight.reshape(devices, part, width)]
-    blocks += [
-        d_expand_weight[:, i * width : (i + 1) * width].reshape(devices, part, width)
-        for i in range(fold)
-    ]
-    blocks += [d_reduce_weight.reshape(devices, -1, width)]
+    if part % 8 == 0 and devices % fold == 0:
+        blocks = matrix_grads(
+            hidden, d_mixed_low, context, d_inner_low, first_low, d_pre_low, devices
+        )
+    else:
+        d_expand_weight = dot(first_low, d_pre_low, 0, 0).astype(BF16)
+        blocks = [
+            dot(hidden, d_mixed_low, 0, 0).astype(BF16).reshape(devices, -1, width),
+            dot(context, d_inner_low, 0, 0).astype(BF16).reshape(devices, part, width),
+        ] + [
+            d_expand_weight[:, i * width : (i + 1) * width].reshape(devices, part, width)
+            for i in range(fold)
+        ]
+        blocks = jnp.concatenate(blocks, 1)
     blocks, d_context, d_inner, rows_t, prompt_t = lax.optimization_barrier(
-        (jnp.concatenate(blocks, 1), d_context, d_inner, rows_t, prompt_t)
+        (blocks, d_context, d_inner, rows_t, prompt_t)
     )
     early = lax.psum_scatter(blocks, BOTH, scatter_dimension=0, tiled=True)
 
@@ -954,11 +1017,11 @@
     d_cont_rows = rows_back(d_inner, d_queries, d_kv, joint_all, 0, cont_count, cont_tile)
     exchanges.finish()
     early = early[0].astype(F32)
-    output_grad = early[:part]
+    reduce_grad = early[: part * fold]
+    output_grad = early[part * fold : part * (fold + 1)]
     expand_grad = jnp.concatenate(
-        [early[part * (1 + i) : part * (2 + i)] for i in range(fold)], 1
-    )
-    reduce_grad = early[part * (1 + fold) :]
+        [early[part * (1 + fold + i) : part * (2 + fold + i)] for i in range(fold)], 1
+    )
     parts = [p.held for p in joint_parts]
     joint_grad = jnp.concatenate(
         [p[:part].reshape(part, nh, 3, PAIR) for p, nh in zip(parts, groups)], 1

time: 515 us -> 509 us (0.988)
  Pallas kernels: 300 us -> 327 us
  matrix products: 38.8 us -> 17.1 us
  local copies, waits for them, and re-layouts: 48.4 us -> 37 us
    pallas_call x0 -> x2, Pallas kernels: none -> 27.1 us  [the longest x1 15.4 us: matrix_grads(): pl.pallas_call(other_grads_kernel, grid=(1 + fold,), in_specs=[kept(), ke...]
    dot_general x5 -> x2, matrix products: 38.8 us -> 17.1 us  [dot(): lax.dot_general(left, right, (((left_dim,), (right_dim,)), ((), ())), pre...]
    unnamed x97 -> x80, local copies, waits for them, and re-layouts: 13.5 us -> 4.8 us
  transfers between devices with their start and end apart: 29 -> 29, of which waited for: 7 -> 7; matrix products, arithmetic and copies ran while one was open for 16% -> 16% of each run, Pallas kernels for 44% -> 45%
where the time goes in v5:
time: 509 us; the launch traced here: 504 us
  Pallas kernels  327 us (64%)
  starting transfers between devices  39.3 us (8%)
  local copies, waits for them, and re-layouts  37 us (7%)
  other arithmetic  35.5 us (7%)
  waiting for transfers between devices  33.4 us (7%)
  matrix products  17.1 us (3%)
  between operations  14.9 us (3%)
    pallas_call x3, Pallas kernels, attention_backward(): pl.pallas_call(functools.partial(attention_backward_kernel, cont_tiles),...  130 us
    pallas_call x2, Pallas kernels, attention_forward(): pl.pallas_call(functools.partial(attention_forward_kernel, near), grid=(p...  74 us
    pallas_call x1, Pallas kernels, dense(): pl.pallas_call(functools.partial(dense_kernel, cont_tiles, length, classe...  72.7 us
    ppermute x23, waiting for transfers between devices, across(): lax.ppermute(array, axis, [(i, i ^ bit) for i in range(lax.axis_size(axis...  33.2 us
    ppermute x23, starting transfers between devices, across(): lax.ppermute(array, axis, [(i, i ^ bit) for i in range(lax.axis_size(axis...  26.4 us
    dot_general x2, matrix products, dot(): lax.dot_general(left, right, (((left_dim,), (right_dim,)), ((), ())), pre...  17.1 us
    pallas_call x1, Pallas kernels, matrix_grads(): pl.pallas_call(other_grads_kernel, grid=(1 + fold,), in_specs=[kept(), ke...  15.4 us
    pallas_call x2, Pallas kernels, rows_back(): pl.pallas_call(rows_back_kernel, grid=(count // tile,), in_specs=[pl.Bloc...  15.2 us
  transfers between devices with their start and end apart: 29, of which 7 were waited for; matrix products, arithmetic and copies ran while one was open for 16% of the time, Pallas kernels for 45%

profile of v5, /device:TPU:0, one launch (start us, length us, event | category | flops | bytes accessed | tf_op | source)
XLA Modules:
  0.0 504.4 jit_solution(17082133427340710031)
XLA Ops:
  13.0 4.1 collective-permute-start
  25.1 4.4 collective-permute-done.6
  33.5 9.2 %collective-permute-done.7 = bf16[2,2,1,1,1,24,1152]{6,5,4,3,2,1,0:T(8,128)(2,1)S(1)} collective-permute-done((bf16[2,2,1,1,1,24,1152]{6,5,4,3,2,1,0:T(8,128)(2,1)S(1)}, bf16[2,2,1,1,1,24,1152]{6,5,4,3,2,1,0:T(8,128)(2,1)S(1)}, u32[]{:S(2)}, u32[]{:S(2)}) %collective-permute-start.7) | collective-permute-done | bytes 221216 | tf_op jit(solution)/shard_map/ppermute | solution.py:681
  46.7 10.1 %collective-permute-done.8 = bf16[2,2,1,2,1,24,1152]{6,5,4,3,2,1,0:T(8,128)(2,1)S(1)} collective-permute-done((bf16[2,2,1,2,1,24,1152]{6,5,4,3,2,1,0:T(8,128)(2,1)S(1)}, bf16[2,2,1,2,1,24,1152]{6,5,4,3,2,1,0:T(8,128)(2,1)S(1)}, u32[]{:S(2)}, u32[]{:S(2)}) %collective-permute-start.8) | collective-permute-done | bytes 442400 | tf_op jit(solution)/shard_map/ppermute | solution.py:681
  59.3 4.1 turn.2.refs_14_
  74.9 5.2 %fusion.4.refs_0_.refs_4_.refs_9_ = bf16[1536,768]{1,0:T(8,128)(2,1)} fusion(f32[768]{0:T(1024)S(1)} %get-tuple-element.221, bf16[768,2432]{1,0:T(8,128)(2,1)} %copy-done, bf16[512,768]{1,0:T(8,128)(2,1)S(1)} %bitcast.242, bf16[1024,768]{1,0:T(8,128)(2,1)} %bitcast.251), kind=kOutput, calls=%fused_computation.10 | convolution fusion | flops 1820196864 | bytes 5901312 | tf_op jit(solution)/shard_map/dot_general | solution.py:26
  80.1 3.4 pad_maximum_fusion.1
  83.5 3.7 turn.3.refs_15_
  88.1 11.9 %add_convert_fusion.refs_1_.refs_2_.refs_3_.refs_4_.refs_0_ = bf16[3072,1536]{1,0:T(8,128)(2,1)} fusion(f32[1536]{0:T(1024)S(1)} %add.115, bf16[1024,768]{1,0:T(8,128)(2,1)S(1)} %bitcast.253, bf16[2048,768]{1,0:T(8,128)(2,1)} %bitcast.236, bf16[768,2432]{1,0:T(8,128)(2,1)S(1)} %copy-done.1), kind=kOutput, calls=%fused_computation | convolution fusion | flops 7266631680 | bytes 16523264 | tf_op jit(solution)/shard_map/dot_general | solution.py:26
  100.0 25.7 %attention_forward.2 = (bf16[1536,768]{1,0:T(8,128)(2,1)}, f32[6,2,2,256]{3,2,1,0:T(2,128)}, bf16[6,2,2,2048,256]{4,3,2,1,0:T(8,128)(2,1)}) custom-call(bf16[1536,768]{1,0:T(8,128)(2,1)} %fusion.4.refs_0_.refs_4_.refs_9_, bf16[3072,1536]{1,0:T(8,128)(2,1)} %add_convert_fusion.refs_1_.refs_2_.refs_3_.refs_4_.refs_0_, ...), custom_call_target="tpu_custom_call" | custom-call | flops 3221225472 | bytes 25165824 | tf_op jit(solution)/shard_map/attention_forward/pallas_call | solution.py:154
  125.7 48.4 %attention_forward.3 = (bf16[1536,768]{1,0:T(8,128)(2,1)}, f32[6,4,2,256]{3,2,1,0:T(2,128)}, bf16[6,4,2,2304,256]{4,3,2,1,0:T(8,128)(2,1)}) custom-call(bf16[1536,768]{1,0:T(8,128)(2,1)} %fusion.4.refs_0_.refs_4_.refs_9_, bf16[3072,1536]{1,0:T(8,128)(2,1)} %add_convert_fusion.refs_1_.refs_2_.refs_3_.refs_4_.refs_0_, ...), custom_call_target="tpu_custom_call", output_to_operand_aliasing={{0}: (5, {})} | custom-call | flops 7247757312 | bytes 56623104 | tf_op jit(solution)/shard_map/attention_forward/pallas_call | solution.py:154
  174.1 72.7 %dense.1 = (bf16[1536,768]{1,0:T(8,128)(2,1)}, f32[4,128]{1,0:T(4,128)}, bf16[1536,768]{1,0:T(8,128)(2,1)}, bf16[1536,3072]{1,0:T(8,128)(2,1)}, bf16[1536,768]{1...) custom-call(s32[4]{0:T(128)} %bitcast.274, ...), custom_call_target="tpu_custom_call" | custom-call | flops 32614907904 | bytes 40108032 | tf_op jit(solution)/shard_map/dense/pallas_call | solution.py:552
  246.8 11.7 %reduce_grad.1._ = bf16[32,216,768]{2,1,0:T(8,128)(2,1)} custom-call(bf16[1536,3072]{1,0:T(8,128)(2,1)} %get-tuple-element.92.hidden_ref, bf16[1536,768]{1,0:T(8,128)(2,1)} %get-tuple-element.93.d_ref), custom_call_target="tpu_custom_call" | custom-call | flops 7247757312 | tf_op jit(solution)/shard_map/reduce_grad/pallas_call | solution.py:642
  258.5 15.4 %other_grads.1 = bf16[32,216,768]{2,1,0:T(8,128)(2,1)} custom-call(bf16[1536,768]{1,0:T(8,128)(2,1)} %get-tuple-element.86.refs_2_.context_ref.refs_5_.refs_10_, bf16[1536,768]{1,0:T(8,128)(2,1)} %get-tuple-element.89.d_inner_ref, bf16[1536,768]{1,0:T(8,128)(2,1)} %get-tuple-element.90.first_ref, ...), custom_call_target="tpu_custom_call", output_to_operand_aliasing={{}: (4, {})} | custom-call | flops 9059696640 | tf_op jit(solution)/shard_map/other_grads/pallas_call | solution.py:654
  277.0 62.4 %attention_backward.3 = (bf16[1536,768]{1,0:T(8,128)(2,1)}, bf16[1024,1536]{1,0:T(8,128)(2,1)}, bf16[2048,768]{1,0:T(8,128)(2,1)}, bf16[768,1152]{1,0:T(8,128)(2,1)}, f32[3,8,384]{2,1,0:T(8,128)}) custom-call(bf16[3072,1536]{1,0:T(8,128)(2,1)} %add_convert_fusion.refs_1_.refs_2_.refs_3_.refs_4_.refs_0_, ...), custom_call_target="tpu_custom_call" | custom-call | flops 20447232 | bytes 1277952 | tf_op jit(solution)/shard_map/attention_backward/pallas_call | solution.py:294
  341.7 3.1 all-to-all-start
  346.0 2.7 slice.257
  352.4 43.7 %attention_backward.4 = (bf16[1536,768]{1,0:T(8,128)(2,1)}, bf16[1024,1536]{1,0:T(8,128)(2,1)}, bf16[2048,512]{1,0:T(8,128)(2,1)}, bf16[768,768]{1,0:T(8,128)(2,1)}, f32[2,8,384]{2,1,0:T(8,128)}) custom-call(bf16[3072,1536]{1,0:T(8,128)(2,1)} %add_convert_fusion.refs_1_.refs_2_.refs_3_.refs_4_.refs_0_, ...), custom_call_target="tpu_custom_call", output_to_operand_aliasing={{0}: (16, {}), {1}: (17, {})} | custom-call | flops 13631488 | bytes 851968 | tf_op jit(solution)/shard_map/attention_backward/pallas_call | solution.py:294
  402.4 4.8 all-to-all-start.1
  412.0 24.3 %attention_backward.5 = (bf16[1536,768]{1,0:T(8,128)(2,1)}, bf16[1024,1536]{1,0:T(8,128)(2,1)}, bf16[2048,256]{1,0:T(8,128)(2,1)}, bf16[768,384]{1,0:T(8,128)(2,1)}, f32[1,8,384]{2,1,0:T(8,128)}) custom-call(bf16[3072,1536]{1,0:T(8,128)(2,1)} %add_convert_fusion.refs_1_.refs_2_.refs_3_.refs_4_.refs_0_, ...), custom_call_target="tpu_custom_call", output_to_operand_aliasing={{0}: (16, {}), {1}: (17, {})} | custom-call | flops 6815744 | bytes 425984 | tf_op jit(solution)/shard_map/attention_backward/pallas_call | solution.py:294
  450.0 4.9 all-to-all-start.2
  461.7 8.7 %rows_back.3 = f32[1024,768]{1,0:T(8,128)} custom-call(f32[1536,768]{1,0:T(8,128)} %get-tuple-element.96.d_inner_ref, bf16[1536,768]{1,0:T(8,128)(2,1)} %get-tuple-element.135.dq_ref, bf16[1024,1536]{1,0:T(8,128)(2,1)} %get-tuple-element.139.dkv_ref, bf16[768,2432]{1,0:T(8,128)(2,1)} %copy-done), custom_call_target="tpu_custom_call" | custom-call | flops 1024 | bytes 1024 | tf_op jit(solution)/shard_map/rows_back/pallas_call | solution.py:599
  470.4 7.6 %collective-permute-done.19 = bf16[1,512,512]{2,1,0:T(8,128)(2,1)} collective-permute-done((bf16[1,512,512]{2,1,0:T(8,128)(2,1)}, bf16[1,512,512]{2,1,0:T(8,128)(2,1)}, u32[]{:S(2)}, u32[]{:S(2)}) %collective-permute-start.19) | collective-permute-done | bytes 524320 | tf_op jit(solution)/shard_map/ppermute | solution.py:681
  489.6 6.5 %rows_back.2 = f32[512,768]{1,0:T(8,128)} custom-call(f32[1536,768]{1,0:T(8,128)} %get-tuple-element.96.d_inner_ref, bf16[1536,768]{1,0:T(8,128)(2,1)} %get-tuple-element.135.dq_ref, bf16[512,1536]{1,0:T(8,128)(2,1)} %pad_maximum_fusion.5.dkv_ref, bf16[768,2432]{1,0:T(8,128)(2,1)} %copy-done), custom_call_target="tpu_custom_call" | custom-call | flops 512 | bytes 512 | tf_op jit(solution)/shard_map/rows_back/pallas_call | solution.py:599
  (241 shorter events, 90.9 us)
Async XLA Ops:
  7.4 166.7 %all-gather.5.cloned.1.call-start = ((), (), s32[]{:S(2)}) async-start(), calls=%async_computation.5 | async-start | bytes 4866048 | tf_op jit(solution)/shard_map/all_gather | solution.py:914
  9.2 164.9 %all-gather.3.cloned.1.call-start = ((), (), s32[]{:S(2)}) async-start(), calls=%async_computation.4 | async-start | bytes 6082560 | tf_op jit(solution)/shard_map/all_gather | solution.py:911
  11.8 435.9 %reduce-scatter.2.cloned.1.call-start = ((), (), s32[]{:S(2)}) async-start(), calls=%async_computation.6 | async-start | bytes 10948608 | tf_op jit(solution)/shard_map/reduce_scatter | solution.py:992
  13.0 11.4 %collective-permute-start = (bf16[1,1,1,1,1,24,1280]{6,5,4,3,2,1,0:T(8,128)(2,1)S(1)}, bf16[1,1,1,1,1,24,1280]{6,5,4,3,2,1,0:T(8,128)(2,1)S(1)}, u32[]{:S(2)}, u32[]{:S(2)}) collective-permute-start(bf16[1,1,1,1,1,24,1280]{6,5,4,3,2,1,0:T(8,128)(2,1)S(1)} %get-tuple-element.249), channel_id=1, source_target_pairs={{0,16},{4,20},{8,24},{12,28},{16,0},{20,4},{24,8},{28,12},{1,17},{... | collective-permute-start | bytes 184328 | tf_op jit(solution)/shard_map/ppermute | solution.py:681
  17.6 47.4 %collective-permute-start.10 = (bf16[1,1,512,768]{3,2,1,0:T(8,128)(2,1)S(1)}, bf16[1,1,512,768]{3,2,1,0:T(8,128)(2,1)S(1)}, u32[]{:S(2)}, u32[]{:S(2)}) collective-permute-start(bf16[1,1,512,768]{3,2,1,0:T(8,128)(2,1)S(1)} %bitcast.239), channel_id=1, source_target_pairs={{0,2},{1,3},{2,0},{3,1},{4,6},{5,7},{6,4},{7,5},{8,10},{9,11},{10,... | collective-permute-start | bytes 2359304 | tf_op jit(solution)/shard_map/ppermute | solution.py:681
  29.6 13.1 %collective-permute-start.7 = (bf16[2,2,1,1,1,24,1152]{6,5,4,3,2,1,0:T(8,128)(2,1)S(1)}, bf16[2,2,1,1,1,24,1152]{6,5,4,3,2,1,0:T(8,128)(2,1)S(1)}, u32[]{:S(2)}, u32[]{:S(2)}) collective-permute-start(bf16[2,2,1,1,1,24,1152]{6,5,4,3,2,1,0:T(8,128)(2,1)S(1)} %maximum_select_fusion.11), channel_id=1, source_target_pairs={{0,2},{1,3},{2,0},{3,1},{4,6},{5,7},{6,4},{7,5},{8,10},{9,11},{10,... | collective-permute-start | bytes 663560 | tf_op jit(solution)/shard_map/ppermute | solution.py:681
  31.9 12.4 %collective-permute-start.2 = (bf16[2,2,1,1,1,24,1280]{6,5,4,3,2,1,0:T(8,128)(2,1)S(1)}, bf16[2,2,1,1,1,24,1280]{6,5,4,3,2,1,0:T(8,128)(2,1)S(1)}, u32[]{:S(2)}, u32[]{:S(2)}) collective-permute-start(bf16[2,2,1,1,1,24,1280]{6,5,4,3,2,1,0:T(8,128)(2,1)S(1)} %maximum_select_fusion.9), channel_id=1, source_target_pairs={{0,4},{4,0},{8,12},{12,8},{16,20},{20,16},{24,28},{28,24},{1,5},{5... | collective-permute-start | bytes 737288 | tf_op jit(solution)/shard_map/ppermute | solution.py:681
  42.8 14.0 %collective-permute-start.8 = (bf16[2,2,1,2,1,24,1152]{6,5,4,3,2,1,0:T(8,128)(2,1)S(1)}, bf16[2,2,1,2,1,24,1152]{6,5,4,3,2,1,0:T(8,128)(2,1)S(1)}, u32[]{:S(2)}, u32[]{:S(2)}) collective-permute-start(bf16[2,2,1,2,1,24,1152]{6,5,4,3,2,1,0:T(8,128)(2,1)S(1)} %maximum_select_fusion.7), channel_id=1, source_target_pairs={{0,4},{4,0},{8,12},{12,8},{16,20},{20,16},{24,28},{28,24},{1,5},{5... | collective-permute-start | bytes 1327112 | tf_op jit(solution)/shard_map/ppermute | solution.py:681
  44.3 12.7 %collective-permute-start.3 = (bf16[2,2,2,1,1,24,1280]{6,5,4,3,2,1,0:T(8,128)(2,1)S(1)}, bf16[2,2,2,1,1,24,1280]{6,5,4,3,2,1,0:T(8,128)(2,1)S(1)}, u32[]{:S(2)}, u32[]{:S(2)}) collective-permute-start(bf16[2,2,2,1,1,24,1280]{6,5,4,3,2,1,0:T(8,128)(2,1)S(1)} %maximum_select_fusion.5), channel_id=1, source_target_pairs={{0,2},{1,3},{2,0},{3,1},{4,6},{5,7},{6,4},{7,5},{8,10},{9,11},{10,... | collective-permute-start | bytes 1474568 | tf_op jit(solution)/shard_map/ppermute | solution.py:681
  57.1 10.0 %collective-permute-start.4 = (bf16[2,2,2,2,1,24,1280]{6,5,4,3,2,1,0:T(8,128)(2,1)S(1)}, bf16[2,2,2,2,1,24,1280]{6,5,4,3,2,1,0:T(8,128)(2,1)}, u32[]{:S(2)}, u32[]{:S(2)}) collective-permute-start(bf16[2,2,2,2,1,24,1280]{6,5,4,3,2,1,0:T(8,128)(2,1)S(1)} %maximum_select_fusion.2), channel_id=1, source_target_pairs={{0,1},{1,0},{2,3},{3,2},{4,5},{5,4},{6,7},{7,6},{8,9},{9,8},{10,11... | collective-permute-start | bytes 2949128 | tf_op jit(solution)/shard_map/ppermute | solution.py:681
  65.2 14.9 %collective-permute-start.11 = (bf16[2,1,512,768]{3,2,1,0:T(8,128)(2,1)S(1)}, bf16[2,1,512,768]{3,2,1,0:T(8,128)(2,1)}, u32[]{:S(2)}, u32[]{:S(2)}) collective-permute-start(bf16[2,1,512,768]{3,2,1,0:T(8,128)(2,1)S(1)} %pad_maximum_fusion.4), channel_id=1, source_target_pairs={{0,1},{1,0},{2,3},{3,2},{4,5},{5,4},{6,7},{7,6},{8,9},{9,8},{10,11... | collective-permute-start | bytes 4718600 | tf_op jit(solution)/shard_map/ppermute | solution.py:681
  275.0 65.9 %collective-permute-start.12 = (bf16[1088,128]{1,0:T(8,128)(2,1)S(1)}, bf16[1088,128]{1,0:T(8,128)(2,1)S(1)}, u32[]{:S(2)}, u32[]{:S(2)}) collective-permute-start(bf16[1088,128]{1,0:T(8,128)(2,1)S(1)} %convert_element_type.197), channel_id=1, source_target_pairs={{0,16},{4,20},{8,24},{12,28},{16,0},{20,4},{24,8},{28,12},{1,17},{... | collective-permute-start | bytes 835592 | tf_op jit(solution)/shard_map/ppermute | solution.py:681
  341.7 60.4 %all-to-all-start = ((bf16[32,24,1152]{2,1,0:T(8,128)(2,1)}), bf16[32,24,1152]{2,1,0:T(8,128)(2,1)S(1)}, u32[]{:S(2)}, u32[]{:S(2)}) async-start(bf16[32,24,1152]{2,1,0:T(8,128)(2,1)} %bitcast.73), calls=%async_computation.1 | async-start | bytes 3538944 | tf_op jit(solution)/shard_map/all_to_all | solution.py:746
  344.8 54.4 %collective-permute-start.14 = (bf16[2,512,768]{2,1,0:T(8,128)(2,1)S(1)}, bf16[2,512,768]{2,1,0:T(8,128)(2,1)}, u32[]{:S(2)}, u32[]{:S(2)}) collective-permute-start(bf16[2,512,768]{2,1,0:T(8,128)(2,1)S(1)} %slice_bitcast_fusion.1), channel_id=1, source_target_pairs={{0,1},{1,0},{2,3},{3,2},{4,5},{5,4},{6,7},{7,6},{8,9},{9,8},{10,11... | collective-permute-start | bytes 4718600 | tf_op jit(solution)/shard_map/ppermute | solution.py:681
  350.7 47.7 %collective-permute-start.13 = (bf16[1088,128]{1,0:T(8,128)(2,1)S(1)}, bf16[1088,128]{1,0:T(8,128)(2,1)S(1)}, u32[]{:S(2)}, u32[]{:S(2)}) collective-permute-start(bf16[1088,128]{1,0:T(8,128)(2,1)S(1)} %copy-done.12), channel_id=1, source_target_pairs={{0,8},{4,12},{8,0},{12,4},{16,24},{20,28},{24,16},{28,20},{1,9},{5... | collective-permute-start | bytes 835592 | tf_op jit(solution)/shard_map/ppermute | solution.py:681
  402.4 45.1 %all-to-all-start.1 = ((bf16[32,24,768]{2,1,0:T(8,128)(2,1)}), bf16[32,24,768]{2,1,0:T(8,128)(2,1)S(1)}, u32[]{:S(2)}, u32[]{:S(2)}) async-start(bf16[32,24,768]{2,1,0:T(8,128)(2,1)} %bitcast.255), calls=%async_computation.2 | async-start | bytes 2359296 | tf_op jit(solution)/shard_map/all_to_all | solution.py:746
  408.5 36.6 %collective-permute-start.17 = (bf16[2,512,512]{2,1,0:T(8,128)(2,1)}, bf16[2,512,512]{2,1,0:T(8,128)(2,1)}, u32[]{:S(2)}, u32[]{:S(2)}) collective-permute-start(bf16[2,512,512]{2,1,0:T(8,128)(2,1)} %slice_bitcast_fusion.3), channel_id=1, source_target_pairs={{0,1},{1,0},{2,3},{3,2},{4,5},{5,4},{6,7},{7,6},{8,9},{9,8},{10,11... | collective-permute-start | bytes 3145736 | tf_op jit(solution)/shard_map/ppermute | solution.py:681
  408.9 33.9 %collective-permute-start.16 = (bf16[1,512,768]{2,1,0:T(8,128)(2,1)}, bf16[1,512,768]{2,1,0:T(8,128)(2,1)}, u32[]{:S(2)}, u32[]{:S(2)}) collective-permute-start(bf16[1,512,768]{2,1,0:T(8,128)(2,1)} %slice_bitcast_fusion.5), channel_id=1, source_target_pairs={{0,2},{1,3},{2,0},{3,1},{4,6},{5,7},{6,4},{7,5},{8,10},{9,11},{10,... | collective-permute-start | bytes 2359304 | tf_op jit(solution)/shard_map/ppermute | solution.py:681
  410.6 31.5 %collective-permute-start.15 = (bf16[1088,128]{1,0:T(8,128)(2,1)S(1)}, bf16[1088,128]{1,0:T(8,128)(2,1)S(1)}, u32[]{:S(2)}, u32[]{:S(2)}) collective-permute-start(bf16[1088,128]{1,0:T(8,128)(2,1)S(1)} %copy-done.10), channel_id=1, source_target_pairs={{0,4},{4,0},{8,12},{12,8},{16,20},{20,16},{24,28},{28,24},{1,5},{5... | collective-permute-start | bytes 835592 | tf_op jit(solution)/shard_map/ppermute | solution.py:681
  447.7 11.4 %collective-permute-start.21 = (bf16[1088,128]{1,0:T(8,128)(2,1)S(1)}, bf16[1088,128]{1,0:T(8,128)(2,1)S(1)}, u32[]{:S(2)}, u32[]{:S(2)}) collective-permute-start(bf16[1088,128]{1,0:T(8,128)(2,1)S(1)} %copy-done.11), channel_id=1, source_target_pairs={{0,2},{1,3},{2,0},{3,1},{4,6},{5,7},{6,4},{7,5},{8,10},{9,11},{10,... | collective-permute-start | bytes 835592 | tf_op jit(solution)/shard_map/ppermute | solution.py:681
  450.0 46.1 %all-to-all-start.2 = ((bf16[32,32,384]{2,1,0:T(8,128)(2,1)}), bf16[32,32,384]{2,1,0:T(8,128)(2,1)S(1)}, u32[]{:S(2)}, u32[]{:S(2)}) async-start(bf16[32,32,384]{2,1,0:T(8,128)(2,1)} %fusion.14), calls=%async_computation.3 | async-start | bytes 1572864 | tf_op jit(solution)/shard_map/all_to_all | solution.py:746
  455.3 22.8 %collective-permute-start.19 = (bf16[1,512,512]{2,1,0:T(8,128)(2,1)}, bf16[1,512,512]{2,1,0:T(8,128)(2,1)}, u32[]{:S(2)}, u32[]{:S(2)}) collective-permute-start(bf16[1,512,512]{2,1,0:T(8,128)(2,1)} %slice_bitcast_fusion.9), channel_id=1, source_target_pairs={{0,2},{1,3},{2,0},{3,1},{4,6},{5,7},{6,4},{7,5},{8,10},{9,11},{10,... | collective-permute-start | bytes 1572872 | tf_op jit(solution)/shard_map/ppermute | solution.py:681
  459.2 20.9 %collective-permute-start.22 = (bf16[1088,128]{1,0:T(8,128)(2,1)S(1)}, bf16[1088,128]{1,0:T(8,128)(2,1)S(1)}, u32[]{:S(2)}, u32[]{:S(2)}) collective-permute-start(bf16[1088,128]{1,0:T(8,128)(2,1)S(1)} %add_convert_fusion.2), channel_id=1, source_target_pairs={{0,1},{1,0},{2,3},{3,2},{4,5},{5,4},{6,7},{7,6},{8,9},{9,8},{10,11... | collective-permute-start | bytes 835592 | tf_op jit(solution)/shard_map/ppermute | solution.py:681
  461.4 25.3 %collective-permute-start.20 = (bf16[1,512,256]{2,1,0:T(8,128)(2,1)}, bf16[1,512,256]{2,1,0:T(8,128)(2,1)}, u32[]{:S(2)}, u32[]{:S(2)}) collective-permute-start(bf16[1,512,256]{2,1,0:T(8,128)(2,1)} %slice_bitcast_fusion.14), channel_id=1, source_target_pairs={{0,2},{1,3},{2,0},{3,1},{4,6},{5,7},{6,4},{7,5},{8,10},{9,11},{10,... | collective-permute-start | bytes 786440 | tf_op jit(solution)/shard_map/ppermute | solution.py:681
  (38 other events, 349.2 us)
Sparse Core Ops, SparseCore 0:
  11.7 68.9 all-gather.4
  84.2 66.5 all-gather.2
  274.0 167.0 reduce-scatter.1
